TPU v7x, 32 devices: a whole 2x2x4 slice. The times are simulated.
32 devices in a mesh: groups: 2 (over y), rows: 4 (over z), cols: 4 (over x, core).
Axes of the slice: x: 2, y: 2, z: 4, core: 2. Of those that a mesh axis runs over, the one named last changes fastest.
Arguments:
- pixels: bfloat16 [128, 64, 128], P(('groups', 'rows'), 'cols'), parts along dimension 0, may hold values from -6 to 6
- cotangent: bfloat16 [128, 64, 128], P(('groups', 'rows'), 'cols'), parts along dimension 0, may hold values from -6 to 6
- w_in: bfloat16 [128, 512], replicated, may hold values from -0.5 to 0.5
- w_out: bfloat16 [256, 128], replicated, may hold values from -0.375 to 0.375
- decay_rates: float32 [4, 256], replicated, may hold values from 0.0015625 to 0.03, as said below
- step_sizes: float32 [4, 128, 64], P(None, ('groups', 'rows'), 'cols'), parts along dimension 1, may hold values from 0.25 to 128, as said below
Outputs:
- grad_pixels: bfloat16 [128, 64, 128], P(('groups', 'rows'), 'cols'), parts along dimension 0
- grad_in: float32 [256, 512], P(('groups', 'rows'), 'cols'), parts along dimension 0
- grad_out: float32 [512, 128], P(('groups', 'rows'), 'cols'), parts along dimension 0
There are 2 independent parts, one for each index of `groups`. A program takes and returns all parts, laid end to end along the dimension named above; an argument that names none is the same for every part. Nothing has to cross between parts.
Inputs may be any that keep to these rules, and one draw needn't show every extreme that they name: `decay_rates`: positive decay rates. `step_sizes`: positive step sizes.
All inputs are finite; a program needn't handle non-finite values.
Results may differ from a plain program's by a relative error of at most 0.005.
Values sent between devices are 32-bit elements; how exact they have to be, the bound alone decides.
No kernel may reach another device: no remote copies, remote signals or barrier semaphores. Data moves between devices by JAX's collectives and lax.ppermute only.
A program may use at most 64 MiB of HBM per device.

v0:
```python
import jax
import jax.numpy as jnp
from jax import lax
from jax.sharding import PartitionSpec as P

line_order = ((1, False), (1, True), (0, False), (0, True))


def entering(value, axis, join, neutral, backward):
    count, mine = (lax.axis_size(axis), lax.axis_index(axis))
    pieces = jax.tree.map(lambda part: lax.all_gather(part, axis), value)
    if backward:
        pieces = jax.tree.map(lambda part: part[::-1], pieces)
        mine = count - 1 - mine
    running = jax.tree.map(
        lambda part, zero: jnp.full_like(part, 0) + jnp.asarray(zero, part.dtype), value, neutral
    )

    def step(position, running):
        longer = join(running, jax.tree.map(lambda part: part[position], pieces))
        return jax.tree.map(lambda new, old: jnp.where(position < mine, new, old), longer, running)

    return lax.fori_loop(0, count - 1, step, running)


def affine(earlier_map, later_map):
    return (earlier_map[0] * later_map[0], later_map[0] * earlier_map[1] + later_map[1])


def pair_combine(earlier_map, later_map):
    first_pair = affine((earlier_map[0], earlier_map[1]), (later_map[0], later_map[1]))
    second_pair = affine((earlier_map[2], earlier_map[3]), (later_map[2], later_map[3]))
    return (first_pair[0], first_pair[1], second_pair[0], second_pair[1])


def shift_in(values, line_axis, backward, filler):
    length = values.shape[line_axis]
    if backward:
        return jnp.concatenate(
            [filler, lax.slice_in_dim(values, 0, length - 1, axis=line_axis)], axis=line_axis
        )
    return jnp.concatenate(
        [lax.slice_in_dim(values, 1, length, axis=line_axis), filler], axis=line_axis
    )


def edge_of(values, line_axis, at_last):
    length = values.shape[line_axis]
    return lax.index_in_dim(values, length - 1 if at_last else 0, line_axis, keepdims=False)


def silu_slope(values):
    sigma = jax.nn.sigmoid(values)
    return sigma * (1.0 + values * (1.0 - sigma))


def per_device(pixels, cotangent, w_in, w_out, decay_rates, step_sizes):
    height, breadth, channels = pixels.shape
    expand = w_out.shape[0]
    pixel_count = height * breadth
    contract_rows = (((0,), (0,)), ((), ()))
    contract_cols = (((1,), (1,)), ((), ()))
    flat_in = pixels.reshape(pixel_count, channels)
    flat_cot = cotangent.reshape(pixel_count, channels)
    mixed_in = jnp.dot(flat_in, w_in, preferred_element_type=jnp.float32)
    inner_part = mixed_in[:, :expand].reshape(height, breadth, expand)
    gate_part = mixed_in[:, expand:].reshape(height, breadth, expand)
    back_grad = lax.dot_general(
        flat_cot, w_out, contract_cols, preferred_element_type=jnp.float32
    ).reshape(height, breadth, expand)
    source = jax.nn.silu(inner_part)
    gated = jax.nn.silu(gate_part)
    seed_grad = back_grad * gated
    state_sum = jnp.zeros_like(source)
    grad_source = jnp.zeros_like(source)
    kept_lines = []
    for line_no in range(4):
        line_axis, backward = line_order[line_no]
        scaled = decay_rates[line_no][None, None, :] * step_sizes[line_no][:, :, None]
        decay_now = jnp.exp(-scaled)
        weight = jnp.sqrt(-jnp.expm1(-2.0 * scaled))
        fwd_cum, fwd_loc = lax.associative_scan(
            affine, (decay_now, weight * source), reverse=backward, axis=line_axis
        )
        adj_cum, adj_loc = lax.associative_scan(
            affine, (decay_now, decay_now * seed_grad), reverse=not backward, axis=line_axis
        )
        zero_edge = jnp.zeros_like(lax.slice_in_dim(adj_loc, 0, 1, axis=line_axis))
        state_sum = state_sum + fwd_loc
        grad_source = grad_source + weight * (
            seed_grad + shift_in(adj_loc, line_axis, backward, zero_edge)
        )
        kept_lines.append(
            (
                fwd_cum,
                adj_cum,
                weight,
                edge_of(fwd_cum, line_axis, not backward),
                edge_of(fwd_loc, line_axis, not backward),
                edge_of(adj_loc, line_axis, backward),
            )
        )
    right_line, left_line, down_line, up_line = kept_lines
    unit_cols = jnp.ones_like(right_line[3])
    zero_cols = jnp.zeros_like(right_line[3])
    unit_rows = jnp.ones_like(down_line[3])
    zero_rows = jnp.zeros_like(down_line[3])
    from_left = entering(
        (right_line[3], right_line[4], left_line[3], left_line[5]),
        "cols",
        pair_combine,
        (unit_cols, zero_cols, unit_cols, zero_cols),
        False,
    )
    from_right = entering(
        (left_line[3], left_line[4], right_line[3], right_line[5]),
        "cols",
        pair_combine,
        (unit_cols, zero_cols, unit_cols, zero_cols),
        True,
    )
    from_top = entering(
        (down_line[3], down_line[4], up_line[3], up_line[5]),
        "rows",
        pair_combine,
        (unit_rows, zero_rows, unit_rows, zero_rows),
        False,
    )
    from_bottom = entering(
        (up_line[3], up_line[4], down_line[3], down_line[5]),
        "rows",
        pair_combine,
        (unit_rows, zero_rows, unit_rows, zero_rows),
        True,
    )
    forward_in = (from_left[1], from_right[1], from_top[1], from_bottom[1])
    adjoint_in = (from_right[3], from_left[3], from_bottom[3], from_top[3])
    for line_no in range(4):
        line_axis, backward = line_order[line_no]
        fwd_cum, adj_cum, weight = kept_lines[line_no][:3]
        unit_edge = jnp.ones_like(lax.slice_in_dim(adj_cum, 0, 1, axis=line_axis))
        state_sum = state_sum + fwd_cum * jnp.expand_dims(forward_in[line_no], line_axis)
        grad_source = grad_source + weight * shift_in(
            adj_cum, line_axis, backward, unit_edge
        ) * jnp.expand_dims(adjoint_in[line_no], line_axis)
    out_flat = (state_sum * gated).astype(jnp.bfloat16).reshape(pixel_count, expand)
    grad_inner = grad_source * silu_slope(inner_part)
    grad_gate = back_grad * state_sum * silu_slope(gate_part)
    grad_mix = (
        jnp.concatenate([grad_inner, grad_gate], axis=-1)
        .astype(jnp.bfloat16)
        .reshape(pixel_count, 2 * expand)
    )
    grad_pixels = (
        (
            flat_cot.astype(jnp.float32)
            + lax.dot_general(grad_mix, w_in, contract_cols, preferred_element_type=jnp.float32)
        )
        .astype(jnp.bfloat16)
        .reshape(height, breadth, channels)
    )
    full_in = lax.dot_general(flat_in, grad_mix, contract_rows, preferred_element_type=jnp.float32)
    full_out = lax.dot_general(
        out_flat, flat_cot, contract_rows, preferred_element_type=jnp.float32
    )
    col_part = (
        lax.psum_scatter(full_in, "cols", scatter_dimension=1, tiled=True),
        lax.psum_scatter(full_out, "cols", scatter_dimension=1, tiled=True),
    )
    grad_in, grad_out = (
        lax.psum_scatter(col_part[0], "rows", scatter_dimension=0, tiled=True),
        lax.psum_scatter(col_part[1], "rows", scatter_dimension=0, tiled=True),
    )
    return (grad_pixels, grad_in, grad_out)


def solution(mesh):
    return jax.shard_map(
        per_device,
        mesh=mesh,
        in_specs=(
            P(("groups", "rows"), "cols", None),
            P(("groups", "rows"), "cols", None),
            P(),
            P(),
            P(),
            P(None, ("groups", "rows"), "cols"),
        ),
        out_specs=(
            P(("groups", "rows"), "cols", None),
            P(("groups", "rows"), "cols"),
            P(("groups", "rows"), "cols"),
        ),
        check_vma=False,
    )
```

profile of v0, /device:TPU:0, one launch (start us, length us, event | category | flops | bytes accessed | tf_op | source)
XLA Modules:
  0.0 491.2 jit_solution(12370333538446631653)
XLA Ops:
  187.7 6.2 %all-gather.5 = f32[64,1,256]{2,1,0:T(1,128)S(1)} all-gather(f32[16,1,256]{2,1,0:T(1,128)S(1)} %slice.1991), channel_id=7, replica_groups=mesh['groups'=2,'rows'=4,'cols'=4] {'cols'}, dimensions={0}, use_global_device_ids=true | all-gather | bytes 81920 | tf_op jit(solution)/shard_map/all_gather | solution.py:11
  201.6 5.7 %all-gather.4 = f32[64,1,256]{2,1,0:T(1,128)S(1)} all-gather(f32[16,1,256]{2,1,0:T(1,128)S(1)} %slice_add_fusion.20), channel_id=6, replica_groups=mesh['groups'=2,'rows'=4,'cols'=4] {'cols'}, dimensions={0}, use_global_device_ids=true | all-gather | bytes 81920 | tf_op jit(solution)/shard_map/all_gather | solution.py:11
  208.2 5.6 %pad.471 = f32[16,16,256]{2,1,0:T(8,128)S(1)} pad(f32[16,8,256]{2,1,0:T(8,128)} %add.938, f32[]{:T(128)} %constant.108.clone.1), padding=0_0_0x1_0_1x0_0_0 | pad | bytes 393220 | tf_op jit(solution)/shard_map/pad | solution.py:82
  213.8 5.2 %all-gather.2 = f32[64,1,256]{2,1,0:T(1,128)S(1)} all-gather(f32[16,1,256]{2,1,0:T(1,128)S(1)} %slice_add_fusion.23), channel_id=4, replica_groups=mesh['groups'=2,'rows'=4,'cols'=4] {'cols'}, dimensions={0}, use_global_device_ids=true | all-gather | bytes 81920 | tf_op jit(solution)/shard_map/all_gather | solution.py:11
  219.8 5.2 %all-gather = f32[64,1,256]{2,1,0:T(1,128)S(1)} all-gather(f32[16,1,256]{2,1,0:T(1,128)S(1)} %copy-done.123), channel_id=2, replica_groups=mesh['groups'=2,'rows'=4,'cols'=4] {'cols'}, dimensions={0}, use_global_device_ids=true | all-gather | bytes 81920 | tf_op jit(solution)/shard_map/all_gather | solution.py:11
  228.0 4.2 while.65
  232.3 5.6 %pad.969 = f32[16,15,256]{2,1,0:T(8,128)} pad(f32[16,8,256]{2,1,0:T(8,128)S(1)} %add.873, f32[]{:T(128)} %constant.108.clone.1), padding=0_0_0x0_0_1x0_0_0 | pad | bytes 376836
  238.7 5.2 %all-gather.3 = f32[64,1,256]{2,1,0:T(1,128)S(1)} all-gather(f32[16,1,256]{2,1,0:T(1,128)S(1)} %slice.1989), channel_id=5, replica_groups=mesh['groups'=2,'rows'=4,'cols'=4] {'cols'}, dimensions={0}, use_global_device_ids=true | all-gather | bytes 81920 | tf_op jit(solution)/shard_map/all_gather | solution.py:11
  246.1 5.2 %all-gather.1 = f32[64,1,256]{2,1,0:T(1,128)S(1)} all-gather(f32[16,1,256]{2,1,0:T(1,128)S(1)} %copy-done.122), channel_id=3, replica_groups=mesh['groups'=2,'rows'=4,'cols'=4] {'cols'}, dimensions={0}, use_global_device_ids=true | all-gather | bytes 81920 | tf_op jit(solution)/shard_map/all_gather | solution.py:11
  255.9 3.1 pad.967
  259.8 14.3 %all_gather.51 = f32[4,16,256]{2,1,0:T(8,128)} all-gather(f32[1,16,256]{2,1,0:T(8,128)S(1)} %slice.1987), channel_id=1, replica_groups=mesh['groups'=2,'rows'=4,'cols'=4] {'rows'}, dimensions={0}, use_global_device_ids=true | all-gather | bytes 81920 | tf_op jit(solution)/shard_map/all_gather | solution.py:11
  274.7 4.8 pad.534
  279.6 3.1 pad.535
  283.5 14.2 %all_gather.50 = f32[4,16,256]{2,1,0:T(8,128)} all-gather(f32[1,16,256]{2,1,0:T(8,128)S(1)} %slice_add_fusion.14), channel_id=1, replica_groups=mesh['groups'=2,'rows'=4,'cols'=4] {'rows'}, dimensions={0}, use_global_device_ids=true | all-gather | bytes 81920 | tf_op jit(solution)/shard_map/all_gather | solution.py:11
  298.3 4.8 pad.518
  307.0 13.3 %all_gather.48 = f32[4,16,256]{2,1,0:T(8,128)S(1)} all-gather(f32[1,16,256]{2,1,0:T(8,128)S(1)} %slice_add_fusion.16), channel_id=1, replica_groups=mesh['groups'=2,'rows'=4,'cols'=4] {'rows'}, dimensions={0}, use_global_device_ids=true | all-gather | bytes 81920 | tf_op jit(solution)/shard_map/all_gather | solution.py:11
  320.3 13.2 %all_gather.46 = f32[4,16,256]{2,1,0:T(8,128)S(1)} all-gather(f32[1,16,256]{2,1,0:T(8,128)S(1)} %copy-done.121), channel_id=1, replica_groups=mesh['groups'=2,'rows'=4,'cols'=4] {'rows'}, dimensions={0}, use_global_device_ids=true | all-gather | bytes 81920 | tf_op jit(solution)/shard_map/all_gather | solution.py:11
  334.7 4.1 while.67
  343.7 14.1 %all_gather.49 = f32[4,16,256]{2,1,0:T(8,128)} all-gather(f32[1,16,256]{2,1,0:T(8,128)S(1)} %slice-done), channel_id=1, replica_groups=mesh['groups'=2,'rows'=4,'cols'=4] {'rows'}, dimensions={0}, use_global_device_ids=true | all-gather | bytes 81920 | tf_op jit(solution)/shard_map/all_gather | solution.py:11
  359.2 14.7 %all_gather.47 = f32[4,16,256]{2,1,0:T(8,128)} all-gather(f32[1,16,256]{2,1,0:T(8,128)} %slice_add_fusion.17), channel_id=1, replica_groups=mesh['groups'=2,'rows'=4,'cols'=4] {'rows'}, dimensions={0}, use_global_device_ids=true | all-gather | bytes 81920 | tf_op jit(solution)/shard_map/all_gather | solution.py:11
  375.4 4.2 while.66
  424.7 18.7 %reduce-scatter.9.cloned.1.call-done = f32[128,128]{0,1:T(8,128)} async-done(((f32[128,512]{0,1:T(8,128)}), f32[128,128]{0,1:T(8,128)}) %reduce-scatter.9.cloned.1.call-update) | async-done | bytes 65552 | tf_op jit(solution)/shard_map/reduce_scatter | solution.py:167
  446.6 18.2 %reduce-scatter.15.cloned.1.call-done = f32[64,32]{1,0:T(8,128)} async-done(((f32[256,32]{1,0:T(8,128)}), f32[64,32]{1,0:T(8,128)}) %reduce-scatter.15.cloned.1.call-update) | async-done | bytes 8208
  466.2 18.5 %reduce-scatter.13.cloned.1.call-done = f32[32,128]{1,0:T(8,128)} async-done(((f32[128,128]{1,0:T(8,128)}), f32[32,128]{1,0:T(8,128)}) %reduce-scatter.13.cloned.1.call-update) | async-done | bytes 16400
  (807 shorter events, 278.5 us)
Async XLA Ops:
  7.2 415.8 %reduce-scatter.11.cloned.1.call-start = ((), (), s32[]{:S(2)}) async-start(), calls=%async_computation.5 | async-start | bytes 163840 | tf_op jit(solution)/shard_map/reduce_scatter | solution.py:168
  68.8 3.2 copy-start.20
  68.8 5.1 %copy-start.22 = (f32[8,16,256]{2,1,0:T(8,128)}, f32[8,16,256]{2,1,0:T(8,128)S(1)}, u32[]{:S(2)}) copy-start(f32[8,16,256]{2,1,0:T(8,128)S(1)} %get-tuple-element.788) | copy-start | bytes 393220
  68.8 2.6 copy-start.24
  162.0 3.5 copy-start.4
  162.0 3.5 copy-start.6
  180.7 3.5 copy-start.54
  180.7 3.4 copy-start.56
  213.8 13.3 %copy-start.3 = (f32[16,16,256]{2,1,0:T(8,128)}, f32[16,16,256]{2,1,0:T(8,128)S(1)}, u32[]{:S(2)}) copy-start(f32[16,16,256]{2,1,0:T(8,128)S(1)} %pad.471) | copy-start | bytes 786436
  255.8 3.2 copy-start.28
  255.8 3.2 copy-start.30
  255.8 18.2 %copy-start.126 = (f32[1,16,256]{2,1,0:T(8,128)S(1)}, f32[1,16,256]{2,1,0:T(8,128)}, u32[]{:S(2)}) copy-start(f32[1,16,256]{2,1,0:T(8,128)} %slice.1578) | copy-start | bytes 49156
  259.0 15.1 %copy-start.68 = (f32[7,16,256]{2,1,0:T(8,128)S(1)}, f32[7,16,256]{2,1,0:T(8,128)}, u32[]{:S(2)}) copy-start(f32[7,16,256]{2,1,0:T(8,128)} %get-tuple-element.774) | copy-start | bytes 344068
  274.7 4.8 copy-start.42
  282.7 14.9 %copy-start.67 = (f32[7,16,256]{2,1,0:T(8,128)S(1)}, f32[7,16,256]{2,1,0:T(8,128)}, u32[]{:S(2)}) copy-start(f32[7,16,256]{2,1,0:T(8,128)} %get-tuple-element.773) | copy-start | bytes 344068
  283.5 14.2 %copy-start.147 = (f32[1,16,256]{2,1,0:T(8,128)S(1)}, f32[1,16,256]{2,1,0:T(8,128)}, u32[]{:S(2)}) copy-start(f32[1,16,256]{2,1,0:T(8,128)} %get-tuple-element.771) | copy-start | bytes 49156
  298.3 4.8 copy-start.41
  307.0 13.3 %copy-start.121 = (f32[1,16,256]{2,1,0:T(8,128)S(1)}, f32[1,16,256]{2,1,0:T(8,128)}, u32[]{:S(2)}) copy-start(f32[1,16,256]{2,1,0:T(8,128)} %slice_add_fusion.19) | copy-start | bytes 49156
  382.8 3.0 copy-start.11
  382.8 3.0 copy-start.188
  386.7 56.6 %reduce-scatter.9.cloned.1.call-start = ((), (), s32[]{:S(2)}) async-start(), calls=%async_computation.4 | async-start | bytes 327680 | tf_op jit(solution)/shard_map/reduce_scatter | solution.py:167
  391.1 2.9 copy-start.25
  423.0 41.8 %reduce-scatter.15.cloned.1.call-start = ((), (), s32[]{:S(2)}) async-start(), calls=%async_computation.7 | async-start | bytes 163840
  424.6 60.1 %reduce-scatter.13.cloned.1.call-start = ((), (), s32[]{:S(2)}) async-start(), calls=%async_computation.6 | async-start | bytes 81920
  (171 other events, 174.8 us)
Sparse Core Ops, SparseCore 0:
  386.9 19.6 reduce-scatter.10
  423.1 20.1 reduce-scatter.8
  445.6 19.1 reduce-scatter.14
  467.5 17.1 reduce-scatter.12
where the time goes:
time: 501 us; the launch traced here: 491 us
  local copies, waits for them, and re-layouts  218 us (44%)
  blocking collectives  117 us (23%)
  other arithmetic  80.9 us (16%)
  waiting for transfers between devices  55.4 us (11%)
  between operations  16 us (3%)
    all_gather x12, blocking collectives, entering(): pieces = jax.tree.map(lambda part: lax.all_gather(part, axis), value)  117 us
    unnamed x397, local copies, waits for them, and re-layouts  65.7 us
    slice x54, local copies, waits for them, and re-layouts, per_device(): lax.associative_scan(affine, (decay_now, decay_now * seed_grad), reverse=...  56.7 us
    unnamed x6, waiting for transfers between devices  36.8 us
    pad x48, local copies, waits for them, and re-layouts, per_device(): lax.associative_scan(affine, (decay_now, weight * source), reverse=backwa...  35.2 us
    slice x47, local copies, waits for them, and re-layouts, per_device(): lax.associative_scan(affine, (decay_now, weight * source), reverse=backwa...  26.9 us
    reduce_scatter x1, waiting for transfers between devices, per_device(): lax.psum_scatter(full_in, 'cols', scatter_dimension=1, tiled=True)  18.7 us
    pad x40, local copies, waits for them, and re-layouts, per_device(): lax.associative_scan(affine, (decay_now, decay_now * seed_grad), reverse=...  15.5 us
  transfers between devices with their start and end apart: 4, of which 3 were waited for; matrix products, arithmetic and copies ran while one was open for 5% of the time, Pallas kernels for 0%

commit v1 on v0

v1 whole, which is shorter than its diff:
```python
import functools

import jax
import jax.numpy as jnp
from jax import lax
from jax.experimental import pallas as pl
from jax.experimental.pallas import tpu as pltpu
from jax.sharding import PartitionSpec as P

F32 = jnp.float32
BF16 = jnp.bfloat16
contract_rows = (((0,), (0,)), ((), ()))
contract_cols = (((1,), (1,)), ((), ()))
VMEM_LIMIT = 20 * 1024 * 1024
PAD = 128


def vmem_call(body, out_shape, scratch=(), flops=0, moved=0, space=pltpu.VMEM):
    spec = pl.BlockSpec(memory_space=pltpu.VMEM)
    given = pl.BlockSpec(memory_space=space)
    return lambda *operands: pl.pallas_call(
        body,
        out_shape=out_shape,
        in_specs=[given] * len(operands),
        out_specs=jax.tree.map(lambda _: spec, out_shape),
        scratch_shapes=scratch,
        compiler_params=pltpu.CompilerParams(vmem_limit_bytes=VMEM_LIMIT),
        cost_estimate=pl.CostEstimate(flops=flops, bytes_accessed=moved, transcendentals=0),
    )(*operands)


def get(ref, rows):
    return jnp.concatenate([ref[k, rows, :] for k in range(ref.shape[0])], axis=1)


def put(ref, rows, value):
    for k in range(ref.shape[0]):
        ref[k, rows, :] = value[:, 128 * k : 128 * k + 128]


def sigmoid(value):
    return 1.0 / (1.0 + jnp.exp(-value))


def decay_pair(rate, step):
    decay = jnp.exp(-(rate * step))
    rest = 1.0 - decay * decay
    return decay, rest * lax.rsqrt(rest)


def edges_body(px_in, ct_in, wi_in, wo_in, rt_in, ss_in, e_cols, e_rows, px, ct, wi, rt, mixed, back, src, seed, dec, wgt, wo, ss, sems):
    pairs = ((px_in, px), (wi_in, wi), (ct_in, ct), (wo_in, wo), (ss_in, ss), (rt_in, rt))
    copies = [pltpu.make_async_copy(a, b, sems.at[k]) for k, (a, b) in enumerate(pairs)]
    for copy in copies:
        copy.start()
    height, breadth, channels = px.shape
    expand = wo.shape[0]
    count = height * breadth
    copies[0].wait()
    copies[1].wait()
    both = jnp.dot(px[...].reshape(count, channels), wi[...], preferred_element_type=F32)
    mixed[...] = both
    copies[2].wait()
    copies[3].wait()
    cot = ct[...].reshape(count, channels)
    bg = lax.dot_general(cot, wo[...], contract_cols, preferred_element_type=F32)
    back[...] = bg
    inner, gate = both[:, :expand], both[:, expand:]
    put(src, slice(None), inner * sigmoid(inner))
    put(seed, slice(None), bg * (gate * sigmoid(gate)))
    copies[4].wait()
    copies[5].wait()

    for axis, payload in ((0, e_cols), (1, e_rows)):
        one, two = 2 * axis, 2 * axis + 1
        length = breadth if axis == 0 else height
        lines = height if axis == 0 else breadth

        def at(ref, i):
            return get(ref, pl.ds(i, lines, stride=length) if axis == 0 else pl.ds(i * lines, lines))

        steps = [ss[d] if axis == 0 else jnp.transpose(ss[d]) for d in (one, two)]
        rates = [rt[d : d + 1, :] for d in (one, two)]
        fwd = jnp.zeros((lines, expand), F32)
        adj = jnp.zeros((lines, expand), F32)
        for i in range(length):
            rows = slice(i * lines, (i + 1) * lines)
            d1, w1 = decay_pair(rates[0], steps[0][:, i : i + 1])
            d2, w2 = decay_pair(rates[1], steps[1][:, i : i + 1])
            dec[one, rows, :] = d1
            wgt[one, rows, :] = w1
            dec[two, rows, :] = d2
            wgt[two, rows, :] = w2
            fwd = d1 * fwd + w1 * at(src, i)
            adj = d2 * (adj + at(seed, i))
        payload[0, :, 0:expand] = fwd
        payload[0, :, expand : 2 * expand] = adj
        fwd = jnp.zeros((lines, expand), F32)
        adj = jnp.zeros((lines, expand), F32)
        for i in reversed(range(length)):
            rows = slice(i * lines, (i + 1) * lines)
            d1, d2, w2 = dec[one, rows, :], dec[two, rows, :], wgt[two, rows, :]
            fwd = d2 * fwd + w2 * at(src, i)
            adj = d1 * (adj + at(seed, i))
        payload[1, :, 0:expand] = adj
        payload[1, :, expand : 2 * expand] = fwd
        lane = lax.broadcasted_iota(jnp.int32, (lines, PAD), 1)
        sums = [jnp.sum(s, axis=1, keepdims=True) for s in steps]
        for way in (0, 1):
            payload[way, :, 2 * expand :] = jnp.where(lane < PAD // 2, sums[0], sums[1])


def local_body(px, ct, mixed, back, src, seed, dec, wgt, s_loc, g_loc, pre, suf, m_in, m_gate, gated, x_t, c_t):
    height, breadth, channels = px.shape
    expand = src.shape[0] * 128
    count = height * breadth
    inner, gate = mixed[:, :expand], mixed[:, expand:]
    s_in = sigmoid(inner)
    m_in[...] = s_in * (1.0 + inner * (1.0 - s_in))
    s_gate = sigmoid(gate)
    gated[...] = gate * s_gate
    m_gate[...] = back[...] * (s_gate * (1.0 + gate * (1.0 - s_gate)))
    x_t[...] = jnp.transpose(px[...].reshape(count, channels).astype(F32)).astype(BF16)
    c_t[...] = jnp.transpose(ct[...].reshape(count, channels).astype(F32)).astype(BF16)
    for axis in (0, 1):
        one, two = 2 * axis, 2 * axis + 1
        length = breadth if axis == 0 else height
        lines = height if axis == 0 else breadth

        def where(i):
            if axis == 0:
                return pl.ds(i, lines, stride=length)
            return pl.ds(i * lines, lines)

        def go(order, a, b, first):
            state = jnp.zeros((lines, expand), F32)
            carried = jnp.zeros((lines, expand), F32)
            upto = jnp.ones((lines, expand), F32)
            after = jnp.ones((lines, expand), F32)
            for i in order:
                rows = slice(i * lines, (i + 1) * lines)
                da, wa, db, wb = dec[a, rows, :], wgt[a, rows, :], dec[b, rows, :], wgt[b, rows, :]
                state = da * state + wa * get(src, where(i))
                upto = upto * da
                adjoint = get(seed, where(i)) + carried
                carried = db * adjoint
                put(pre.at[a], where(i), upto)
                put(suf.at[b], where(i), wb * after)
                after = after * db
                grad = wb * adjoint
                if not first:
                    state_sum, grad = get(s_loc, where(i)) + state, get(g_loc, where(i)) + grad
                else:
                    state_sum = state
                put(s_loc, where(i), state_sum)
                put(g_loc, where(i), grad)

        go(range(length), one, two, axis == 0)
        go(reversed(range(length)), two, one, False)


def entering(axis, rates, parts):
    count, mine = len(parts) + 1, lax.axis_index(axis)
    expand = rates[0].shape[1]
    lines = parts[0].shape[0]
    sums = [
        jnp.concatenate([jnp.broadcast_to(part[:, c : c + 1], (lines, expand)) for c in (2 * expand, 2 * expand + PAD // 2)], axis=1)
        for part in parts
    ]
    both = jnp.concatenate(rates, axis=1)
    below = jnp.zeros((lines, 2 * expand), F32)
    above = jnp.zeros((lines, 2 * expand), F32)
    for k in range(1, count):
        place = mine ^ k
        between = jnp.zeros((lines, 2 * expand), F32)
        for m in range(1, count):
            if m == k:
                continue
            middle = mine ^ m
            inside = ((middle - mine) * (middle - place) < 0).astype(F32)
            between = between + inside * sums[m - 1]
        value = jnp.exp(-both * between) * parts[k - 1][:, : 2 * expand]
        lower = (place < mine).astype(F32)
        below = below + lower * value
        above = above + (1.0 - lower) * value
    return below, above


def join_body(shape, split, counts, rt, *refs):
    height, breadth = shape
    n_cols, n_rows = counts[0] - 1, counts[1] - 1
    from_cols, from_rows = refs[:n_cols], refs[n_cols : n_cols + n_rows]
    s_loc, g_loc, pre, suf, m_in, m_gate, gated, x_t, c_t, mix = refs[n_cols + n_rows : n_cols + n_rows + 10]
    outs = refs[n_cols + n_rows + 10 :]
    expand = s_loc.shape[0] * 128
    out_state = outs[-1]
    grads = outs[:-1]
    rates = [rt[d : d + 1, :] for d in range(4)]
    below, above = entering("rows", rates[2:], [r[...] for r in from_rows])
    f2, a3, a2, f3 = below[:, :expand], below[:, expand:], above[:, :expand], above[:, expand:]
    below, above = entering("cols", rates[:2], [r[...] for r in from_cols])
    for h in range(height):
        rows = slice(h * breadth, (h + 1) * breadth)
        f0, a1 = below[h : h + 1, :expand], below[h : h + 1, expand:]
        a0, f1 = above[h : h + 1, :expand], above[h : h + 1, expand:]
        total, grad = get(s_loc, rows), get(g_loc, rows)
        for d, (state_in, adjoint_in) in enumerate(((f0, a0), (f1, a1), (f2, a2), (f3, a3))):
            total = total + get(pre.at[d], rows) * state_in
            grad = grad + get(suf.at[d], rows) * adjoint_in
        out_state[rows, :] = (total * gated[rows, :]).astype(BF16)
        mix[rows, :expand] = (grad * m_in[rows, :]).astype(BF16)
        mix[rows, expand:] = (total * m_gate[rows, :]).astype(BF16)
    grad_in = jnp.dot(x_t[...], mix[...], preferred_element_type=F32)
    grad_out = jnp.dot(c_t[...], out_state[...], preferred_element_type=F32)
    if not split:
        grads[0][...] = grad_in
        grads[1][...] = grad_out
        return
    packed = grads[0]
    lane = lax.broadcasted_iota(jnp.int32, (16, 128), 1)
    for c in range(4):
        for t in range(2):
            top = grad_out[32 * c : 32 * c + 16, 128 * t : 128 * t + 128]
            bottom = grad_out[32 * c + 16 : 32 * c + 32, 128 * t : 128 * t + 128]
            low = jnp.where(lane < 64, top, pltpu.roll(bottom, 64, 1))
            high = jnp.where(lane < 64, pltpu.roll(top, 64, 1), bottom)
            for k, piece in ((0, low), (1, high)):
                r = 2 * t + k
                packed[c & 1, c >> 1, k, t, 0:32, :] = grad_in[32 * r : 32 * r + 32, 128 * c : 128 * c + 128]
                packed[c & 1, c >> 1, k, t, 32:48, :] = piece


def pixels_body(ct, mix, wi, out):
    height, breadth, channels = ct.shape
    grad = lax.dot_general(mix[...], wi[...], contract_cols, preferred_element_type=F32)
    cot = ct[...].reshape(height * breadth, channels).astype(F32)
    out[...] = (cot + grad).astype(BF16).reshape(height, breadth, channels)


def final_body(mine, other, g_in, g_out):
    total = mine[...] + other[...]
    g_in[...] = total[0:32, :]
    g_out[0:16, :] = total[32:48, 0:64]
    g_out[16:32, :] = total[32:48, 64:128]


def partner(value, axis, bit):
    return lax.ppermute(value, axis, [(i, i ^ bit) for i in range(lax.axis_size(axis))])


def exchange(payload, axis):
    mine = lax.axis_index(axis)
    received = []
    for k in range(1, lax.axis_size(axis)):
        way = ((mine ^ k) < mine).astype(jnp.int32)
        received.append(partner(lax.dynamic_index_in_dim(payload, way, 0, keepdims=False), axis, k))
    return received


def halve(value, axis, bit):
    mine = (lax.axis_index(axis) & bit) // bit
    pick = lambda i: lax.dynamic_index_in_dim(value, i, 0, keepdims=False)
    return pick(mine), partner(pick(1 - mine), axis, bit)


def per_device(pixels, cotangent, w_in, w_out, decay_rates, step_sizes):
    height, breadth, channels = pixels.shape
    expand = w_out.shape[0]
    count = height * breadth
    rows, cols = lax.axis_size("rows"), lax.axis_size("cols")
    full = jax.ShapeDtypeStruct((count, expand), F32)
    tall = jax.ShapeDtypeStruct((expand // 128, count, 128), F32)
    four_tall = jax.ShapeDtypeStruct((4, expand // 128, count, 128), F32)
    four = jax.ShapeDtypeStruct((4, count, expand), F32)
    wide = jax.ShapeDtypeStruct((count, 2 * expand), F32)
    like = lambda a: jax.ShapeDtypeStruct(a.shape, a.dtype)
    e_cols, e_rows, px, ct, wi, rt, mixed, back, src, seed, dec, wgt = vmem_call(
        edges_body,
        (
            jax.ShapeDtypeStruct((2, height, 2 * expand + PAD), F32),
            jax.ShapeDtypeStruct((2, breadth, 2 * expand + PAD), F32),
            like(pixels), like(cotangent), like(w_in), like(decay_rates),
            wide, full, tall, tall, four, four,
        ),
        scratch=[pltpu.VMEM(w_out.shape, BF16), pltpu.VMEM(step_sizes.shape, F32), pltpu.SemaphoreType.DMA((6,))],
        space=pl.ANY,
    )(pixels, cotangent, w_in, w_out, decay_rates, step_sizes)
    turned = jax.ShapeDtypeStruct((channels, count), BF16)
    s_loc, g_loc, pre, suf, m_in, m_gate, gated, x_t, c_t = vmem_call(
        local_body, (tall, tall, four_tall, four_tall, full, full, full, turned, turned)
    )(px, ct, mixed, back, src, seed, dec, wgt)
    from_rows = exchange(e_rows, "rows")
    from_cols = exchange(e_cols, "cols")
    split = rows == 4 and cols == 4 and channels == 128 and expand == 256
    if split:
        grads = (jax.ShapeDtypeStruct((2, 2, 2, 2, 48, 128), F32),)
    else:
        grads = (
            jax.ShapeDtypeStruct((channels, 2 * expand), F32),
            jax.ShapeDtypeStruct((channels, expand), F32),
        )
    outs = vmem_call(
        functools.partial(join_body, (height, breadth), split, (cols, rows)),
        (jax.ShapeDtypeStruct((count, 2 * expand), BF16), *grads, jax.ShapeDtypeStruct((count, expand), BF16)),
    )(rt, *from_cols, *from_rows, s_loc, g_loc, pre, suf, m_in, m_gate, gated, x_t, c_t)
    mix, grads = outs[0], outs[1:-1]
    grad_pixels = vmem_call(pixels_body, jax.ShapeDtypeStruct(pixels.shape, BF16))(ct, mix, wi)
    if split:
        value = grads[0]
        for axis, bit in (("cols", 1), ("cols", 2), ("rows", 1)):
            kept, got = halve(value, axis, bit)
            value = kept + got
        kept, got = halve(value, "rows", 2)
        grad_in, grad_out = vmem_call(
            final_body, (jax.ShapeDtypeStruct((32, 128), F32), jax.ShapeDtypeStruct((32, 64), F32))
        )(kept, got)
        return grad_pixels, grad_in, jnp.transpose(grad_out)
    full_in, full_out = grads[0], jnp.transpose(grads[1])
    full_in = lax.psum_scatter(full_in, "cols", scatter_dimension=1, tiled=True)
    full_out = lax.psum_scatter(full_out, "cols", scatter_dimension=1, tiled=True)
    return (
        grad_pixels,
        lax.psum_scatter(full_in, "rows", scatter_dimension=0, tiled=True),
        lax.psum_scatter(full_out, "rows", scatter_dimension=0, tiled=True),
    )


def solution(mesh):
    return jax.shard_map(
        per_device,
        mesh=mesh,
        in_specs=(
            P(("groups", "rows"), "cols", None),
            P(("groups", "rows"), "cols", None),
            P(),
            P(),
            P(),
            P(None, ("groups", "rows"), "cols"),
        ),
        out_specs=(
            P(("groups", "rows"), "cols", None),
            P(("groups", "rows"), "cols"),
            P(("groups", "rows"), "cols"),
        ),
        check_vma=False,
    )
```

time: 501 us -> 39.2 us (0.08); the launches traced: 491 us -> 38.7 us
  local copies, waits for them, and re-layouts: 218 us -> 7.79 us
  blocking collectives: 117 us -> 0 us
  other arithmetic: 80.9 us -> 0.04 us
  waiting for transfers between devices: 55.4 us -> 10.9 us
  between operations: 16 us -> 0.77 us
  starting transfers between devices: 0.16 us -> 12.2 us
  Pallas kernels: 0 us -> 7.01 us
    all_gather x12 -> x0, blocking collectives: 117 us -> none  [entering(): pieces = jax.tree.map(lambda part: lax.all_gather(part, axis), value)]
    slice x116 -> x0, local copies, waits for them, and re-layouts: 88.1 us -> none  [the longest x54 56.7 us: per_device(): lax.associative_scan(affine, (decay_now, decay_now * seed_grad), reverse=...]
    unnamed x397 -> x24, local copies, waits for them, and re-layouts: 65.7 us -> 6.4 us
    pad x88 -> x0, local copies, waits for them, and re-layouts: 50.7 us -> none  [the longest x48 35.2 us: per_device(): lax.associative_scan(affine, (decay_now, weight * source), reverse=backwa...]
    unnamed x6 -> x0, waiting for transfers between devices: 36.8 us -> none
    add x91 -> x3, other arithmetic: 35.2 us -> 0.04 us  [per_device(): value = kept + got]
    reduce_scatter x2 -> x0, waiting for transfers between devices: 18.7 us -> none  [the longest x1 18.7 us: per_device(): lax.psum_scatter(full_in, 'cols', scatter_dimension=1, tiled=True)]
    select_n x12 -> x0, other arithmetic: 14.9 us -> none  [step(): jnp.where(position < mine, new, old)]
  transfers between devices with their start and end apart: 4 -> 10, of which waited for: 3 -> 6; matrix products, arithmetic and copies ran while one was open for 5% -> 2% of each run, Pallas kernels for 0% -> 7%
where the time goes in v1:
time: 39.2 us; the launch traced here: 38.7 us
  starting transfers between devices  12.2 us (31%)
  waiting for transfers between devices  10.9 us (28%)
  local copies, waits for them, and re-layouts  7.79 us (20%)
  Pallas kernels  7.01 us (18%)
  between operations  0.77 us (2%)
    ppermute x10, starting transfers between devices, partner(): lax.ppermute(value, axis, [(i, i ^ bit) for i in range(lax.axis_size(axis...  12.2 us
    ppermute x10, waiting for transfers between devices, partner(): lax.ppermute(value, axis, [(i, i ^ bit) for i in range(lax.axis_size(axis...  10.9 us
    pallas_call x5, Pallas kernels, vmem_call(): pl.pallas_call(body, out_shape=out_shape, in_specs=[given] * len(operands...  7.01 us
    unnamed x24, local copies, waits for them, and re-layouts  6.4 us
    squeeze x2, local copies, waits for them, and re-layouts, exchange(): lax.dynamic_index_in_dim(payload, way, 0, keepdims=False)  1.33 us
  transfers between devices with their start and end apart: 10, of which 6 were waited for; matrix products, arithmetic and copies ran while one was open for 2% of the time, Pallas kernels for 7%

profile of v1, /device:TPU:0, one launch (start us, length us, event | category | flops | bytes accessed | tf_op | source)
XLA Modules:
  0.0 38.7 jit_solution(12554033772157460785)
XLA Ops:
  0.7 0.9 %copy-done = bf16[128,512]{1,0:T(8,128)(2,1)S(1)} copy-done((bf16[128,512]{1,0:T(8,128)(2,1)S(1)}, bf16[128,512]{1,0:T(8,128)(2,1)}, u32[]{:S(2)}) %copy-start) | copy-done | bytes 131096
  1.6 0.8 %copy-done.5 = bf16[16,16,128]{2,1,0:T(8,128)(2,1)S(1)} copy-done((bf16[16,16,128]{2,1,0:T(8,128)(2,1)S(1)}, bf16[16,16,128]{2,1,0:T(8,128)(2,1)}, u32[]{:S(2)}) %copy-start.5) | copy-done | bytes 65560
  2.4 0.8 %copy-done.6 = bf16[16,16,128]{2,1,0:T(8,128)(2,1)S(1)} copy-done((bf16[16,16,128]{2,1,0:T(8,128)(2,1)S(1)}, bf16[16,16,128]{2,1,0:T(8,128)(2,1)}, u32[]{:S(2)}) %copy-start.6) | copy-done | bytes 65560
  3.2 0.8 %copy-done.7 = bf16[256,128]{1,0:T(8,128)(2,1)S(1)} copy-done((bf16[256,128]{1,0:T(8,128)(2,1)S(1)}, bf16[256,128]{1,0:T(8,128)(2,1)}, u32[]{:S(2)}) %copy-start.7) | copy-done | bytes 65560
  4.1 0.8 %copy-done.8 = f32[4,16,16]{2,1,0:T(8,128)S(1)} copy-done((f32[4,16,16]{2,1,0:T(8,128)S(1)}, f32[4,16,16]{2,1,0:T(8,128)}, u32[]{:S(2)}) %copy-start.8) | copy-done | bytes 4120
  4.8 0.7 %copy-done.9 = f32[4,256]{1,0:T(4,128)S(1)} copy-done((f32[4,256]{1,0:T(4,128)S(1)}, f32[4,256]{1,0:T(4,128)}, u32[]{:S(2)}) %copy-start.9) | copy-done | bytes 4120
  5.5 1.8 %shard_map.85 = (f32[2,16,640]{2,1,0:T(8,128)S(1)}, f32[2,16,640]{2,1,0:T(8,128)S(1)}, bf16[16,16,128]{2,1,0:T(8,128)(2,1)S(1)}, bf16[16,16,128]{2,1,0:T(8,128)(...) custom-call(bf16[16,16,128]{2,1,0:T(8,128)(2,1)S(1)} %copy-done.5, ...), custom_call_target="tpu_custom_call" | custom-call | tf_op jit(solution)/shard_map/pallas_call | solution.py:21
  8.0 3.1 %collective-permute-start.3 = (f32[16,640]{1,0:T(8,128)}, f32[16,640]{1,0:T(8,128)}, u32[]{:S(2)}, u32[]{:S(2)}) collective-permute-start(f32[16,640]{1,0:T(8,128)} %get-tuple-element.55), channel_id=1, source_target_pairs={{0,4},{4,0},{8,12},{12,8},{1,5},{5,1},{9,13},{13,9},{2,6},{6,2},{1... | collective-permute-start | bytes 122888 | tf_op jit(solution)/shard_map/ppermute | solution.py:248
  11.1 2.6 %collective-permute-start.4 = (f32[16,640]{1,0:T(8,128)}, f32[16,640]{1,0:T(8,128)}, u32[]{:S(2)}, u32[]{:S(2)}) collective-permute-start(f32[16,640]{1,0:T(8,128)} %get-tuple-element.54), channel_id=1, source_target_pairs={{0,8},{4,12},{8,0},{12,4},{1,9},{5,13},{9,1},{13,5},{2,10},{6,14},... | collective-permute-start | bytes 122888 | tf_op jit(solution)/shard_map/ppermute | solution.py:248
  14.4 1.7 %collective-permute-start.1 = (f32[16,640]{1,0:T(8,128)}, f32[16,640]{1,0:T(8,128)S(1)}, u32[]{:S(2)}, u32[]{:S(2)}) collective-permute-start(f32[16,640]{1,0:T(8,128)} %get-tuple-element.57), channel_id=1, source_target_pairs={{0,2},{1,3},{2,0},{3,1},{4,6},{5,7},{6,4},{7,5},{8,10},{9,11},{10,... | collective-permute-start | bytes 122888 | tf_op jit(solution)/shard_map/ppermute | solution.py:248
  16.2 0.8 %copy-done.4 = bf16[16,16,128]{2,1,0:T(8,128)(2,1)S(1)} copy-done((bf16[16,16,128]{2,1,0:T(8,128)(2,1)S(1)}, bf16[16,16,128]{2,1,0:T(8,128)(2,1)}, u32[]{:S(2)}) %copy-start.4) | copy-done | bytes 65560
  17.1 1.8 %shard_map.86 = (f32[2,256,128]{2,1,0:T(8,128)S(1)}, f32[2,256,128]{2,1,0:T(8,128)S(1)}, f32[4,2,256,128]{3,2,1,0:T(8,128)S(1)}, f32[4,2,256,128]{3,2,1,0:T(8,12...) custom-call(bf16[16,16,128]{2,1,0:T(8,128)(2,1)S(1)} %copy-done.4, ...), custom_call_target="tpu_custom_call" | custom-call | tf_op jit(solution)/shard_map/pallas_call | solution.py:21
  18.9 0.9 %collective-permute-done.5.refs_5_ = f32[16,640]{1,0:T(8,128)} collective-permute-done((f32[16,640]{1,0:T(8,128)}, f32[16,640]{1,0:T(8,128)}, u32[]{:S(2)}, u32[]{:S(2)}) %collective-permute-start.5) | collective-permute-done | bytes 40992 | tf_op jit(solution)/shard_map/ppermute | solution.py:248
  19.9 0.7 %copy-done.11 = f32[4,256]{1,0:T(4,128)S(1)} copy-done((f32[4,256]{1,0:T(4,128)S(1)}, f32[4,256]{1,0:T(4,128)}, u32[]{:S(2)}) %copy-start.11) | copy-done | bytes 4120
  20.6 1.9 %shard_map.87 = (bf16[256,512]{1,0:T(8,128)(2,1)S(1)}, f32[2,2,2,2,48,128]{5,4,3,2,1,0:T(8,128)S(1)}, bf16[256,256]{1,0:T(8,128)(2,1)}) custom-call(f32[4,256]{1,0:T(4,128)S(1)} %copy-done.11, f32[16,640]{1,0:T(8,128)S(1)} %collective-permute-done.refs_0_, f32[16,640]{1,0:T(8,128)S(1)} %collective-permute-done.1.refs_1_, ...), custom_call_target="tpu_custom_call" | custom-call | tf_op jit(solution)/shard_map/pallas_call | solution.py:21
  22.7 1.3 %collective-permute-done.6 = f32[2,2,2,48,128]{4,3,2,1,0:T(8,128)S(1)} collective-permute-done((f32[2,2,2,48,128]{4,3,2,1,0:T(8,128)S(1)}, f32[2,2,2,48,128]{4,3,2,1,0:T(8,128)S(1)}, u32[]{:S(2)}, u32[]{:S(2)}) %collective-permute-start.6) | collective-permute-done | bytes 196640 | tf_op jit(solution)/shard_map/ppermute | solution.py:248
  24.1 1.5 %collective-permute-start.7 = (f32[2,2,48,128]{3,2,1,0:T(8,128)S(1)}, f32[2,2,48,128]{3,2,1,0:T(8,128)S(1)}, u32[]{:S(2)}, u32[]{:S(2)}) collective-permute-start(f32[2,2,48,128]{3,2,1,0:T(8,128)S(1)} %dynamic-slice_bitcast_fusion.1), channel_id=1, source_target_pairs={{0,2},{1,3},{2,0},{3,1},{4,6},{5,7},{6,4},{7,5},{8,10},{9,11},{10,... | collective-permute-start | bytes 294920 | tf_op jit(solution)/shard_map/ppermute | solution.py:248
  25.5 3.5 %collective-permute-done.7 = f32[2,2,48,128]{3,2,1,0:T(8,128)S(1)} collective-permute-done((f32[2,2,48,128]{3,2,1,0:T(8,128)S(1)}, f32[2,2,48,128]{3,2,1,0:T(8,128)S(1)}, u32[]{:S(2)}, u32[]{:S(2)}) %collective-permute-start.7) | collective-permute-done | bytes 98336 | tf_op jit(solution)/shard_map/ppermute | solution.py:248
  29.0 0.7 %collective-permute-start.8 = (f32[2,48,128]{2,1,0:T(8,128)S(1)}, f32[2,48,128]{2,1,0:T(8,128)S(1)}, u32[]{:S(2)}, u32[]{:S(2)}) collective-permute-start(f32[2,48,128]{2,1,0:T(8,128)S(1)} %dynamic-slice_bitcast_fusion.2), channel_id=1, source_target_pairs={{0,4},{4,0},{8,12},{12,8},{1,5},{5,1},{9,13},{13,9},{2,6},{6,2},{1... | collective-permute-start | bytes 147464 | tf_op jit(solution)/shard_map/ppermute | solution.py:248
  29.7 3.4 %collective-permute-done.8 = f32[2,48,128]{2,1,0:T(8,128)S(1)} collective-permute-done((f32[2,48,128]{2,1,0:T(8,128)S(1)}, f32[2,48,128]{2,1,0:T(8,128)S(1)}, u32[]{:S(2)}, u32[]{:S(2)}) %collective-permute-start.8) | collective-permute-done | bytes 49184 | tf_op jit(solution)/shard_map/ppermute | solution.py:248
  33.2 2.2 %collective-permute-start.9 = (f32[48,128]{1,0:T(8,128)S(1)}, f32[48,128]{1,0:T(8,128)S(1)}, u32[]{:S(2)}, u32[]{:S(2)}) collective-permute-start(f32[48,128]{1,0:T(8,128)S(1)} %get-tuple-element.59), channel_id=1, source_target_pairs={{0,8},{4,12},{8,0},{12,4},{1,9},{5,13},{9,1},{13,5},{2,10},{6,14},... | collective-permute-start | bytes 73736 | tf_op jit(solution)/shard_map/ppermute | solution.py:248
  35.4 0.9 %shard_map.88 = bf16[16,16,128]{2,1,0:T(8,128)(2,1)} custom-call(bf16[16,16,128]{2,1,0:T(8,128)(2,1)S(1)} %get-tuple-element.28.ct, bf16[256,512]{1,0:T(8,128)(2,1)S(1)} %get-tuple-element.48.mix, bf16[128,512]{1,0:T(8,128)(2,1)S(1)} %copy-done.2), custom_call_target="tpu_custom_call" | custom-call | tf_op jit(solution)/shard_map/pallas_call | solution.py:21
  36.3 1.7 %collective-permute-done.9.other = f32[48,128]{1,0:T(8,128)S(1)} collective-permute-done((f32[48,128]{1,0:T(8,128)S(1)}, f32[48,128]{1,0:T(8,128)S(1)}, u32[]{:S(2)}, u32[]{:S(2)}) %collective-permute-start.9) | collective-permute-done | bytes 24608 | tf_op jit(solution)/shard_map/ppermute | solution.py:248
  38.0 0.7 %shard_map.89 = (f32[32,128]{1,0:T(8,128)}, f32[32,64]{1,0:T(8,128)}) custom-call(f32[48,128]{1,0:T(8,128)S(1)} %get-tuple-element.60.mine, f32[48,128]{1,0:T(8,128)S(1)} %collective-permute-done.9.other), custom_call_target="tpu_custom_call" | custom-call | tf_op jit(solution)/shard_map/pallas_call | solution.py:21
  (34 shorter events, 2.0 us)
Async XLA Ops:
  0.7 0.9 %copy-start = (bf16[128,512]{1,0:T(8,128)(2,1)S(1)}, bf16[128,512]{1,0:T(8,128)(2,1)}, u32[]{:S(2)}) copy-start(bf16[128,512]{1,0:T(8,128)(2,1)} %wi_in.1) | copy-start | bytes 393220
  1.6 0.8 %copy-start.5 = (bf16[16,16,128]{2,1,0:T(8,128)(2,1)S(1)}, bf16[16,16,128]{2,1,0:T(8,128)(2,1)}, u32[]{:S(2)}) copy-start(bf16[16,16,128]{2,1,0:T(8,128)(2,1)} %px_in.1) | copy-start | bytes 196612
  2.4 0.8 %copy-start.6 = (bf16[16,16,128]{2,1,0:T(8,128)(2,1)S(1)}, bf16[16,16,128]{2,1,0:T(8,128)(2,1)}, u32[]{:S(2)}) copy-start(bf16[16,16,128]{2,1,0:T(8,128)(2,1)} %ct_in.1) | copy-start | bytes 196612
  3.2 0.8 %copy-start.7 = (bf16[256,128]{1,0:T(8,128)(2,1)S(1)}, bf16[256,128]{1,0:T(8,128)(2,1)}, u32[]{:S(2)}) copy-start(bf16[256,128]{1,0:T(8,128)(2,1)} %wo_in.1) | copy-start | bytes 196612
  4.1 0.8 %copy-start.8 = (f32[4,16,16]{2,1,0:T(8,128)S(1)}, f32[4,16,16]{2,1,0:T(8,128)}, u32[]{:S(2)}) copy-start(f32[4,16,16]{2,1,0:T(8,128)} %ss_in.1) | copy-start | bytes 12292
  4.8 0.7 %copy-start.9 = (f32[4,256]{1,0:T(4,128)S(1)}, f32[4,256]{1,0:T(4,128)}, u32[]{:S(2)}) copy-start(f32[4,256]{1,0:T(4,128)} %rt_in.1) | copy-start | bytes 12292
  7.3 0.7 %copy-start.1 = (bf16[128,512]{1,0:T(8,128)(2,1)}, bf16[128,512]{1,0:T(8,128)(2,1)S(1)}, u32[]{:S(2)}) copy-start(bf16[128,512]{1,0:T(8,128)(2,1)S(1)} %get-tuple-element.49.wi) | copy-start | bytes 393220
  7.3 0.7 %copy-start.3 = (bf16[16,16,128]{2,1,0:T(8,128)(2,1)}, bf16[16,16,128]{2,1,0:T(8,128)(2,1)S(1)}, u32[]{:S(2)}) copy-start(bf16[16,16,128]{2,1,0:T(8,128)(2,1)S(1)} %get-tuple-element.32.px) | copy-start | bytes 196612
  7.3 0.7 %copy-start.10 = (f32[4,256]{1,0:T(4,128)}, f32[4,256]{1,0:T(4,128)S(1)}, u32[]{:S(2)}) copy-start(f32[4,256]{1,0:T(4,128)S(1)} %get-tuple-element.29.rt) | copy-start | bytes 12292
  8.0 8.1 %collective-permute-start.3 = (f32[16,640]{1,0:T(8,128)}, f32[16,640]{1,0:T(8,128)}, u32[]{:S(2)}, u32[]{:S(2)}) collective-permute-start(f32[16,640]{1,0:T(8,128)} %get-tuple-element.55), channel_id=1, source_target_pairs={{0,4},{4,0},{8,12},{12,8},{1,5},{5,1},{9,13},{13,9},{2,6},{6,2},{1... | collective-permute-start | bytes 122888 | tf_op jit(solution)/shard_map/ppermute | solution.py:248
  11.1 7.8 %collective-permute-start.4 = (f32[16,640]{1,0:T(8,128)}, f32[16,640]{1,0:T(8,128)}, u32[]{:S(2)}, u32[]{:S(2)}) collective-permute-start(f32[16,640]{1,0:T(8,128)} %get-tuple-element.54), channel_id=1, source_target_pairs={{0,8},{4,12},{8,0},{12,4},{1,9},{5,13},{9,1},{13,5},{2,10},{6,14},... | collective-permute-start | bytes 122888 | tf_op jit(solution)/shard_map/ppermute | solution.py:248
  13.7 6.1 %collective-permute-start.5 = (f32[16,640]{1,0:T(8,128)}, f32[16,640]{1,0:T(8,128)}, u32[]{:S(2)}, u32[]{:S(2)}) collective-permute-start(f32[16,640]{1,0:T(8,128)} %get-tuple-element.53), channel_id=1, source_target_pairs={{0,12},{4,8},{8,4},{12,0},{1,13},{5,9},{9,5},{13,1},{2,14},{6,10},... | collective-permute-start | bytes 122888 | tf_op jit(solution)/shard_map/ppermute | solution.py:248
  14.4 5.5 %collective-permute-start = (f32[16,640]{1,0:T(8,128)}, f32[16,640]{1,0:T(8,128)S(1)}, u32[]{:S(2)}, u32[]{:S(2)}) collective-permute-start(f32[16,640]{1,0:T(8,128)} %get-tuple-element.58), channel_id=1, source_target_pairs={{0,1},{1,0},{2,3},{3,2},{4,5},{5,4},{6,7},{7,6},{8,9},{9,8},{10,11... | collective-permute-start | bytes 122888 | tf_op jit(solution)/shard_map/ppermute | solution.py:248
  14.4 5.5 %collective-permute-start.1 = (f32[16,640]{1,0:T(8,128)}, f32[16,640]{1,0:T(8,128)S(1)}, u32[]{:S(2)}, u32[]{:S(2)}) collective-permute-start(f32[16,640]{1,0:T(8,128)} %get-tuple-element.57), channel_id=1, source_target_pairs={{0,2},{1,3},{2,0},{3,1},{4,6},{5,7},{6,4},{7,5},{8,10},{9,11},{10,... | collective-permute-start | bytes 122888 | tf_op jit(solution)/shard_map/ppermute | solution.py:248
  16.1 3.9 %collective-permute-start.2 = (f32[16,640]{1,0:T(8,128)}, f32[16,640]{1,0:T(8,128)}, u32[]{:S(2)}, u32[]{:S(2)}) collective-permute-start(f32[16,640]{1,0:T(8,128)} %get-tuple-element.56), channel_id=1, source_target_pairs={{0,3},{1,2},{2,1},{3,0},{4,7},{5,6},{6,5},{7,4},{8,11},{9,10},{10,... | collective-permute-start | bytes 122888 | tf_op jit(solution)/shard_map/ppermute | solution.py:248
  16.2 0.8 %copy-start.4 = (bf16[16,16,128]{2,1,0:T(8,128)(2,1)S(1)}, bf16[16,16,128]{2,1,0:T(8,128)(2,1)}, u32[]{:S(2)}) copy-start(bf16[16,16,128]{2,1,0:T(8,128)(2,1)} %copy-done.3) | copy-start | bytes 196612
  19.9 0.7 %copy-start.11 = (f32[4,256]{1,0:T(4,128)S(1)}, f32[4,256]{1,0:T(4,128)}, u32[]{:S(2)}) copy-start(f32[4,256]{1,0:T(4,128)} %copy-done.10) | copy-start | bytes 12292
  22.5 1.5 %collective-permute-start.6 = (f32[2,2,2,48,128]{4,3,2,1,0:T(8,128)S(1)}, f32[2,2,2,48,128]{4,3,2,1,0:T(8,128)S(1)}, u32[]{:S(2)}, u32[]{:S(2)}) collective-permute-start(f32[2,2,2,48,128]{4,3,2,1,0:T(8,128)S(1)} %dynamic-slice_bitcast_fusion), channel_id=1, source_target_pairs={{0,1},{1,0},{2,3},{3,2},{4,5},{5,4},{6,7},{7,6},{8,9},{9,8},{10,11... | collective-permute-start | bytes 589832 | tf_op jit(solution)/shard_map/ppermute | solution.py:248
  24.1 4.9 %collective-permute-start.7 = (f32[2,2,48,128]{3,2,1,0:T(8,128)S(1)}, f32[2,2,48,128]{3,2,1,0:T(8,128)S(1)}, u32[]{:S(2)}, u32[]{:S(2)}) collective-permute-start(f32[2,2,48,128]{3,2,1,0:T(8,128)S(1)} %dynamic-slice_bitcast_fusion.1), channel_id=1, source_target_pairs={{0,2},{1,3},{2,0},{3,1},{4,6},{5,7},{6,4},{7,5},{8,10},{9,11},{10,... | collective-permute-start | bytes 294920 | tf_op jit(solution)/shard_map/ppermute | solution.py:248
  29.0 4.2 %collective-permute-start.8 = (f32[2,48,128]{2,1,0:T(8,128)S(1)}, f32[2,48,128]{2,1,0:T(8,128)S(1)}, u32[]{:S(2)}, u32[]{:S(2)}) collective-permute-start(f32[2,48,128]{2,1,0:T(8,128)S(1)} %dynamic-slice_bitcast_fusion.2), channel_id=1, source_target_pairs={{0,4},{4,0},{8,12},{12,8},{1,5},{5,1},{9,13},{13,9},{2,6},{6,2},{1... | collective-permute-start | bytes 147464 | tf_op jit(solution)/shard_map/ppermute | solution.py:248
  29.7 5.7 %copy-start.2 = (bf16[128,512]{1,0:T(8,128)(2,1)S(1)}, bf16[128,512]{1,0:T(8,128)(2,1)}, u32[]{:S(2)}) copy-start(bf16[128,512]{1,0:T(8,128)(2,1)} %copy-done.1) | copy-start | bytes 393220
  33.2 4.8 %collective-permute-start.9 = (f32[48,128]{1,0:T(8,128)S(1)}, f32[48,128]{1,0:T(8,128)S(1)}, u32[]{:S(2)}, u32[]{:S(2)}) collective-permute-start(f32[48,128]{1,0:T(8,128)S(1)} %get-tuple-element.59), channel_id=1, source_target_pairs={{0,8},{4,12},{8,0},{12,4},{1,9},{5,13},{9,1},{13,5},{2,10},{6,14},... | collective-permute-start | bytes 73736 | tf_op jit(solution)/shard_map/ppermute | solution.py:248

commit v2 on v1

--- a/solution.py
+++ b/solution.py
@@ -11,22 +11,28 @@
 BF16 = jnp.bfloat16
 contract_rows = (((0,), (0,)), ((), ()))
 contract_cols = (((1,), (1,)), ((), ()))
-VMEM_LIMIT = 20 * 1024 * 1024
+VMEM_LIMIT = 6 * 1024 * 1024
 PAD = 128
 
 
-def vmem_call(body, out_shape, scratch=(), flops=0, moved=0, space=pltpu.VMEM):
+def vmem_call(body, out_shape, scratch=(), given=pltpu.VMEM, kept=True):
     spec = pl.BlockSpec(memory_space=pltpu.VMEM)
-    given = pl.BlockSpec(memory_space=space)
-    return lambda *operands: pl.pallas_call(
-        body,
-        out_shape=out_shape,
-        in_specs=[given] * len(operands),
-        out_specs=jax.tree.map(lambda _: spec, out_shape),
-        scratch_shapes=scratch,
-        compiler_params=pltpu.CompilerParams(vmem_limit_bytes=VMEM_LIMIT),
-        cost_estimate=pl.CostEstimate(flops=flops, bytes_accessed=moved, transcendentals=0),
-    )(*operands)
+    if kept:
+        out_shape = jax.tree.map(lambda s: pltpu.VMEM(s.shape, s.dtype), out_shape)
+
+    def call(*operands):
+        operands = [pltpu.with_memory_space_constraint(a, given) for a in operands]
+        return pl.pallas_call(
+            body,
+            out_shape=out_shape,
+            in_specs=[pl.BlockSpec(memory_space=given)] * len(operands),
+            out_specs=jax.tree.map(lambda _: spec, out_shape),
+            scratch_shapes=scratch,
+            compiler_params=pltpu.CompilerParams(vmem_limit_bytes=VMEM_LIMIT),
+            cost_estimate=pl.CostEstimate(flops=0, bytes_accessed=0, transcendentals=0),
+        )(*operands)
+
+    return call
 
 
 def get(ref, rows):
@@ -48,7 +54,10 @@
     return decay, rest * lax.rsqrt(rest)
 
 
-def edges_body(px_in, ct_in, wi_in, wo_in, rt_in, ss_in, e_cols, e_rows, px, ct, wi, rt, mixed, back, src, seed, dec, wgt, wo, ss, sems):
+def edges_body(counts, px_in, ct_in, wi_in, wo_in, rt_in, ss_in, *refs):
+    n_cols, n_rows = counts[0] - 1, counts[1] - 1
+    sent = (refs[:n_cols], refs[n_cols : n_cols + n_rows])
+    px, ct, wi, rt, ss, mixed, back, src, seed, dec, wgt, wo, ways, sems = refs[n_cols + n_rows :]
     pairs = ((px_in, px), (wi_in, wi), (ct_in, ct), (wo_in, wo), (ss_in, ss), (rt_in, rt))
     copies = [pltpu.make_async_copy(a, b, sems.at[k]) for k, (a, b) in enumerate(pairs)]
     for copy in copies:
@@ -71,7 +80,8 @@
     copies[4].wait()
     copies[5].wait()
 
-    for axis, payload in ((0, e_cols), (1, e_rows)):
+    for axis, name in ((0, "cols"), (1, "rows")):
+        payload = ways.at[axis]
         one, two = 2 * axis, 2 * axis + 1
         length = breadth if axis == 0 else height
         lines = height if axis == 0 else breadth
@@ -108,9 +118,12 @@
         sums = [jnp.sum(s, axis=1, keepdims=True) for s in steps]
         for way in (0, 1):
             payload[way, :, 2 * expand :] = jnp.where(lane < PAD // 2, sums[0], sums[1])
-
-
-def local_body(px, ct, mixed, back, src, seed, dec, wgt, s_loc, g_loc, pre, suf, m_in, m_gate, gated, x_t, c_t):
+        mine = lax.axis_index(name)
+        for k, out in enumerate(sent[axis], 1):
+            out[...] = payload[((mine ^ k) < mine).astype(jnp.int32)]
+
+
+def local_body(px, ct, rt, ss, mixed, back, s_loc, g_loc, pre, suf, m_in, m_gate, gated, x_t, c_t, src, seed):
     height, breadth, channels = px.shape
     expand = src.shape[0] * 128
     count = height * breadth
@@ -118,7 +131,10 @@
     s_in = sigmoid(inner)
     m_in[...] = s_in * (1.0 + inner * (1.0 - s_in))
     s_gate = sigmoid(gate)
-    gated[...] = gate * s_gate
+    gate_silu = gate * s_gate
+    gated[...] = gate_silu
+    put(src, slice(None), inner * s_in)
+    put(seed, slice(None), back[...] * gate_silu)
     m_gate[...] = back[...] * (s_gate * (1.0 + gate * (1.0 - s_gate)))
     x_t[...] = jnp.transpose(px[...].reshape(count, channels).astype(F32)).astype(BF16)
     c_t[...] = jnp.transpose(ct[...].reshape(count, channels).astype(F32)).astype(BF16)
@@ -132,14 +148,16 @@
                 return pl.ds(i, lines, stride=length)
             return pl.ds(i * lines, lines)
 
+        steps = {d: ss[d] if axis == 0 else jnp.transpose(ss[d]) for d in (one, two)}
+
         def go(order, a, b, first):
             state = jnp.zeros((lines, expand), F32)
             carried = jnp.zeros((lines, expand), F32)
             upto = jnp.ones((lines, expand), F32)
             after = jnp.ones((lines, expand), F32)
             for i in order:
-                rows = slice(i * lines, (i + 1) * lines)
-                da, wa, db, wb = dec[a, rows, :], wgt[a, rows, :], dec[b, rows, :], wgt[b, rows, :]
+                da, wa = decay_pair(rt[a : a + 1, :], steps[a][:, i : i + 1])
+                db, wb = decay_pair(rt[b : b + 1, :], steps[b][:, i : i + 1])
                 state = da * state + wa * get(src, where(i))
                 upto = upto * da
                 adjoint = get(seed, where(i)) + carried
@@ -248,13 +266,8 @@
     return lax.ppermute(value, axis, [(i, i ^ bit) for i in range(lax.axis_size(axis))])
 
 
-def exchange(payload, axis):
-    mine = lax.axis_index(axis)
-    received = []
-    for k in range(1, lax.axis_size(axis)):
-        way = ((mine ^ k) < mine).astype(jnp.int32)
-        received.append(partner(lax.dynamic_index_in_dim(payload, way, 0, keepdims=False), axis, k))
-    return received
+def exchange(payloads, axis):
+    return [partner(payload, axis, k) for k, payload in enumerate(payloads, 1)]
 
 
 def halve(value, axis, bit):
@@ -274,23 +287,30 @@
     four = jax.ShapeDtypeStruct((4, count, expand), F32)
     wide = jax.ShapeDtypeStruct((count, 2 * expand), F32)
     like = lambda a: jax.ShapeDtypeStruct(a.shape, a.dtype)
-    e_cols, e_rows, px, ct, wi, rt, mixed, back, src, seed, dec, wgt = vmem_call(
-        edges_body,
-        (
-            jax.ShapeDtypeStruct((2, height, 2 * expand + PAD), F32),
-            jax.ShapeDtypeStruct((2, breadth, 2 * expand + PAD), F32),
-            like(pixels), like(cotangent), like(w_in), like(decay_rates),
-            wide, full, tall, tall, four, four,
-        ),
-        scratch=[pltpu.VMEM(w_out.shape, BF16), pltpu.VMEM(step_sizes.shape, F32), pltpu.SemaphoreType.DMA((6,))],
-        space=pl.ANY,
+    pay_cols = jax.ShapeDtypeStruct((height, 2 * expand + PAD), F32)
+    pay_rows = jax.ShapeDtypeStruct((breadth, 2 * expand + PAD), F32)
+    pays = (pay_cols,) * (cols - 1) + (pay_rows,) * (rows - 1)
+    outs = vmem_call(
+        functools.partial(edges_body, (cols, rows)),
+        (*pays, like(pixels), like(cotangent), like(w_in), like(decay_rates), like(step_sizes), wide, full),
+        scratch=[
+            *(pltpu.VMEM(s.shape, F32) for s in (tall, tall, four, four)),
+            pltpu.VMEM(w_out.shape, BF16),
+            pltpu.VMEM((2, 2, *pay_cols.shape), F32),
+            pltpu.SemaphoreType.DMA((6,)),
+        ],
+        given=pltpu.HBM,
     )(pixels, cotangent, w_in, w_out, decay_rates, step_sizes)
+    sent = outs[: len(pays)]
+    px, ct, wi, rt, ss, mixed, back = outs[len(pays) :]
     turned = jax.ShapeDtypeStruct((channels, count), BF16)
     s_loc, g_loc, pre, suf, m_in, m_gate, gated, x_t, c_t = vmem_call(
-        local_body, (tall, tall, four_tall, four_tall, full, full, full, turned, turned)
-    )(px, ct, mixed, back, src, seed, dec, wgt)
-    from_rows = exchange(e_rows, "rows")
-    from_cols = exchange(e_cols, "cols")
+        local_body,
+        (tall, tall, four_tall, four_tall, full, full, full, turned, turned),
+        scratch=[pltpu.VMEM(tall.shape, F32)] * 2,
+    )(px, ct, rt, ss, mixed, back)
+    from_rows = exchange(sent[cols - 1 :], "rows")
+    from_cols = exchange(sent[: cols - 1], "cols")
     split = rows == 4 and cols == 4 and channels == 128 and expand == 256
     if split:
         grads = (jax.ShapeDtypeStruct((2, 2, 2, 2, 48, 128), F32),)
@@ -304,7 +324,7 @@
         (jax.ShapeDtypeStruct((count, 2 * expand), BF16), *grads, jax.ShapeDtypeStruct((count, expand), BF16)),
     )(rt, *from_cols, *from_rows, s_loc, g_loc, pre, suf, m_in, m_gate, gated, x_t, c_t)
     mix, grads = outs[0], outs[1:-1]
-    grad_pixels = vmem_call(pixels_body, jax.ShapeDtypeStruct(pixels.shape, BF16))(ct, mix, wi)
+    grad_pixels = vmem_call(pixels_body, like(pixels), kept=False)(ct, mix, wi)
     if split:
         value = grads[0]
         for axis, bit in (("cols", 1), ("cols", 2), ("rows", 1)):
@@ -312,7 +332,7 @@
             value = kept + got
         kept, got = halve(value, "rows", 2)
         grad_in, grad_out = vmem_call(
-            final_body, (jax.ShapeDtypeStruct((32, 128), F32), jax.ShapeDtypeStruct((32, 64), F32))
+            final_body, (jax.ShapeDtypeStruct((32, 128), F32), jax.ShapeDtypeStruct((32, 64), F32)), kept=False
         )(kept, got)
         return grad_pixels, grad_in, jnp.transpose(grad_out)
     full_in, full_out = grads[0], jnp.transpose(grads[1])

time: 39.2 us -> 33.6 us (0.86)
  local copies, waits for them, and re-layouts: 7.79 us -> 0.06 us
  waiting for transfers between devices: 10.9 us -> 16 us
  starting transfers between devices: 12.2 us -> 9.6 us
    unnamed x24 -> x0, local copies, waits for them, and re-layouts: 6.4 us -> none
    ppermute x10, waiting for transfers between devices: 10.9 us -> 16 us  [partner(): lax.ppermute(value, axis, [(i, i ^ bit) for i in range(lax.axis_size(axis...]
    ppermute x10, starting transfers between devices: 12.2 us -> 9.6 us  [partner(): lax.ppermute(value, axis, [(i, i ^ bit) for i in range(lax.axis_size(axis...]
    squeeze x2 -> x0, local copies, waits for them, and re-layouts: 1.33 us -> none  [exchange(): lax.dynamic_index_in_dim(payload, way, 0, keepdims=False)]
  transfers between devices with their start and end apart: 10 -> 10, of which waited for: 6 -> 6; matrix products, arithmetic and copies ran while one was open for 2% -> 0% of each run, Pallas kernels for 7% -> 9%
where the time goes in v2:
time: 33.6 us; the launch traced here: 33.4 us
  waiting for transfers between devices  16 us (48%)
  starting transfers between devices  9.6 us (29%)
  Pallas kernels  6.93 us (21%)
  between operations  0.78 us (2%)
    ppermute x10, waiting for transfers between devices, partner(): lax.ppermute(value, axis, [(i, i ^ bit) for i in range(lax.axis_size(axis...  16 us
    ppermute x10, starting transfers between devices, partner(): lax.ppermute(value, axis, [(i, i ^ bit) for i in range(lax.axis_size(axis...  9.6 us
    pallas_call x5, Pallas kernels, call(): pl.pallas_call(body, out_shape=out_shape, in_specs=[pl.BlockSpec(memory_s...  6.93 us
  transfers between devices with their start and end apart: 10, of which 6 were waited for; matrix products, arithmetic and copies ran while one was open for 0% of the time, Pallas kernels for 9%

profile of v2, /device:TPU:0, one launch (start us, length us, event | category | flops | bytes accessed | tf_op | source)
XLA Modules:
  0.0 33.4 jit_solution(12845635985144913772)
XLA Ops:
  0.6 2.2 %shard_map.85 = (f32[16,640]{1,0:T(8,128)S(1)}, f32[16,640]{1,0:T(8,128)S(1)}, f32[16,640]{1,0:T(8,128)S(1)}, f32[16,640]{1,0:T(8,128)S(1)}, f32[16,640]{1,0:T(8...) custom-call(bf16[16,16,128]{2,1,0:T(8,128)(2,1)} %px_in.1, ...), custom_call_target="tpu_custom_call" | custom-call | tf_op jit(solution)/shard_map/pallas_call | solution.py:25
  2.9 0.5 %collective-permute-start = (f32[16,640]{1,0:T(8,128)S(1)}, f32[16,640]{1,0:T(8,128)S(1)}, u32[]{:S(2)}, u32[]{:S(2)}) collective-permute-start(f32[16,640]{1,0:T(8,128)S(1)} %get-tuple-element.31), channel_id=1, source_target_pairs={{0,1},{1,0},{2,3},{3,2},{4,5},{5,4},{6,7},{7,6},{8,9},{9,8},{10,11... | collective-permute-start | bytes 122888 | tf_op jit(solution)/shard_map/ppermute | solution.py:266
  3.4 2.6 %collective-permute-start.1 = (f32[16,640]{1,0:T(8,128)S(1)}, f32[16,640]{1,0:T(8,128)S(1)}, u32[]{:S(2)}, u32[]{:S(2)}) collective-permute-start(f32[16,640]{1,0:T(8,128)S(1)} %get-tuple-element.32), channel_id=1, source_target_pairs={{0,2},{1,3},{2,0},{3,1},{4,6},{5,7},{6,4},{7,5},{8,10},{9,11},{10,... | collective-permute-start | bytes 122888 | tf_op jit(solution)/shard_map/ppermute | solution.py:266
  5.9 0.1 collective-permute-start.2
  6.0 1.8 %collective-permute-start.3 = (f32[16,640]{1,0:T(8,128)S(1)}, f32[16,640]{1,0:T(8,128)S(1)}, u32[]{:S(2)}, u32[]{:S(2)}) collective-permute-start(f32[16,640]{1,0:T(8,128)S(1)} %get-tuple-element.34), channel_id=1, source_target_pairs={{0,4},{4,0},{8,12},{12,8},{1,5},{5,1},{9,13},{13,9},{2,6},{6,2},{1... | collective-permute-start | bytes 122888 | tf_op jit(solution)/shard_map/ppermute | solution.py:266
  7.8 2.6 %collective-permute-start.4 = (f32[16,640]{1,0:T(8,128)S(1)}, f32[16,640]{1,0:T(8,128)S(1)}, u32[]{:S(2)}, u32[]{:S(2)}) collective-permute-start(f32[16,640]{1,0:T(8,128)S(1)} %get-tuple-element.35), channel_id=1, source_target_pairs={{0,8},{4,12},{8,0},{12,4},{1,9},{5,13},{9,1},{13,5},{2,10},{6,14},... | collective-permute-start | bytes 122888 | tf_op jit(solution)/shard_map/ppermute | solution.py:266
  10.4 0.0 collective-permute-done.refs_0_
  10.4 0.0 collective-permute-start.5
  10.4 2.2 %shard_map.86 = (f32[2,256,128]{2,1,0:T(8,128)S(1)}, f32[2,256,128]{2,1,0:T(8,128)S(1)}, f32[4,2,256,128]{3,2,1,0:T(8,128)S(1)}, f32[4,2,256,128]{3,2,1,0:T(8,12...) custom-call(bf16[16,16,128]{2,1,0:T(8,128)(2,1)S(1)} %get-tuple-elem, ...), custom_call_target="tpu_custom_call" | custom-call | tf_op jit(solution)/shard_map/pallas_call | solution.py:25
  12.6 0.0 collective-permute-done.2.refs_2_
  12.6 0.0 collective-permute-done.3.refs_3_
  12.6 0.8 %collective-permute-done.4.refs_4_ = f32[16,640]{1,0:T(8,128)S(1)} collective-permute-done((f32[16,640]{1,0:T(8,128)S(1)}, f32[16,640]{1,0:T(8,128)S(1)}, u32[]{:S(2)}, u32[]{:S(2)}) %collective-permute-start.4) | collective-permute-done | bytes 40992 | tf_op jit(solution)/shard_map/ppermute | solution.py:266
  13.5 2.7 %collective-permute-done.5.refs_5_ = f32[16,640]{1,0:T(8,128)S(1)} collective-permute-done((f32[16,640]{1,0:T(8,128)S(1)}, f32[16,640]{1,0:T(8,128)S(1)}, u32[]{:S(2)}, u32[]{:S(2)}) %collective-permute-start.5) | collective-permute-done | bytes 40992 | tf_op jit(solution)/shard_map/ppermute | solution.py:266
  16.2 1.0 %shard_map.87 = (bf16[256,512]{1,0:T(8,128)(2,1)S(1)}, f32[2,2,2,2,48,128]{5,4,3,2,1,0:T(8,128)S(1)}, bf16[256,256]{1,0:T(8,128)(2,1)}) custom-call(f32[4,256]{1,0:T(4,128)S(1)} %get-tuple-element.30.rt, f32[16,640]{1,0:T(8,128)S(1)} %collective-permute-done.refs_0_, f32[16,640]{1,0:T(8,128)S(1)} %collective-permute-done.1.refs_1_, ...), custom_call_target="tpu_custom_call" | custom-call | tf_op jit(solution)/shard_map/pallas_call | solution.py:25
  17.3 0.1 collective-permute-start.6
  17.4 1.4 %collective-permute-done.6 = f32[2,2,2,48,128]{4,3,2,1,0:T(8,128)S(1)} collective-permute-done((f32[2,2,2,48,128]{4,3,2,1,0:T(8,128)S(1)}, f32[2,2,2,48,128]{4,3,2,1,0:T(8,128)S(1)}, u32[]{:S(2)}, u32[]{:S(2)}) %collective-permute-start.6) | collective-permute-done | bytes 196640 | tf_op jit(solution)/shard_map/ppermute | solution.py:266
  18.8 1.6 %collective-permute-start.7 = (f32[2,2,48,128]{3,2,1,0:T(8,128)S(1)}, f32[2,2,48,128]{3,2,1,0:T(8,128)S(1)}, u32[]{:S(2)}, u32[]{:S(2)}) collective-permute-start(f32[2,2,48,128]{3,2,1,0:T(8,128)S(1)} %dynamic-slice_bitcast_fusion.1), channel_id=1, source_target_pairs={{0,2},{1,3},{2,0},{3,1},{4,6},{5,7},{6,4},{7,5},{8,10},{9,11},{10,... | collective-permute-start | bytes 294920 | tf_op jit(solution)/shard_map/ppermute | solution.py:266
  20.4 3.3 %collective-permute-done.7 = f32[2,2,48,128]{3,2,1,0:T(8,128)S(1)} collective-permute-done((f32[2,2,48,128]{3,2,1,0:T(8,128)S(1)}, f32[2,2,48,128]{3,2,1,0:T(8,128)S(1)}, u32[]{:S(2)}, u32[]{:S(2)}) %collective-permute-start.7) | collective-permute-done | bytes 98336 | tf_op jit(solution)/shard_map/ppermute | solution.py:266
  23.8 0.1 collective-permute-start.8
  23.9 4.1 %collective-permute-done.8 = f32[2,48,128]{2,1,0:T(8,128)S(1)} collective-permute-done((f32[2,48,128]{2,1,0:T(8,128)S(1)}, f32[2,48,128]{2,1,0:T(8,128)S(1)}, u32[]{:S(2)}, u32[]{:S(2)}) %collective-permute-start.8) | collective-permute-done | bytes 49184 | tf_op jit(solution)/shard_map/ppermute | solution.py:266
  27.9 0.3 %collective-permute-start.9 = (f32[48,128]{1,0:T(8,128)S(1)}, f32[48,128]{1,0:T(8,128)S(1)}, u32[]{:S(2)}, u32[]{:S(2)}) collective-permute-start(f32[48,128]{1,0:T(8,128)S(1)} %get-tuple-element.55), channel_id=1, source_target_pairs={{0,8},{4,12},{8,0},{12,4},{1,9},{5,13},{9,1},{13,5},{2,10},{6,14},... | collective-permute-start | bytes 73736 | tf_op jit(solution)/shard_map/ppermute | solution.py:266
  28.3 0.9 %shard_map.88 = bf16[16,16,128]{2,1,0:T(8,128)(2,1)} custom-call(bf16[16,16,128]{2,1,0:T(8,128)(2,1)S(1)} %get-tuple-element.29.ct, bf16[256,512]{1,0:T(8,128)(2,1)S(1)} %get-tuple-element.50.mix, bf16[128,512]{1,0:T(8,128)(2,1)S(1)} %get-tuple-element.51.wi), custom_call_target="tpu_custom_call" | custom-call | tf_op jit(solution)/shard_map/pallas_call | solution.py:25
  29.1 3.6 %collective-permute-done.9.other = f32[48,128]{1,0:T(8,128)S(1)} collective-permute-done((f32[48,128]{1,0:T(8,128)S(1)}, f32[48,128]{1,0:T(8,128)S(1)}, u32[]{:S(2)}, u32[]{:S(2)}) %collective-permute-start.9) | collective-permute-done | bytes 24608 | tf_op jit(solution)/shard_map/ppermute | solution.py:266
  32.7 0.7 %shard_map.89 = (f32[32,128]{1,0:T(8,128)}, f32[32,64]{1,0:T(8,128)}) custom-call(f32[48,128]{1,0:T(8,128)S(1)} %get-tuple-element.56.mine, f32[48,128]{1,0:T(8,128)S(1)} %collective-permute-done.9.other), custom_call_target="tpu_custom_call" | custom-call | tf_op jit(solution)/shard_map/pallas_call | solution.py:25
  (8 shorter events, 0.1 us)
Async XLA Ops:
  2.9 7.6 %collective-permute-start = (f32[16,640]{1,0:T(8,128)S(1)}, f32[16,640]{1,0:T(8,128)S(1)}, u32[]{:S(2)}, u32[]{:S(2)}) collective-permute-start(f32[16,640]{1,0:T(8,128)S(1)} %get-tuple-element.31), channel_id=1, source_target_pairs={{0,1},{1,0},{2,3},{3,2},{4,5},{5,4},{6,7},{7,6},{8,9},{9,8},{10,11... | collective-permute-start | bytes 122888 | tf_op jit(solution)/shard_map/ppermute | solution.py:266
  3.4 9.2 %collective-permute-start.1 = (f32[16,640]{1,0:T(8,128)S(1)}, f32[16,640]{1,0:T(8,128)S(1)}, u32[]{:S(2)}, u32[]{:S(2)}) collective-permute-start(f32[16,640]{1,0:T(8,128)S(1)} %get-tuple-element.32), channel_id=1, source_target_pairs={{0,2},{1,3},{2,0},{3,1},{4,6},{5,7},{6,4},{7,5},{8,10},{9,11},{10,... | collective-permute-start | bytes 122888 | tf_op jit(solution)/shard_map/ppermute | solution.py:266
  5.9 6.7 %collective-permute-start.2 = (f32[16,640]{1,0:T(8,128)S(1)}, f32[16,640]{1,0:T(8,128)S(1)}, u32[]{:S(2)}, u32[]{:S(2)}) collective-permute-start(f32[16,640]{1,0:T(8,128)S(1)} %get-tuple-element.33), channel_id=1, source_target_pairs={{0,3},{1,2},{2,1},{3,0},{4,7},{5,6},{6,5},{7,4},{8,11},{9,10},{10,... | collective-permute-start | bytes 122888 | tf_op jit(solution)/shard_map/ppermute | solution.py:266
  6.0 6.6 %collective-permute-start.3 = (f32[16,640]{1,0:T(8,128)S(1)}, f32[16,640]{1,0:T(8,128)S(1)}, u32[]{:S(2)}, u32[]{:S(2)}) collective-permute-start(f32[16,640]{1,0:T(8,128)S(1)} %get-tuple-element.34), channel_id=1, source_target_pairs={{0,4},{4,0},{8,12},{12,8},{1,5},{5,1},{9,13},{13,9},{2,6},{6,2},{1... | collective-permute-start | bytes 122888 | tf_op jit(solution)/shard_map/ppermute | solution.py:266
  7.8 5.6 %collective-permute-start.4 = (f32[16,640]{1,0:T(8,128)S(1)}, f32[16,640]{1,0:T(8,128)S(1)}, u32[]{:S(2)}, u32[]{:S(2)}) collective-permute-start(f32[16,640]{1,0:T(8,128)S(1)} %get-tuple-element.35), channel_id=1, source_target_pairs={{0,8},{4,12},{8,0},{12,4},{1,9},{5,13},{9,1},{13,5},{2,10},{6,14},... | collective-permute-start | bytes 122888 | tf_op jit(solution)/shard_map/ppermute | solution.py:266
  10.4 5.8 %collective-permute-start.5 = (f32[16,640]{1,0:T(8,128)S(1)}, f32[16,640]{1,0:T(8,128)S(1)}, u32[]{:S(2)}, u32[]{:S(2)}) collective-permute-start(f32[16,640]{1,0:T(8,128)S(1)} %get-tuple-element.36), channel_id=1, source_target_pairs={{0,12},{4,8},{8,4},{12,0},{1,13},{5,9},{9,5},{13,1},{2,14},{6,10},... | collective-permute-start | bytes 122888 | tf_op jit(solution)/shard_map/ppermute | solution.py:266
  17.3 1.5 %collective-permute-start.6 = (f32[2,2,2,48,128]{4,3,2,1,0:T(8,128)S(1)}, f32[2,2,2,48,128]{4,3,2,1,0:T(8,128)S(1)}, u32[]{:S(2)}, u32[]{:S(2)}) collective-permute-start(f32[2,2,2,48,128]{4,3,2,1,0:T(8,128)S(1)} %dynamic-slice_bitcast_fusion), channel_id=1, source_target_pairs={{0,1},{1,0},{2,3},{3,2},{4,5},{5,4},{6,7},{7,6},{8,9},{9,8},{10,11... | collective-permute-start | bytes 589832 | tf_op jit(solution)/shard_map/ppermute | solution.py:266
  18.8 4.9 %collective-permute-start.7 = (f32[2,2,48,128]{3,2,1,0:T(8,128)S(1)}, f32[2,2,48,128]{3,2,1,0:T(8,128)S(1)}, u32[]{:S(2)}, u32[]{:S(2)}) collective-permute-start(f32[2,2,48,128]{3,2,1,0:T(8,128)S(1)} %dynamic-slice_bitcast_fusion.1), channel_id=1, source_target_pairs={{0,2},{1,3},{2,0},{3,1},{4,6},{5,7},{6,4},{7,5},{8,10},{9,11},{10,... | collective-permute-start | bytes 294920 | tf_op jit(solution)/shard_map/ppermute | solution.py:266
  23.8 4.2 %collective-permute-start.8 = (f32[2,48,128]{2,1,0:T(8,128)S(1)}, f32[2,48,128]{2,1,0:T(8,128)S(1)}, u32[]{:S(2)}, u32[]{:S(2)}) collective-permute-start(f32[2,48,128]{2,1,0:T(8,128)S(1)} %dynamic-slice_bitcast_fusion.2), channel_id=1, source_target_pairs={{0,4},{4,0},{8,12},{12,8},{1,5},{5,1},{9,13},{13,9},{2,6},{6,2},{1... | collective-permute-start | bytes 147464 | tf_op jit(solution)/shard_map/ppermute | solution.py:266
  27.9 4.8 %collective-permute-start.9 = (f32[48,128]{1,0:T(8,128)S(1)}, f32[48,128]{1,0:T(8,128)S(1)}, u32[]{:S(2)}, u32[]{:S(2)}) collective-permute-start(f32[48,128]{1,0:T(8,128)S(1)} %get-tuple-element.55), channel_id=1, source_target_pairs={{0,8},{4,12},{8,0},{12,4},{1,9},{5,13},{9,1},{13,5},{2,10},{6,14},... | collective-permute-start | bytes 73736 | tf_op jit(solution)/shard_map/ppermute | solution.py:266

commit v3 on v2

--- a/solution.py
+++ b/solution.py
@@ -54,10 +54,9 @@
     return decay, rest * lax.rsqrt(rest)
 
 
-def edges_body(counts, px_in, ct_in, wi_in, wo_in, rt_in, ss_in, *refs):
-    n_cols, n_rows = counts[0] - 1, counts[1] - 1
-    sent = (refs[:n_cols], refs[n_cols : n_cols + n_rows])
-    px, ct, wi, rt, ss, mixed, back, src, seed, dec, wgt, wo, ways, sems = refs[n_cols + n_rows :]
+def edges_body(order, px_in, ct_in, wi_in, wo_in, rt_in, ss_in, *refs):
+    sent = refs[: len(order)]
+    px, ct, wi, rt, ss, mixed, back, src, seed, dec, wgt, wo, ways, sems = refs[len(order) :]
     pairs = ((px_in, px), (wi_in, wi), (ct_in, ct), (wo_in, wo), (ss_in, ss), (rt_in, rt))
     copies = [pltpu.make_async_copy(a, b, sems.at[k]) for k, (a, b) in enumerate(pairs)]
     for copy in copies:
@@ -119,8 +118,9 @@
         for way in (0, 1):
             payload[way, :, 2 * expand :] = jnp.where(lane < PAD // 2, sums[0], sums[1])
         mine = lax.axis_index(name)
-        for k, out in enumerate(sent[axis], 1):
-            out[...] = payload[((mine ^ k) < mine).astype(jnp.int32)]
+        for (out_axis, k), out in zip(order, sent):
+            if out_axis == name:
+                out[...] = payload[((mine ^ k) < mine).astype(jnp.int32)]
 
 
 def local_body(px, ct, rt, ss, mixed, back, s_loc, g_loc, pre, suf, m_in, m_gate, gated, x_t, c_t, src, seed):
@@ -177,7 +177,8 @@
         go(reversed(range(length)), two, one, False)
 
 
-def entering(axis, rates, parts):
+def entering(axis, rates, received):
+    parts = [received[key] for key in sorted(received) if key[0] == axis]
     count, mine = len(parts) + 1, lax.axis_index(axis)
     expand = rates[0].shape[1]
     lines = parts[0].shape[0]
@@ -204,19 +205,18 @@
     return below, above
 
 
-def join_body(shape, split, counts, rt, *refs):
+def join_body(shape, split, order, rt, *refs):
     height, breadth = shape
-    n_cols, n_rows = counts[0] - 1, counts[1] - 1
-    from_cols, from_rows = refs[:n_cols], refs[n_cols : n_cols + n_rows]
-    s_loc, g_loc, pre, suf, m_in, m_gate, gated, x_t, c_t, mix = refs[n_cols + n_rows : n_cols + n_rows + 10]
-    outs = refs[n_cols + n_rows + 10 :]
+    received = {key: ref[...] for key, ref in zip(order, refs)}
+    s_loc, g_loc, pre, suf, m_in, m_gate, gated, x_t, c_t, mix = refs[len(order) : len(order) + 10]
+    outs = refs[len(order) + 10 :]
     expand = s_loc.shape[0] * 128
     out_state = outs[-1]
     grads = outs[:-1]
     rates = [rt[d : d + 1, :] for d in range(4)]
-    below, above = entering("rows", rates[2:], [r[...] for r in from_rows])
+    below, above = entering("rows", rates[2:], received)
     f2, a3, a2, f3 = below[:, :expand], below[:, expand:], above[:, :expand], above[:, expand:]
-    below, above = entering("cols", rates[:2], [r[...] for r in from_cols])
+    below, above = entering("cols", rates[:2], received)
     for h in range(height):
         rows = slice(h * breadth, (h + 1) * breadth)
         f0, a1 = below[h : h + 1, :expand], below[h : h + 1, expand:]
@@ -266,8 +266,8 @@
     return lax.ppermute(value, axis, [(i, i ^ bit) for i in range(lax.axis_size(axis))])
 
 
-def exchange(payloads, axis):
-    return [partner(payload, axis, k) for k, payload in enumerate(payloads, 1)]
+def send_order(cols, rows):
+    return [("rows", k) for k in reversed(range(1, rows))] + [("cols", k) for k in reversed(range(1, cols))]
 
 
 def halve(value, axis, bit):
@@ -289,9 +289,10 @@
     like = lambda a: jax.ShapeDtypeStruct(a.shape, a.dtype)
     pay_cols = jax.ShapeDtypeStruct((height, 2 * expand + PAD), F32)
     pay_rows = jax.ShapeDtypeStruct((breadth, 2 * expand + PAD), F32)
-    pays = (pay_cols,) * (cols - 1) + (pay_rows,) * (rows - 1)
+    order = send_order(cols, rows)
+    pays = tuple(pay_cols if axis == "cols" else pay_rows for axis, _ in order)
     outs = vmem_call(
-        functools.partial(edges_body, (cols, rows)),
+        functools.partial(edges_body, order),
         (*pays, like(pixels), like(cotangent), like(w_in), like(decay_rates), like(step_sizes), wide, full),
         scratch=[
             *(pltpu.VMEM(s.shape, F32) for s in (tall, tall, four, four)),
@@ -309,8 +310,7 @@
         (tall, tall, four_tall, four_tall, full, full, full, turned, turned),
         scratch=[pltpu.VMEM(tall.shape, F32)] * 2,
     )(px, ct, rt, ss, mixed, back)
-    from_rows = exchange(sent[cols - 1 :], "rows")
-    from_cols = exchange(sent[: cols - 1], "cols")
+    received = {key: partner(payload, *key) for key, payload in zip(order, sent)}
     split = rows == 4 and cols == 4 and channels == 128 and expand == 256
     if split:
         grads = (jax.ShapeDtypeStruct((2, 2, 2, 2, 48, 128), F32),)
@@ -320,9 +320,9 @@
             jax.ShapeDtypeStruct((channels, expand), F32),
         )
     outs = vmem_call(
-        functools.partial(join_body, (height, breadth), split, (cols, rows)),
+        functools.partial(join_body, (height, breadth), split, order),
         (jax.ShapeDtypeStruct((count, 2 * expand), BF16), *grads, jax.ShapeDtypeStruct((count, expand), BF16)),
-    )(rt, *from_cols, *from_rows, s_loc, g_loc, pre, suf, m_in, m_gate, gated, x_t, c_t)
+    )(rt, *received.values(), s_loc, g_loc, pre, suf, m_in, m_gate, gated, x_t, c_t)
     mix, grads = outs[0], outs[1:-1]
     grad_pixels = vmem_call(pixels_body, like(pixels), kept=False)(ct, mix, wi)
     if split:

time: 33.6 us -> 30.5 us (0.908)
  waiting for transfers between devices: 16 us -> 9.32 us
  starting transfers between devices: 9.6 us -> 13.3 us
    ppermute x10, waiting for transfers between devices: 16 us -> 9.32 us  [partner(): lax.ppermute(value, axis, [(i, i ^ bit) for i in range(lax.axis_size(axis...]
    ppermute x10, starting transfers between devices: 9.6 us -> 13.3 us  [partner(): lax.ppermute(value, axis, [(i, i ^ bit) for i in range(lax.axis_size(axis...]
  transfers between devices with their start and end apart: 10 -> 10, of which waited for: 6 -> 6; matrix products, arithmetic and copies ran while one was open for 0% -> 0% of each run, Pallas kernels for 9% -> 10%
where the time goes in v3:
time: 30.5 us; the launch traced here: 30.3 us
  starting transfers between devices  13.3 us (44%)
  waiting for transfers between devices  9.32 us (31%)
  Pallas kernels  6.94 us (23%)
  between operations  0.7 us (2%)
    ppermute x10, starting transfers between devices, partner(): lax.ppermute(value, axis, [(i, i ^ bit) for i in range(lax.axis_size(axis...  13.3 us
    ppermute x10, waiting for transfers between devices, partner(): lax.ppermute(value, axis, [(i, i ^ bit) for i in range(lax.axis_size(axis...  9.32 us
    pallas_call x5, Pallas kernels, call(): pl.pallas_call(body, out_shape=out_shape, in_specs=[pl.BlockSpec(memory_s...  6.94 us
  transfers between devices with their start and end apart: 10, of which 6 were waited for; matrix products, arithmetic and copies ran while one was open for 0% of the time, Pallas kernels for 10%

profile of v3, /device:TPU:0, one launch (start us, length us, event | category | flops | bytes accessed | tf_op | source)
XLA Modules:
  0.0 30.3 jit_solution(5136208424102960343)
XLA Ops:
  0.6 2.2 %shard_map.85 = (f32[16,640]{1,0:T(8,128)S(1)}, f32[16,640]{1,0:T(8,128)S(1)}, f32[16,640]{1,0:T(8,128)S(1)}, f32[16,640]{1,0:T(8,128)S(1)}, f32[16,640]{1,0:T(8...) custom-call(bf16[16,16,128]{2,1,0:T(8,128)(2,1)} %px_in.1, ...), custom_call_target="tpu_custom_call" | custom-call | tf_op jit(solution)/shard_map/pallas_call | solution.py:25
  2.9 5.1 %collective-permute-start = (f32[16,640]{1,0:T(8,128)S(1)}, f32[16,640]{1,0:T(8,128)S(1)}, u32[]{:S(2)}, u32[]{:S(2)}) collective-permute-start(f32[16,640]{1,0:T(8,128)S(1)} %get-tuple-element.31), channel_id=1, source_target_pairs={{0,12},{4,8},{8,4},{12,0},{1,13},{5,9},{9,5},{13,1},{2,14},{6,10},... | collective-permute-start | bytes 122888 | tf_op jit(solution)/shard_map/ppermute | solution.py:266
  8.0 0.0 collective-permute-start.1
  8.0 0.6 %collective-permute-start.2 = (f32[16,640]{1,0:T(8,128)S(1)}, f32[16,640]{1,0:T(8,128)S(1)}, u32[]{:S(2)}, u32[]{:S(2)}) collective-permute-start(f32[16,640]{1,0:T(8,128)S(1)} %get-tuple-element.33), channel_id=1, source_target_pairs={{0,4},{4,0},{8,12},{12,8},{1,5},{5,1},{9,13},{13,9},{2,6},{6,2},{1... | collective-permute-start | bytes 122888 | tf_op jit(solution)/shard_map/ppermute | solution.py:266
  8.6 0.4 %collective-permute-start.3 = (f32[16,640]{1,0:T(8,128)S(1)}, f32[16,640]{1,0:T(8,128)S(1)}, u32[]{:S(2)}, u32[]{:S(2)}) collective-permute-start(f32[16,640]{1,0:T(8,128)S(1)} %get-tuple-element.34), channel_id=1, source_target_pairs={{0,3},{1,2},{2,1},{3,0},{4,7},{5,6},{6,5},{7,4},{8,11},{9,10},{10,... | collective-permute-start | bytes 122888 | tf_op jit(solution)/shard_map/ppermute | solution.py:266
  9.0 1.3 %collective-permute-start.4 = (f32[16,640]{1,0:T(8,128)S(1)}, f32[16,640]{1,0:T(8,128)S(1)}, u32[]{:S(2)}, u32[]{:S(2)}) collective-permute-start(f32[16,640]{1,0:T(8,128)S(1)} %get-tuple-element.35), channel_id=1, source_target_pairs={{0,2},{1,3},{2,0},{3,1},{4,6},{5,7},{6,4},{7,5},{8,10},{9,11},{10,... | collective-permute-start | bytes 122888 | tf_op jit(solution)/shard_map/ppermute | solution.py:266
  10.3 0.0 collective-permute-done.refs_0_
  10.3 0.2 collective-permute-start.5
  10.5 2.2 %shard_map.86 = (f32[2,256,128]{2,1,0:T(8,128)S(1)}, f32[2,256,128]{2,1,0:T(8,128)S(1)}, f32[4,2,256,128]{3,2,1,0:T(8,128)S(1)}, f32[4,2,256,128]{3,2,1,0:T(8,12...) custom-call(bf16[16,16,128]{2,1,0:T(8,128)(2,1)S(1)} %get-tuple-elem, ...), custom_call_target="tpu_custom_call" | custom-call | tf_op jit(solution)/shard_map/pallas_call | solution.py:25
  12.7 0.2 collective-permute-done.1.refs_1_
  12.9 0.0 collective-permute-done.2.refs_2_
  12.9 0.0 collective-permute-done.3.refs_3_
  12.9 0.2 collective-permute-done.4.refs_4_
  13.1 1.0 %shard_map.87 = (bf16[256,512]{1,0:T(8,128)(2,1)S(1)}, f32[2,2,2,2,48,128]{5,4,3,2,1,0:T(8,128)S(1)}, bf16[256,256]{1,0:T(8,128)(2,1)}) custom-call(f32[4,256]{1,0:T(4,128)S(1)} %get-tuple-element.30.rt, f32[16,640]{1,0:T(8,128)S(1)} %collective-permute-done.refs_0_, f32[16,640]{1,0:T(8,128)S(1)} %collective-permute-done.1.refs_1_, ...), custom_call_target="tpu_custom_call" | custom-call | tf_op jit(solution)/shard_map/pallas_call | solution.py:25
  14.1 0.2 collective-permute-start.6
  14.4 1.3 %collective-permute-done.6 = f32[2,2,2,48,128]{4,3,2,1,0:T(8,128)S(1)} collective-permute-done((f32[2,2,2,48,128]{4,3,2,1,0:T(8,128)S(1)}, f32[2,2,2,48,128]{4,3,2,1,0:T(8,128)S(1)}, u32[]{:S(2)}, u32[]{:S(2)}) %collective-permute-start.6) | collective-permute-done | bytes 196640 | tf_op jit(solution)/shard_map/ppermute | solution.py:266
  15.7 1.5 %collective-permute-start.7 = (f32[2,2,48,128]{3,2,1,0:T(8,128)S(1)}, f32[2,2,48,128]{3,2,1,0:T(8,128)S(1)}, u32[]{:S(2)}, u32[]{:S(2)}) collective-permute-start(f32[2,2,48,128]{3,2,1,0:T(8,128)S(1)} %dynamic-slice_bitcast_fusion.1), channel_id=1, source_target_pairs={{0,2},{1,3},{2,0},{3,1},{4,6},{5,7},{6,4},{7,5},{8,10},{9,11},{10,... | collective-permute-start | bytes 294920 | tf_op jit(solution)/shard_map/ppermute | solution.py:266
  17.2 3.4 %collective-permute-done.7 = f32[2,2,48,128]{3,2,1,0:T(8,128)S(1)} collective-permute-done((f32[2,2,48,128]{3,2,1,0:T(8,128)S(1)}, f32[2,2,48,128]{3,2,1,0:T(8,128)S(1)}, u32[]{:S(2)}, u32[]{:S(2)}) %collective-permute-start.7) | collective-permute-done | bytes 98336 | tf_op jit(solution)/shard_map/ppermute | solution.py:266
  20.7 1.5 %collective-permute-start.8 = (f32[2,48,128]{2,1,0:T(8,128)S(1)}, f32[2,48,128]{2,1,0:T(8,128)S(1)}, u32[]{:S(2)}, u32[]{:S(2)}) collective-permute-start(f32[2,48,128]{2,1,0:T(8,128)S(1)} %dynamic-slice_bitcast_fusion.2), channel_id=1, source_target_pairs={{0,4},{4,0},{8,12},{12,8},{1,5},{5,1},{9,13},{13,9},{2,6},{6,2},{1... | collective-permute-start | bytes 147464 | tf_op jit(solution)/shard_map/ppermute | solution.py:266
  22.2 2.7 %collective-permute-done.8 = f32[2,48,128]{2,1,0:T(8,128)S(1)} collective-permute-done((f32[2,48,128]{2,1,0:T(8,128)S(1)}, f32[2,48,128]{2,1,0:T(8,128)S(1)}, u32[]{:S(2)}, u32[]{:S(2)}) %collective-permute-start.8) | collective-permute-done | bytes 49184 | tf_op jit(solution)/shard_map/ppermute | solution.py:266
  24.8 2.4 %collective-permute-start.9 = (f32[48,128]{1,0:T(8,128)S(1)}, f32[48,128]{1,0:T(8,128)S(1)}, u32[]{:S(2)}, u32[]{:S(2)}) collective-permute-start(f32[48,128]{1,0:T(8,128)S(1)} %get-tuple-element.55), channel_id=1, source_target_pairs={{0,8},{4,12},{8,0},{12,4},{1,9},{5,13},{9,1},{13,5},{2,10},{6,14},... | collective-permute-start | bytes 73736 | tf_op jit(solution)/shard_map/ppermute | solution.py:266
  27.2 0.9 %shard_map.88 = bf16[16,16,128]{2,1,0:T(8,128)(2,1)} custom-call(bf16[16,16,128]{2,1,0:T(8,128)(2,1)S(1)} %get-tuple-element.29.ct, bf16[256,512]{1,0:T(8,128)(2,1)S(1)} %get-tuple-element.50.mix, bf16[128,512]{1,0:T(8,128)(2,1)S(1)} %get-tuple-element.51.wi), custom_call_target="tpu_custom_call" | custom-call | tf_op jit(solution)/shard_map/pallas_call | solution.py:25
  28.1 1.5 %collective-permute-done.9.other = f32[48,128]{1,0:T(8,128)S(1)} collective-permute-done((f32[48,128]{1,0:T(8,128)S(1)}, f32[48,128]{1,0:T(8,128)S(1)}, u32[]{:S(2)}, u32[]{:S(2)}) %collective-permute-start.9) | collective-permute-done | bytes 24608 | tf_op jit(solution)/shard_map/ppermute | solution.py:266
  29.6 0.7 %shard_map.89 = (f32[32,128]{1,0:T(8,128)}, f32[32,64]{1,0:T(8,128)}) custom-call(f32[48,128]{1,0:T(8,128)S(1)} %get-tuple-element.56.mine, f32[48,128]{1,0:T(8,128)S(1)} %collective-permute-done.9.other), custom_call_target="tpu_custom_call" | custom-call | tf_op jit(solution)/shard_map/pallas_call | solution.py:25
  (8 shorter events, 0.1 us)
Async XLA Ops:
  2.9 7.4 %collective-permute-start = (f32[16,640]{1,0:T(8,128)S(1)}, f32[16,640]{1,0:T(8,128)S(1)}, u32[]{:S(2)}, u32[]{:S(2)}) collective-permute-start(f32[16,640]{1,0:T(8,128)S(1)} %get-tuple-element.31), channel_id=1, source_target_pairs={{0,12},{4,8},{8,4},{12,0},{1,13},{5,9},{9,5},{13,1},{2,14},{6,10},... | collective-permute-start | bytes 122888 | tf_op jit(solution)/shard_map/ppermute | solution.py:266
  8.0 4.9 %collective-permute-start.1 = (f32[16,640]{1,0:T(8,128)S(1)}, f32[16,640]{1,0:T(8,128)S(1)}, u32[]{:S(2)}, u32[]{:S(2)}) collective-permute-start(f32[16,640]{1,0:T(8,128)S(1)} %get-tuple-element.32), channel_id=1, source_target_pairs={{0,8},{4,12},{8,0},{12,4},{1,9},{5,13},{9,1},{13,5},{2,10},{6,14},... | collective-permute-start | bytes 122888 | tf_op jit(solution)/shard_map/ppermute | solution.py:266
  8.0 4.9 %collective-permute-start.2 = (f32[16,640]{1,0:T(8,128)S(1)}, f32[16,640]{1,0:T(8,128)S(1)}, u32[]{:S(2)}, u32[]{:S(2)}) collective-permute-start(f32[16,640]{1,0:T(8,128)S(1)} %get-tuple-element.33), channel_id=1, source_target_pairs={{0,4},{4,0},{8,12},{12,8},{1,5},{5,1},{9,13},{13,9},{2,6},{6,2},{1... | collective-permute-start | bytes 122888 | tf_op jit(solution)/shard_map/ppermute | solution.py:266
  8.6 4.3 %collective-permute-start.3 = (f32[16,640]{1,0:T(8,128)S(1)}, f32[16,640]{1,0:T(8,128)S(1)}, u32[]{:S(2)}, u32[]{:S(2)}) collective-permute-start(f32[16,640]{1,0:T(8,128)S(1)} %get-tuple-element.34), channel_id=1, source_target_pairs={{0,3},{1,2},{2,1},{3,0},{4,7},{5,6},{6,5},{7,4},{8,11},{9,10},{10,... | collective-permute-start | bytes 122888 | tf_op jit(solution)/shard_map/ppermute | solution.py:266
  9.0 4.1 %collective-permute-start.4 = (f32[16,640]{1,0:T(8,128)S(1)}, f32[16,640]{1,0:T(8,128)S(1)}, u32[]{:S(2)}, u32[]{:S(2)}) collective-permute-start(f32[16,640]{1,0:T(8,128)S(1)} %get-tuple-element.35), channel_id=1, source_target_pairs={{0,2},{1,3},{2,0},{3,1},{4,6},{5,7},{6,4},{7,5},{8,10},{9,11},{10,... | collective-permute-start | bytes 122888 | tf_op jit(solution)/shard_map/ppermute | solution.py:266
  10.3 2.8 %collective-permute-start.5 = (f32[16,640]{1,0:T(8,128)S(1)}, f32[16,640]{1,0:T(8,128)S(1)}, u32[]{:S(2)}, u32[]{:S(2)}) collective-permute-start(f32[16,640]{1,0:T(8,128)S(1)} %get-tuple-element.36), channel_id=1, source_target_pairs={{0,1},{1,0},{2,3},{3,2},{4,5},{5,4},{6,7},{7,6},{8,9},{9,8},{10,11... | collective-permute-start | bytes 122888 | tf_op jit(solution)/shard_map/ppermute | solution.py:266
  14.1 1.5 %collective-permute-start.6 = (f32[2,2,2,48,128]{4,3,2,1,0:T(8,128)S(1)}, f32[2,2,2,48,128]{4,3,2,1,0:T(8,128)S(1)}, u32[]{:S(2)}, u32[]{:S(2)}) collective-permute-start(f32[2,2,2,48,128]{4,3,2,1,0:T(8,128)S(1)} %dynamic-slice_bitcast_fusion), channel_id=1, source_target_pairs={{0,1},{1,0},{2,3},{3,2},{4,5},{5,4},{6,7},{7,6},{8,9},{9,8},{10,11... | collective-permute-start | bytes 589832 | tf_op jit(solution)/shard_map/ppermute | solution.py:266
  15.7 4.9 %collective-permute-start.7 = (f32[2,2,48,128]{3,2,1,0:T(8,128)S(1)}, f32[2,2,48,128]{3,2,1,0:T(8,128)S(1)}, u32[]{:S(2)}, u32[]{:S(2)}) collective-permute-start(f32[2,2,48,128]{3,2,1,0:T(8,128)S(1)} %dynamic-slice_bitcast_fusion.1), channel_id=1, source_target_pairs={{0,2},{1,3},{2,0},{3,1},{4,6},{5,7},{6,4},{7,5},{8,10},{9,11},{10,... | collective-permute-start | bytes 294920 | tf_op jit(solution)/shard_map/ppermute | solution.py:266
  20.7 4.2 %collective-permute-start.8 = (f32[2,48,128]{2,1,0:T(8,128)S(1)}, f32[2,48,128]{2,1,0:T(8,128)S(1)}, u32[]{:S(2)}, u32[]{:S(2)}) collective-permute-start(f32[2,48,128]{2,1,0:T(8,128)S(1)} %dynamic-slice_bitcast_fusion.2), channel_id=1, source_target_pairs={{0,4},{4,0},{8,12},{12,8},{1,5},{5,1},{9,13},{13,9},{2,6},{6,2},{1... | collective-permute-start | bytes 147464 | tf_op jit(solution)/shard_map/ppermute | solution.py:266
  24.8 4.8 %collective-permute-start.9 = (f32[48,128]{1,0:T(8,128)S(1)}, f32[48,128]{1,0:T(8,128)S(1)}, u32[]{:S(2)}, u32[]{:S(2)}) collective-permute-start(f32[48,128]{1,0:T(8,128)S(1)} %get-tuple-element.55), channel_id=1, source_target_pairs={{0,8},{4,12},{8,0},{12,4},{1,9},{5,13},{9,1},{13,5},{2,10},{6,14},... | collective-permute-start | bytes 73736 | tf_op jit(solution)/shard_map/ppermute | solution.py:266

commit v4 on v3

--- a/solution.py
+++ b/solution.py
@@ -45,7 +45,7 @@
 
 
 def sigmoid(value):
-    return 1.0 / (1.0 + jnp.exp(-value))
+    return 0.5 * jnp.tanh(0.5 * value) + 0.5
 
 
 def decay_pair(rate, step):
@@ -56,7 +56,7 @@
 
 def edges_body(order, px_in, ct_in, wi_in, wo_in, rt_in, ss_in, *refs):
     sent = refs[: len(order)]
-    px, ct, wi, rt, ss, mixed, back, src, seed, dec, wgt, wo, ways, sems = refs[len(order) :]
+    px, ct, rt, mixed, back, dec, wgt, wi, wo, ss, src, seed, ways, sems = refs[len(order) :]
     pairs = ((px_in, px), (wi_in, wi), (ct_in, ct), (wo_in, wo), (ss_in, ss), (rt_in, rt))
     copies = [pltpu.make_async_copy(a, b, sems.at[k]) for k, (a, b) in enumerate(pairs)]
     for copy in copies:
@@ -68,13 +68,13 @@
     copies[1].wait()
     both = jnp.dot(px[...].reshape(count, channels), wi[...], preferred_element_type=F32)
     mixed[...] = both
+    inner, gate = both[:, :expand], both[:, expand:]
+    put(src, slice(None), inner * sigmoid(inner))
     copies[2].wait()
     copies[3].wait()
     cot = ct[...].reshape(count, channels)
     bg = lax.dot_general(cot, wo[...], contract_cols, preferred_element_type=F32)
     back[...] = bg
-    inner, gate = both[:, :expand], both[:, expand:]
-    put(src, slice(None), inner * sigmoid(inner))
     put(seed, slice(None), bg * (gate * sigmoid(gate)))
     copies[4].wait()
     copies[5].wait()
@@ -123,18 +123,17 @@
                 out[...] = payload[((mine ^ k) < mine).astype(jnp.int32)]
 
 
-def local_body(px, ct, rt, ss, mixed, back, s_loc, g_loc, pre, suf, m_in, m_gate, gated, x_t, c_t, src, seed):
+def local_body(px, ct, mixed, back, dec, wgt, s_loc, g_loc, pre, suf, m_in, m_gate, gated, x_t, c_t, src, seed):
     height, breadth, channels = px.shape
     expand = src.shape[0] * 128
     count = height * breadth
     inner, gate = mixed[:, :expand], mixed[:, expand:]
-    s_in = sigmoid(inner)
-    m_in[...] = s_in * (1.0 + inner * (1.0 - s_in))
-    s_gate = sigmoid(gate)
+    s_in, s_gate = sigmoid(inner), sigmoid(gate)
     gate_silu = gate * s_gate
-    gated[...] = gate_silu
     put(src, slice(None), inner * s_in)
     put(seed, slice(None), back[...] * gate_silu)
+    m_in[...] = s_in * (1.0 + inner * (1.0 - s_in))
+    gated[...] = gate_silu
     m_gate[...] = back[...] * (s_gate * (1.0 + gate * (1.0 - s_gate)))
     x_t[...] = jnp.transpose(px[...].reshape(count, channels).astype(F32)).astype(BF16)
     c_t[...] = jnp.transpose(ct[...].reshape(count, channels).astype(F32)).astype(BF16)
@@ -148,16 +147,14 @@
                 return pl.ds(i, lines, stride=length)
             return pl.ds(i * lines, lines)
 
-        steps = {d: ss[d] if axis == 0 else jnp.transpose(ss[d]) for d in (one, two)}
-
         def go(order, a, b, first):
             state = jnp.zeros((lines, expand), F32)
             carried = jnp.zeros((lines, expand), F32)
             upto = jnp.ones((lines, expand), F32)
             after = jnp.ones((lines, expand), F32)
             for i in order:
-                da, wa = decay_pair(rt[a : a + 1, :], steps[a][:, i : i + 1])
-                db, wb = decay_pair(rt[b : b + 1, :], steps[b][:, i : i + 1])
+                rows = slice(i * lines, (i + 1) * lines)
+                da, wa, db, wb = dec[a, rows, :], wgt[a, rows, :], dec[b, rows, :], wgt[b, rows, :]
                 state = da * state + wa * get(src, where(i))
                 upto = upto * da
                 adjoint = get(seed, where(i)) + carried
@@ -244,8 +241,8 @@
             high = jnp.where(lane < 64, pltpu.roll(top, 64, 1), bottom)
             for k, piece in ((0, low), (1, high)):
                 r = 2 * t + k
-                packed[c & 1, c >> 1, k, t, 0:32, :] = grad_in[32 * r : 32 * r + 32, 128 * c : 128 * c + 128]
-                packed[c & 1, c >> 1, k, t, 32:48, :] = piece
+                packed[c, r, 0:32, :] = grad_in[32 * r : 32 * r + 32, 128 * c : 128 * c + 128]
+                packed[c, r, 32:48, :] = piece
 
 
 def pixels_body(ct, mix, wi, out):
@@ -255,8 +252,8 @@
     out[...] = (cot + grad).astype(BF16).reshape(height, breadth, channels)
 
 
-def final_body(mine, other, g_in, g_out):
-    total = mine[...] + other[...]
+def final_body(mine, one, two, three, g_in, g_out):
+    total = (mine[...] + one[...]) + (two[...] + three[...])
     g_in[...] = total[0:32, :]
     g_out[0:16, :] = total[32:48, 0:64]
     g_out[16:32, :] = total[32:48, 64:128]
@@ -270,10 +267,15 @@
     return [("rows", k) for k in reversed(range(1, rows))] + [("cols", k) for k in reversed(range(1, cols))]
 
 
-def halve(value, axis, bit):
-    mine = (lax.axis_index(axis) & bit) // bit
+def shifted(value, axis, k):
+    count = lax.axis_size(axis)
+    return lax.ppermute(value, axis, [(i, (i + k) % count) for i in range(count)])
+
+
+def spread(value, axis, order):
+    count, mine = lax.axis_size(axis), lax.axis_index(axis)
     pick = lambda i: lax.dynamic_index_in_dim(value, i, 0, keepdims=False)
-    return pick(mine), partner(pick(1 - mine), axis, bit)
+    return [pick(mine)] + [shifted(pick(lax.rem(mine + k, count)), axis, k) for k in order]
 
 
 def per_device(pixels, cotangent, w_in, w_out, decay_rates, step_sizes):
@@ -293,27 +295,30 @@
     pays = tuple(pay_cols if axis == "cols" else pay_rows for axis, _ in order)
     outs = vmem_call(
         functools.partial(edges_body, order),
-        (*pays, like(pixels), like(cotangent), like(w_in), like(decay_rates), like(step_sizes), wide, full),
+        (*pays, like(pixels), like(cotangent), like(decay_rates), wide, full, four, four),
         scratch=[
-            *(pltpu.VMEM(s.shape, F32) for s in (tall, tall, four, four)),
+            pltpu.VMEM(w_in.shape, BF16),
             pltpu.VMEM(w_out.shape, BF16),
+            pltpu.VMEM(step_sizes.shape, F32),
+            pltpu.VMEM(tall.shape, F32),
+            pltpu.VMEM(tall.shape, F32),
             pltpu.VMEM((2, 2, *pay_cols.shape), F32),
             pltpu.SemaphoreType.DMA((6,)),
         ],
         given=pltpu.HBM,
     )(pixels, cotangent, w_in, w_out, decay_rates, step_sizes)
     sent = outs[: len(pays)]
-    px, ct, wi, rt, ss, mixed, back = outs[len(pays) :]
+    px, ct, rt, mixed, back, dec, wgt = outs[len(pays) :]
     turned = jax.ShapeDtypeStruct((channels, count), BF16)
     s_loc, g_loc, pre, suf, m_in, m_gate, gated, x_t, c_t = vmem_call(
         local_body,
         (tall, tall, four_tall, four_tall, full, full, full, turned, turned),
         scratch=[pltpu.VMEM(tall.shape, F32)] * 2,
-    )(px, ct, rt, ss, mixed, back)
+    )(px, ct, mixed, back, dec, wgt)
     received = {key: partner(payload, *key) for key, payload in zip(order, sent)}
     split = rows == 4 and cols == 4 and channels == 128 and expand == 256
     if split:
-        grads = (jax.ShapeDtypeStruct((2, 2, 2, 2, 48, 128), F32),)
+        grads = (jax.ShapeDtypeStruct((4, 4, 48, 128), F32),)
     else:
         grads = (
             jax.ShapeDtypeStruct((channels, 2 * expand), F32),
@@ -324,16 +329,14 @@
         (jax.ShapeDtypeStruct((count, 2 * expand), BF16), *grads, jax.ShapeDtypeStruct((count, expand), BF16)),
     )(rt, *received.values(), s_loc, g_loc, pre, suf, m_in, m_gate, gated, x_t, c_t)
     mix, grads = outs[0], outs[1:-1]
-    grad_pixels = vmem_call(pixels_body, like(pixels), kept=False)(ct, mix, wi)
+    grad_pixels = vmem_call(pixels_body, like(pixels), kept=False)(ct, mix, w_in)
     if split:
-        value = grads[0]
-        for axis, bit in (("cols", 1), ("cols", 2), ("rows", 1)):
-            kept, got = halve(value, axis, bit)
-            value = kept + got
-        kept, got = halve(value, "rows", 2)
+        parts = spread(grads[0], "cols", (1, 2, 3))
+        value = (parts[0] + parts[1]) + (parts[2] + parts[3])
+        parts = spread(value, "rows", (1, 2, 3))
         grad_in, grad_out = vmem_call(
             final_body, (jax.ShapeDtypeStruct((32, 128), F32), jax.ShapeDtypeStruct((32, 64), F32)), kept=False
-        )(kept, got)
+        )(*parts)
         return grad_pixels, grad_in, jnp.transpose(grad_out)
     full_in, full_out = grads[0], jnp.transpose(grads[1])
     full_in = lax.psum_scatter(full_in, "cols", scatter_dimension=1, tiled=True)

time: 30.5 us -> 29.4 us (0.964)
  waiting for transfers between devices: 9.32 us -> 6.08 us
  starting transfers between devices: 13.3 us -> 15.7 us
    ppermute x10 -> x6, waiting for transfers between devices: 9.32 us -> 0.77 us  [partner(): lax.ppermute(value, axis, [(i, i ^ bit) for i in range(lax.axis_size(axis...]
    ppermute x0 -> x6, starting transfers between devices: none -> 8.09 us  [shifted(): lax.ppermute(value, axis, [(i, (i + k) % count) for i in range(count)])]
    ppermute x10 -> x6, starting transfers between devices: 13.3 us -> 7.62 us  [partner(): lax.ppermute(value, axis, [(i, i ^ bit) for i in range(lax.axis_size(axis...]
    ppermute x0 -> x6, waiting for transfers between devices: none -> 5.31 us  [shifted(): lax.ppermute(value, axis, [(i, (i + k) % count) for i in range(count)])]
  transfers between devices with their start and end apart: 10 -> 12, of which waited for: 6 -> 7; matrix products, arithmetic and copies ran while one was open for 0% -> 0% of each run, Pallas kernels for 10% -> 9%
where the time goes in v4:
time: 29.4 us; the launch traced here: 29.2 us
  starting transfers between devices  15.7 us (53%)
  Pallas kernels  6.69 us (23%)
  waiting for transfers between devices  6.08 us (21%)
  between operations  0.68 us (2%)
    ppermute x6, starting transfers between devices, shifted(): lax.ppermute(value, axis, [(i, (i + k) % count) for i in range(count)])  8.09 us
    ppermute x6, starting transfers between devices, partner(): lax.ppermute(value, axis, [(i, i ^ bit) for i in range(lax.axis_size(axis...  7.62 us
    pallas_call x5, Pallas kernels, call(): pl.pallas_call(body, out_shape=out_shape, in_specs=[pl.BlockSpec(memory_s...  6.69 us
    ppermute x6, waiting for transfers between devices, shifted(): lax.ppermute(value, axis, [(i, (i + k) % count) for i in range(count)])  5.31 us
    ppermute x6, waiting for transfers between devices, partner(): lax.ppermute(value, axis, [(i, i ^ bit) for i in range(lax.axis_size(axis...  0.77 us
  transfers between devices with their start and end apart: 12, of which 7 were waited for; matrix products, arithmetic and copies ran while one was open for 0% of the time, Pallas kernels for 9%

profile of v4, /device:TPU:0, one launch (start us, length us, event | category | flops | bytes accessed | tf_op | source)
XLA Modules:
  0.0 29.2 jit_solution(4491333593922990467)
XLA Ops:
  0.6 2.2 %shard_map.85 = (f32[16,640]{1,0:T(8,128)S(1)}, f32[16,640]{1,0:T(8,128)S(1)}, f32[16,640]{1,0:T(8,128)S(1)}, f32[16,640]{1,0:T(8,128)S(1)}, f32[16,640]{1,0:T(8...) custom-call(bf16[16,16,128]{2,1,0:T(8,128)(2,1)} %px_in.1, ...), custom_call_target="tpu_custom_call" | custom-call | tf_op jit(solution)/shard_map/pallas_call | solution.py:25
  2.9 5.1 %collective-permute-start = (f32[16,640]{1,0:T(8,128)S(1)}, f32[16,640]{1,0:T(8,128)S(1)}, u32[]{:S(2)}, u32[]{:S(2)}) collective-permute-start(f32[16,640]{1,0:T(8,128)S(1)} %get-tuple-element.31), channel_id=1, source_target_pairs={{0,12},{4,8},{8,4},{12,0},{1,13},{5,9},{9,5},{13,1},{2,14},{6,10},... | collective-permute-start | bytes 122888 | tf_op jit(solution)/shard_map/ppermute | solution.py:263
  8.0 0.0 collective-permute-start.1
  8.0 0.6 %collective-permute-start.2 = (f32[16,640]{1,0:T(8,128)S(1)}, f32[16,640]{1,0:T(8,128)S(1)}, u32[]{:S(2)}, u32[]{:S(2)}) collective-permute-start(f32[16,640]{1,0:T(8,128)S(1)} %get-tuple-element.33), channel_id=1, source_target_pairs={{0,4},{4,0},{8,12},{12,8},{1,5},{5,1},{9,13},{13,9},{2,6},{6,2},{1... | collective-permute-start | bytes 122888 | tf_op jit(solution)/shard_map/ppermute | solution.py:263
  8.6 0.4 %collective-permute-start.3 = (f32[16,640]{1,0:T(8,128)S(1)}, f32[16,640]{1,0:T(8,128)S(1)}, u32[]{:S(2)}, u32[]{:S(2)}) collective-permute-start(f32[16,640]{1,0:T(8,128)S(1)} %get-tuple-element.34), channel_id=1, source_target_pairs={{0,3},{1,2},{2,1},{3,0},{4,7},{5,6},{6,5},{7,4},{8,11},{9,10},{10,... | collective-permute-start | bytes 122888 | tf_op jit(solution)/shard_map/ppermute | solution.py:263
  9.0 1.3 %collective-permute-start.4 = (f32[16,640]{1,0:T(8,128)S(1)}, f32[16,640]{1,0:T(8,128)S(1)}, u32[]{:S(2)}, u32[]{:S(2)}) collective-permute-start(f32[16,640]{1,0:T(8,128)S(1)} %get-tuple-element.35), channel_id=1, source_target_pairs={{0,2},{1,3},{2,0},{3,1},{4,6},{5,7},{6,4},{7,5},{8,10},{9,11},{10,... | collective-permute-start | bytes 122888 | tf_op jit(solution)/shard_map/ppermute | solution.py:263
  10.3 0.2 collective-permute-start.5
  10.5 1.8 %shard_map.86 = (f32[2,256,128]{2,1,0:T(8,128)S(1)}, f32[2,256,128]{2,1,0:T(8,128)S(1)}, f32[4,2,256,128]{3,2,1,0:T(8,128)S(1)}, f32[4,2,256,128]{3,2,1,0:T(8,12...) custom-call(bf16[16,16,128]{2,1,0:T(8,128)(2,1)S(1)} %get-tuple-elem, ...), custom_call_target="tpu_custom_call" | custom-call | tf_op jit(solution)/shard_map/pallas_call | solution.py:25
  12.4 0.5 %collective-permute-done.1.refs_1_ = f32[16,640]{1,0:T(8,128)S(1)} collective-permute-done((f32[16,640]{1,0:T(8,128)S(1)}, f32[16,640]{1,0:T(8,128)S(1)}, u32[]{:S(2)}, u32[]{:S(2)}) %collective-permute-start.1) | collective-permute-done | bytes 40992 | tf_op jit(solution)/shard_map/ppermute | solution.py:263
  12.9 0.2 collective-permute-done.4.refs_4_
  13.1 1.1 %shard_map.87 = (bf16[256,512]{1,0:T(8,128)(2,1)S(1)}, f32[4,4,48,128]{3,2,1,0:T(8,128)S(1)}, bf16[256,256]{1,0:T(8,128)(2,1)}) custom-call(f32[4,256]{1,0:T(4,128)S(1)} %get-tuple-element.30.rt, f32[16,640]{1,0:T(8,128)S(1)} %collective-permute-done.refs_0_, f32[16,640]{1,0:T(8,128)S(1)} %collective-permute-done.1.refs_1_, ...), custom_call_target="tpu_custom_call" | custom-call | tf_op jit(solution)/shard_map/pallas_call | solution.py:25
  14.2 0.2 collective-permute-start.6
  14.4 1.4 %collective-permute-start.7 = (f32[4,48,128]{2,1,0:T(8,128)S(1)}, f32[4,48,128]{2,1,0:T(8,128)S(1)}, u32[]{:S(2)}, u32[]{:S(2)}) collective-permute-start(f32[4,48,128]{2,1,0:T(8,128)S(1)} %get-tuple-element.56), channel_id=1, source_target_pairs={{0,2},{1,3},{2,0},{3,1},{4,6},{5,7},{6,4},{7,5},{8,10},{9,11},{10,... | collective-permute-start | bytes 294920 | tf_op jit(solution)/shard_map/ppermute | solution.py:272
  15.8 1.4 %collective-permute-start.8 = (f32[4,48,128]{2,1,0:T(8,128)S(1)}, f32[4,48,128]{2,1,0:T(8,128)S(1)}, u32[]{:S(2)}, u32[]{:S(2)}) collective-permute-start(f32[4,48,128]{2,1,0:T(8,128)S(1)} %get-tuple-element.55), channel_id=1, source_target_pairs={{0,3},{1,0},{2,1},{3,2},{4,7},{5,4},{6,5},{7,6},{8,11},{9,8},{10,9... | collective-permute-start | bytes 294920 | tf_op jit(solution)/shard_map/ppermute | solution.py:272
  17.2 1.5 %collective-permute-done.6 = f32[4,48,128]{2,1,0:T(8,128)S(1)} collective-permute-done((f32[4,48,128]{2,1,0:T(8,128)S(1)}, f32[4,48,128]{2,1,0:T(8,128)S(1)}, u32[]{:S(2)}, u32[]{:S(2)}) %collective-permute-start.6) | collective-permute-done | bytes 98336 | tf_op jit(solution)/shard_map/ppermute | solution.py:272
  18.7 1.3 %collective-permute-done.7 = f32[4,48,128]{2,1,0:T(8,128)S(1)} collective-permute-done((f32[4,48,128]{2,1,0:T(8,128)S(1)}, f32[4,48,128]{2,1,0:T(8,128)S(1)}, u32[]{:S(2)}, u32[]{:S(2)}) %collective-permute-start.7) | collective-permute-done | bytes 98336 | tf_op jit(solution)/shard_map/ppermute | solution.py:272
  20.0 0.4 %collective-permute-done.8 = f32[4,48,128]{2,1,0:T(8,128)S(1)} collective-permute-done((f32[4,48,128]{2,1,0:T(8,128)S(1)}, f32[4,48,128]{2,1,0:T(8,128)S(1)}, u32[]{:S(2)}, u32[]{:S(2)}) %collective-permute-start.8) | collective-permute-done | bytes 98336 | tf_op jit(solution)/shard_map/ppermute | solution.py:272
  20.5 1.3 %collective-permute-start.9 = (f32[48,128]{1,0:T(8,128)S(1)}, f32[48,128]{1,0:T(8,128)S(1)}, u32[]{:S(2)}, u32[]{:S(2)}) collective-permute-start(f32[48,128]{1,0:T(8,128)S(1)} %get-tuple-element.60), channel_id=1, source_target_pairs={{0,4},{4,8},{8,12},{12,0},{1,5},{5,9},{9,13},{13,1},{2,6},{6,10},{... | collective-permute-start | bytes 73736 | tf_op jit(solution)/shard_map/ppermute | solution.py:272
  21.8 2.9 %collective-permute-start.10 = (f32[48,128]{1,0:T(8,128)S(1)}, f32[48,128]{1,0:T(8,128)S(1)}, u32[]{:S(2)}, u32[]{:S(2)}) collective-permute-start(f32[48,128]{1,0:T(8,128)S(1)} %get-tuple-element.59), channel_id=1, source_target_pairs={{0,8},{4,12},{8,0},{12,4},{1,9},{5,13},{9,1},{13,5},{2,10},{6,14},... | collective-permute-start | bytes 73736 | tf_op jit(solution)/shard_map/ppermute | solution.py:272
  24.7 0.9 %collective-permute-start.11 = (f32[48,128]{1,0:T(8,128)S(1)}, f32[48,128]{1,0:T(8,128)S(1)}, u32[]{:S(2)}, u32[]{:S(2)}) collective-permute-start(f32[48,128]{1,0:T(8,128)S(1)} %get-tuple-element.58), channel_id=1, source_target_pairs={{0,12},{4,0},{8,4},{12,8},{1,13},{5,1},{9,5},{13,9},{2,14},{6,2},{... | collective-permute-start | bytes 73736 | tf_op jit(solution)/shard_map/ppermute | solution.py:272
  25.6 0.9 %shard_map.88 = bf16[16,16,128]{2,1,0:T(8,128)(2,1)} custom-call(bf16[16,16,128]{2,1,0:T(8,128)(2,1)S(1)} %get-tuple-element.29.ct, bf16[256,512]{1,0:T(8,128)(2,1)S(1)} %get-tuple-element.51.mix, bf16[128,512]{1,0:T(8,128)(2,1)S(1)} %copy-done), custom_call_target="tpu_custom_call" | custom-call | tf_op jit(solution)/shard_map/pallas_call | solution.py:25
  26.5 0.5 %collective-permute-done.10.two = f32[48,128]{1,0:T(8,128)S(1)} collective-permute-done((f32[48,128]{1,0:T(8,128)S(1)}, f32[48,128]{1,0:T(8,128)S(1)}, u32[]{:S(2)}, u32[]{:S(2)}) %collective-permute-start.10) | collective-permute-done | bytes 24608 | tf_op jit(solution)/shard_map/ppermute | solution.py:272
  27.0 1.6 %collective-permute-done.11.three = f32[48,128]{1,0:T(8,128)S(1)} collective-permute-done((f32[48,128]{1,0:T(8,128)S(1)}, f32[48,128]{1,0:T(8,128)S(1)}, u32[]{:S(2)}, u32[]{:S(2)}) %collective-permute-start.11) | collective-permute-done | bytes 24608 | tf_op jit(solution)/shard_map/ppermute | solution.py:272
  28.5 0.7 %shard_map.89 = (f32[32,128]{1,0:T(8,128)}, f32[32,64]{1,0:T(8,128)}) custom-call(f32[48,128]{1,0:T(8,128)S(1)} %get-tuple-element.61.mine, f32[48,128]{1,0:T(8,128)S(1)} %collective-permute-done.9.one, f32[48,128]{1,0:T(8,128)S(1)} %collective-permute-done.10.two, f32[48,128]{1,0:T(8,128)S(1)} %collective-permute-done.11.three), custom_call_target="tpu_custom_call" | custom-call | tf_op jit(solution)/shard_map/pallas_call | solution.py:25
  (10 shorter events, 0.1 us)
Async XLA Ops:
  2.9 7.4 %collective-permute-start = (f32[16,640]{1,0:T(8,128)S(1)}, f32[16,640]{1,0:T(8,128)S(1)}, u32[]{:S(2)}, u32[]{:S(2)}) collective-permute-start(f32[16,640]{1,0:T(8,128)S(1)} %get-tuple-element.31), channel_id=1, source_target_pairs={{0,12},{4,8},{8,4},{12,0},{1,13},{5,9},{9,5},{13,1},{2,14},{6,10},... | collective-permute-start | bytes 122888 | tf_op jit(solution)/shard_map/ppermute | solution.py:263
  8.0 4.9 %collective-permute-start.1 = (f32[16,640]{1,0:T(8,128)S(1)}, f32[16,640]{1,0:T(8,128)S(1)}, u32[]{:S(2)}, u32[]{:S(2)}) collective-permute-start(f32[16,640]{1,0:T(8,128)S(1)} %get-tuple-element.32), channel_id=1, source_target_pairs={{0,8},{4,12},{8,0},{12,4},{1,9},{5,13},{9,1},{13,5},{2,10},{6,14},... | collective-permute-start | bytes 122888 | tf_op jit(solution)/shard_map/ppermute | solution.py:263
  8.0 4.9 %collective-permute-start.2 = (f32[16,640]{1,0:T(8,128)S(1)}, f32[16,640]{1,0:T(8,128)S(1)}, u32[]{:S(2)}, u32[]{:S(2)}) collective-permute-start(f32[16,640]{1,0:T(8,128)S(1)} %get-tuple-element.33), channel_id=1, source_target_pairs={{0,4},{4,0},{8,12},{12,8},{1,5},{5,1},{9,13},{13,9},{2,6},{6,2},{1... | collective-permute-start | bytes 122888 | tf_op jit(solution)/shard_map/ppermute | solution.py:263
  8.6 4.3 %collective-permute-start.3 = (f32[16,640]{1,0:T(8,128)S(1)}, f32[16,640]{1,0:T(8,128)S(1)}, u32[]{:S(2)}, u32[]{:S(2)}) collective-permute-start(f32[16,640]{1,0:T(8,128)S(1)} %get-tuple-element.34), channel_id=1, source_target_pairs={{0,3},{1,2},{2,1},{3,0},{4,7},{5,6},{6,5},{7,4},{8,11},{9,10},{10,... | collective-permute-start | bytes 122888 | tf_op jit(solution)/shard_map/ppermute | solution.py:263
  9.0 4.1 %collective-permute-start.4 = (f32[16,640]{1,0:T(8,128)S(1)}, f32[16,640]{1,0:T(8,128)S(1)}, u32[]{:S(2)}, u32[]{:S(2)}) collective-permute-start(f32[16,640]{1,0:T(8,128)S(1)} %get-tuple-element.35), channel_id=1, source_target_pairs={{0,2},{1,3},{2,0},{3,1},{4,6},{5,7},{6,4},{7,5},{8,10},{9,11},{10,... | collective-permute-start | bytes 122888 | tf_op jit(solution)/shard_map/ppermute | solution.py:263
  10.3 2.8 %collective-permute-start.5 = (f32[16,640]{1,0:T(8,128)S(1)}, f32[16,640]{1,0:T(8,128)S(1)}, u32[]{:S(2)}, u32[]{:S(2)}) collective-permute-start(f32[16,640]{1,0:T(8,128)S(1)} %get-tuple-element.36), channel_id=1, source_target_pairs={{0,1},{1,0},{2,3},{3,2},{4,5},{5,4},{6,7},{7,6},{8,9},{9,8},{10,11... | collective-permute-start | bytes 122888 | tf_op jit(solution)/shard_map/ppermute | solution.py:263
  14.2 4.5 %collective-permute-start.6 = (f32[4,48,128]{2,1,0:T(8,128)S(1)}, f32[4,48,128]{2,1,0:T(8,128)S(1)}, u32[]{:S(2)}, u32[]{:S(2)}) collective-permute-start(f32[4,48,128]{2,1,0:T(8,128)S(1)} %get-tuple-element.57), channel_id=1, source_target_pairs={{0,1},{1,2},{2,3},{3,0},{4,5},{5,6},{6,7},{7,4},{8,9},{9,10},{10,1... | collective-permute-start | bytes 294920 | tf_op jit(solution)/shard_map/ppermute | solution.py:272
  14.4 5.6 %collective-permute-start.7 = (f32[4,48,128]{2,1,0:T(8,128)S(1)}, f32[4,48,128]{2,1,0:T(8,128)S(1)}, u32[]{:S(2)}, u32[]{:S(2)}) collective-permute-start(f32[4,48,128]{2,1,0:T(8,128)S(1)} %get-tuple-element.56), channel_id=1, source_target_pairs={{0,2},{1,3},{2,0},{3,1},{4,6},{5,7},{6,4},{7,5},{8,10},{9,11},{10,... | collective-permute-start | bytes 294920 | tf_op jit(solution)/shard_map/ppermute | solution.py:272
  15.8 4.6 %collective-permute-start.8 = (f32[4,48,128]{2,1,0:T(8,128)S(1)}, f32[4,48,128]{2,1,0:T(8,128)S(1)}, u32[]{:S(2)}, u32[]{:S(2)}) collective-permute-start(f32[4,48,128]{2,1,0:T(8,128)S(1)} %get-tuple-element.55), channel_id=1, source_target_pairs={{0,3},{1,0},{2,1},{3,2},{4,7},{5,4},{6,5},{7,6},{8,11},{9,8},{10,9... | collective-permute-start | bytes 294920 | tf_op jit(solution)/shard_map/ppermute | solution.py:272
  20.5 5.2 %copy-start = (bf16[128,512]{1,0:T(8,128)(2,1)S(1)}, bf16[128,512]{1,0:T(8,128)(2,1)}, u32[]{:S(2)}) copy-start(bf16[128,512]{1,0:T(8,128)(2,1)} %wi.1) | copy-start | bytes 393220
  20.5 6.0 %collective-permute-start.9 = (f32[48,128]{1,0:T(8,128)S(1)}, f32[48,128]{1,0:T(8,128)S(1)}, u32[]{:S(2)}, u32[]{:S(2)}) collective-permute-start(f32[48,128]{1,0:T(8,128)S(1)} %get-tuple-element.60), channel_id=1, source_target_pairs={{0,4},{4,8},{8,12},{12,0},{1,5},{5,9},{9,13},{13,1},{2,6},{6,10},{... | collective-permute-start | bytes 73736 | tf_op jit(solution)/shard_map/ppermute | solution.py:272
  21.8 5.2 %collective-permute-start.10 = (f32[48,128]{1,0:T(8,128)S(1)}, f32[48,128]{1,0:T(8,128)S(1)}, u32[]{:S(2)}, u32[]{:S(2)}) collective-permute-start(f32[48,128]{1,0:T(8,128)S(1)} %get-tuple-element.59), channel_id=1, source_target_pairs={{0,8},{4,12},{8,0},{12,4},{1,9},{5,13},{9,1},{13,5},{2,10},{6,14},... | collective-permute-start | bytes 73736 | tf_op jit(solution)/shard_map/ppermute | solution.py:272
  24.7 3.8 %collective-permute-start.11 = (f32[48,128]{1,0:T(8,128)S(1)}, f32[48,128]{1,0:T(8,128)S(1)}, u32[]{:S(2)}, u32[]{:S(2)}) collective-permute-start(f32[48,128]{1,0:T(8,128)S(1)} %get-tuple-element.58), channel_id=1, source_target_pairs={{0,12},{4,0},{8,4},{12,8},{1,13},{5,1},{9,5},{13,9},{2,14},{6,2},{... | collective-permute-start | bytes 73736 | tf_op jit(solution)/shard_map/ppermute | solution.py:272

commit v5 on v4

--- a/solution.py
+++ b/solution.py
@@ -12,7 +12,6 @@
 contract_rows = (((0,), (0,)), ((), ()))
 contract_cols = (((1,), (1,)), ((), ()))
 VMEM_LIMIT = 6 * 1024 * 1024
-PAD = 128
 
 
 def vmem_call(body, out_shape, scratch=(), given=pltpu.VMEM, kept=True):
@@ -54,10 +53,39 @@
     return decay, rest * lax.rsqrt(rest)
 
 
+def pack_column(column):
+    pieces = column.shape[0] // 8
+    lane = lax.broadcasted_iota(jnp.int32, (8, 128), 1)
+    packed = jnp.broadcast_to(column[0:8], (8, 128))
+    for k in range(1, pieces):
+        packed = jnp.where(lane < k * (128 // pieces), packed, column[8 * k : 8 * k + 8])
+    return packed
+
+
+def pack_states(out, one, two):
+    lines = one.shape[0]
+    both = jnp.concatenate([one, two], axis=1)
+    for k in range(both.shape[1] // 128):
+        out[k * lines : (k + 1) * lines, :] = both[:, 128 * k : 128 * k + 128]
+
+
+def unpack(part, lines, expand):
+    tiles = 2 * expand // 128
+    states = jnp.concatenate([part[k * lines : (k + 1) * lines, :] for k in range(tiles)], axis=1)
+    packed = part[tiles * lines :, :]
+    pieces = 2 * lines // 8
+    columns = [
+        jnp.broadcast_to(packed[:, k * (128 // pieces) : k * (128 // pieces) + 1], (8, expand)) for k in range(pieces)
+    ]
+    half = pieces // 2
+    sums = [jnp.concatenate(columns[d * half : (d + 1) * half], axis=0) for d in (0, 1)]
+    return states, jnp.concatenate(sums, axis=1)
+
+
 def edges_body(order, px_in, ct_in, wi_in, wo_in, rt_in, ss_in, *refs):
     sent = refs[: len(order)]
-    px, ct, rt, mixed, back, dec, wgt, wi, wo, ss, src, seed, ways, sems = refs[len(order) :]
-    pairs = ((px_in, px), (wi_in, wi), (ct_in, ct), (wo_in, wo), (ss_in, ss), (rt_in, rt))
+    px, ct, rt, mixed, back, dec, wgt, wi, wo, ss, src, seed, src_lines, seed_lines, ways, sems = refs[len(order) :]
+    pairs = ((ss_in, ss), (rt_in, rt), (px_in, px), (wi_in, wi), (ct_in, ct), (wo_in, wo))
     copies = [pltpu.make_async_copy(a, b, sems.at[k]) for k, (a, b) in enumerate(pairs)]
     for copy in copies:
         copy.start()
@@ -66,57 +94,54 @@
     count = height * breadth
     copies[0].wait()
     copies[1].wait()
+    for axis, length, lines in ((0, breadth, height), (1, height, breadth)):
+        one, two = 2 * axis, 2 * axis + 1
+        steps = {d: ss[d] if axis == 0 else jnp.transpose(ss[d]) for d in (one, two)}
+        for i in range(length):
+            rows = slice(i * lines, (i + 1) * lines)
+            for d, step in steps.items():
+                dec[d, rows, :], wgt[d, rows, :] = decay_pair(rt[d : d + 1, :], step[:, i : i + 1])
+        sums = jnp.concatenate([jnp.sum(step, axis=1, keepdims=True) for step in steps.values()], axis=0)
+        for way in (0, 1):
+            ways[axis, way, 2 * lines * expand // 128 :, :] = pack_column(sums)
+    for copy in copies[2:]:
+        copy.wait()
     both = jnp.dot(px[...].reshape(count, channels), wi[...], preferred_element_type=F32)
     mixed[...] = both
     inner, gate = both[:, :expand], both[:, expand:]
     put(src, slice(None), inner * sigmoid(inner))
-    copies[2].wait()
-    copies[3].wait()
     cot = ct[...].reshape(count, channels)
     bg = lax.dot_general(cot, wo[...], contract_cols, preferred_element_type=F32)
     back[...] = bg
     put(seed, slice(None), bg * (gate * sigmoid(gate)))
-    copies[4].wait()
-    copies[5].wait()
-
     for axis, name in ((0, "cols"), (1, "rows")):
         payload = ways.at[axis]
         one, two = 2 * axis, 2 * axis + 1
         length = breadth if axis == 0 else height
         lines = height if axis == 0 else breadth
 
-        def at(ref, i):
-            return get(ref, pl.ds(i, lines, stride=length) if axis == 0 else pl.ds(i * lines, lines))
-
-        steps = [ss[d] if axis == 0 else jnp.transpose(ss[d]) for d in (one, two)]
-        rates = [rt[d : d + 1, :] for d in (one, two)]
+        if axis == 0:
+            for i in range(length):
+                for ref, line_ref in ((src, src_lines), (seed, seed_lines)):
+                    put(line_ref, pl.ds(i * lines, lines), get(ref, pl.ds(i, lines, stride=length)))
+            source, grad = src_lines, seed_lines
+        else:
+            source, grad = src, seed
+
         fwd = jnp.zeros((lines, expand), F32)
         adj = jnp.zeros((lines, expand), F32)
         for i in range(length):
             rows = slice(i * lines, (i + 1) * lines)
-            d1, w1 = decay_pair(rates[0], steps[0][:, i : i + 1])
-            d2, w2 = decay_pair(rates[1], steps[1][:, i : i + 1])
-            dec[one, rows, :] = d1
-            wgt[one, rows, :] = w1
-            dec[two, rows, :] = d2
-            wgt[two, rows, :] = w2
-            fwd = d1 * fwd + w1 * at(src, i)
-            adj = d2 * (adj + at(seed, i))
-        payload[0, :, 0:expand] = fwd
-        payload[0, :, expand : 2 * expand] = adj
+            fwd = dec[one, rows, :] * fwd + wgt[one, rows, :] * get(source, rows)
+            adj = dec[two, rows, :] * (adj + get(grad, rows))
+        pack_states(payload.at[0], fwd, adj)
         fwd = jnp.zeros((lines, expand), F32)
         adj = jnp.zeros((lines, expand), F32)
         for i in reversed(range(length)):
             rows = slice(i * lines, (i + 1) * lines)
-            d1, d2, w2 = dec[one, rows, :], dec[two, rows, :], wgt[two, rows, :]
-            fwd = d2 * fwd + w2 * at(src, i)
-            adj = d1 * (adj + at(seed, i))
-        payload[1, :, 0:expand] = adj
-        payload[1, :, expand : 2 * expand] = fwd
-        lane = lax.broadcasted_iota(jnp.int32, (lines, PAD), 1)
-        sums = [jnp.sum(s, axis=1, keepdims=True) for s in steps]
-        for way in (0, 1):
-            payload[way, :, 2 * expand :] = jnp.where(lane < PAD // 2, sums[0], sums[1])
+            fwd = dec[two, rows, :] * fwd + wgt[two, rows, :] * get(source, rows)
+            adj = dec[one, rows, :] * (adj + get(grad, rows))
+        pack_states(payload.at[1], adj, fwd)
         mine = lax.axis_index(name)
         for (out_axis, k), out in zip(order, sent):
             if out_axis == name:
@@ -178,11 +203,8 @@
     parts = [received[key] for key in sorted(received) if key[0] == axis]
     count, mine = len(parts) + 1, lax.axis_index(axis)
     expand = rates[0].shape[1]
-    lines = parts[0].shape[0]
-    sums = [
-        jnp.concatenate([jnp.broadcast_to(part[:, c : c + 1], (lines, expand)) for c in (2 * expand, 2 * expand + PAD // 2)], axis=1)
-        for part in parts
-    ]
+    lines = (parts[0].shape[0] - 8) * 128 // (2 * expand)
+    parts, sums = zip(*(unpack(part, lines, expand) for part in parts))
     both = jnp.concatenate(rates, axis=1)
     below = jnp.zeros((lines, 2 * expand), F32)
     above = jnp.zeros((lines, 2 * expand), F32)
@@ -195,7 +217,7 @@
             middle = mine ^ m
             inside = ((middle - mine) * (middle - place) < 0).astype(F32)
             between = between + inside * sums[m - 1]
-        value = jnp.exp(-both * between) * parts[k - 1][:, : 2 * expand]
+        value = jnp.exp(-both * between) * parts[k - 1]
         lower = (place < mine).astype(F32)
         below = below + lower * value
         above = above + (1.0 - lower) * value
@@ -206,10 +228,8 @@
     height, breadth = shape
     received = {key: ref[...] for key, ref in zip(order, refs)}
     s_loc, g_loc, pre, suf, m_in, m_gate, gated, x_t, c_t, mix = refs[len(order) : len(order) + 10]
-    outs = refs[len(order) + 10 :]
+    *grads, out_state = refs[len(order) + 10 :]
     expand = s_loc.shape[0] * 128
-    out_state = outs[-1]
-    grads = outs[:-1]
     rates = [rt[d : d + 1, :] for d in range(4)]
     below, above = entering("rows", rates[2:], received)
     f2, a3, a2, f3 = below[:, :expand], below[:, expand:], above[:, :expand], above[:, expand:]
@@ -289,8 +309,9 @@
     four = jax.ShapeDtypeStruct((4, count, expand), F32)
     wide = jax.ShapeDtypeStruct((count, 2 * expand), F32)
     like = lambda a: jax.ShapeDtypeStruct(a.shape, a.dtype)
-    pay_cols = jax.ShapeDtypeStruct((height, 2 * expand + PAD), F32)
-    pay_rows = jax.ShapeDtypeStruct((breadth, 2 * expand + PAD), F32)
+    pay_cols, pay_rows = (
+        jax.ShapeDtypeStruct((2 * lines * expand // 128 + 8, 128), F32) for lines in (height, breadth)
+    )
     order = send_order(cols, rows)
     pays = tuple(pay_cols if axis == "cols" else pay_rows for axis, _ in order)
     outs = vmem_call(
@@ -300,8 +321,7 @@
             pltpu.VMEM(w_in.shape, BF16),
             pltpu.VMEM(w_out.shape, BF16),
             pltpu.VMEM(step_sizes.shape, F32),
-            pltpu.VMEM(tall.shape, F32),
-            pltpu.VMEM(tall.shape, F32),
+            *(pltpu.VMEM(tall.shape, F32) for _ in range(4)),
             pltpu.VMEM((2, 2, *pay_cols.shape), F32),
             pltpu.SemaphoreType.DMA((6,)),
         ],
@@ -326,9 +346,10 @@
         )
     outs = vmem_call(
         functools.partial(join_body, (height, breadth), split, order),
-        (jax.ShapeDtypeStruct((count, 2 * expand), BF16), *grads, jax.ShapeDtypeStruct((count, expand), BF16)),
+        (jax.ShapeDtypeStruct((count, 2 * expand), BF16), *grads),
+        scratch=[pltpu.VMEM((count, expand), BF16)],
     )(rt, *received.values(), s_loc, g_loc, pre, suf, m_in, m_gate, gated, x_t, c_t)
-    mix, grads = outs[0], outs[1:-1]
+    mix, grads = outs[0], outs[1:]
     grad_pixels = vmem_call(pixels_body, like(pixels), kept=False)(ct, mix, w_in)
     if split:
         parts = spread(grads[0], "cols", (1, 2, 3))

time: 29.4 us -> 28.6 us (0.973)
  Pallas kernels: 6.69 us -> 5.98 us
    pallas_call x5, Pallas kernels: 6.69 us -> 5.98 us  [call(): pl.pallas_call(body, out_shape=out_shape, in_specs=[pl.BlockSpec(memory_s...]
  transfers between devices with their start and end apart: 12 -> 12, of which waited for: 7 -> 7; matrix products, arithmetic and copies ran while one was open for 0% -> 0% of each run, Pallas kernels for 9% -> 10%
where the time goes in v5:
time: 28.6 us; the launch traced here: 28.4 us
  starting transfers between devices  15.7 us (55%)
  Pallas kernels  5.98 us (21%)
  waiting for transfers between devices  5.94 us (21%)
  between operations  0.69 us (2%)
    ppermute x6, starting transfers between devices, shifted(): lax.ppermute(value, axis, [(i, (i + k) % count) for i in range(count)])  8.11 us
    ppermute x6, starting transfers between devices, partner(): lax.ppermute(value, axis, [(i, i ^ bit) for i in range(lax.axis_size(axis...  7.63 us
    pallas_call x5, Pallas kernels, call(): pl.pallas_call(body, out_shape=out_shape, in_specs=[pl.BlockSpec(memory_s...  5.98 us
    ppermute x6, waiting for transfers between devices, shifted(): lax.ppermute(value, axis, [(i, (i + k) % count) for i in range(count)])  5.32 us
    ppermute x6, waiting for transfers between devices, partner(): lax.ppermute(value, axis, [(i, i ^ bit) for i in range(lax.axis_size(axis...  0.62 us
  transfers between devices with their start and end apart: 12, of which 7 were waited for; matrix products, arithmetic and copies ran while one was open for 0% of the time, Pallas kernels for 10%

profile of v5, /device:TPU:0, one launch (start us, length us, event | category | flops | bytes accessed | tf_op | source)
XLA Modules:
  0.0 28.4 jit_solution(17242360043987515866)
XLA Ops:
  0.6 2.0 %shard_map.85 = (f32[72,128]{1,0:T(8,128)S(1)}, f32[72,128]{1,0:T(8,128)S(1)}, f32[72,128]{1,0:T(8,128)S(1)}, f32[72,128]{1,0:T(8,128)S(1)}, f32[72,128]{1,0:T(8...) custom-call(bf16[16,16,128]{2,1,0:T(8,128)(2,1)} %px_in.1, ...), custom_call_target="tpu_custom_call" | custom-call | tf_op jit(solution)/shard_map/pallas_call | solution.py:24
  2.6 5.1 %collective-permute-start = (f32[72,128]{1,0:T(8,128)S(1)}, f32[72,128]{1,0:T(8,128)S(1)}, u32[]{:S(2)}, u32[]{:S(2)}) collective-permute-start(f32[72,128]{1,0:T(8,128)S(1)} %get-tuple-element.31), channel_id=1, source_target_pairs={{0,12},{4,8},{8,4},{12,0},{1,13},{5,9},{9,5},{13,1},{2,14},{6,10},... | collective-permute-start | bytes 110600 | tf_op jit(solution)/shard_map/ppermute | solution.py:283
  7.7 0.0 collective-permute-start.1
  7.7 0.6 %collective-permute-start.2 = (f32[72,128]{1,0:T(8,128)S(1)}, f32[72,128]{1,0:T(8,128)S(1)}, u32[]{:S(2)}, u32[]{:S(2)}) collective-permute-start(f32[72,128]{1,0:T(8,128)S(1)} %get-tuple-element.33), channel_id=1, source_target_pairs={{0,4},{4,0},{8,12},{12,8},{1,5},{5,1},{9,13},{13,9},{2,6},{6,2},{1... | collective-permute-start | bytes 110600 | tf_op jit(solution)/shard_map/ppermute | solution.py:283
  8.4 0.4 %collective-permute-start.3 = (f32[72,128]{1,0:T(8,128)S(1)}, f32[72,128]{1,0:T(8,128)S(1)}, u32[]{:S(2)}, u32[]{:S(2)}) collective-permute-start(f32[72,128]{1,0:T(8,128)S(1)} %get-tuple-element.34), channel_id=1, source_target_pairs={{0,3},{1,2},{2,1},{3,0},{4,7},{5,6},{6,5},{7,4},{8,11},{9,10},{10,... | collective-permute-start | bytes 110600 | tf_op jit(solution)/shard_map/ppermute | solution.py:283
  8.7 1.3 %collective-permute-start.4 = (f32[72,128]{1,0:T(8,128)S(1)}, f32[72,128]{1,0:T(8,128)S(1)}, u32[]{:S(2)}, u32[]{:S(2)}) collective-permute-start(f32[72,128]{1,0:T(8,128)S(1)} %get-tuple-element.35), channel_id=1, source_target_pairs={{0,2},{1,3},{2,0},{3,1},{4,6},{5,7},{6,4},{7,5},{8,10},{9,11},{10,... | collective-permute-start | bytes 110600 | tf_op jit(solution)/shard_map/ppermute | solution.py:283
  10.0 0.2 collective-permute-start.5
  10.2 1.9 %shard_map.86 = (f32[2,256,128]{2,1,0:T(8,128)S(1)}, f32[2,256,128]{2,1,0:T(8,128)S(1)}, f32[4,2,256,128]{3,2,1,0:T(8,128)S(1)}, f32[4,2,256,128]{3,2,1,0:T(8,12...) custom-call(bf16[16,16,128]{2,1,0:T(8,128)(2,1)S(1)} %get-tuple-elem, ...), custom_call_target="tpu_custom_call" | custom-call | tf_op jit(solution)/shard_map/pallas_call | solution.py:24
  12.1 0.5 %collective-permute-done.1.refs_1_ = f32[72,128]{1,0:T(8,128)S(1)} collective-permute-done((f32[72,128]{1,0:T(8,128)S(1)}, f32[72,128]{1,0:T(8,128)S(1)}, u32[]{:S(2)}, u32[]{:S(2)}) %collective-permute-start.1) | collective-permute-done | bytes 36896 | tf_op jit(solution)/shard_map/ppermute | solution.py:283
  12.6 0.1 collective-permute-done.4.refs_4_
  12.7 0.6 %shard_map.87 = (bf16[256,512]{1,0:T(8,128)(2,1)S(1)}, f32[4,4,48,128]{3,2,1,0:T(8,128)S(1)}) custom-call(f32[4,256]{1,0:T(4,128)S(1)} %get-tuple-element.30.rt, f32[72,128]{1,0:T(8,128)S(1)} %collective-permute-done.refs_0_, f32[72,128]{1,0:T(8,128)S(1)} %collective-permute-done.1.refs_1_, f32[72,128]{1,0:T(8,128)S(1)} %collective-permute-done.2.refs_2_, ...), custom_call_target="tpu_custom_call" | custom-call | tf_op jit(solution)/shard_map/pallas_call | solution.py:24
  13.4 0.3 collective-permute-start.6
  13.7 1.3 %collective-permute-start.7 = (f32[4,48,128]{2,1,0:T(8,128)S(1)}, f32[4,48,128]{2,1,0:T(8,128)S(1)}, u32[]{:S(2)}, u32[]{:S(2)}) collective-permute-start(f32[4,48,128]{2,1,0:T(8,128)S(1)} %get-tuple-element.56), channel_id=1, source_target_pairs={{0,2},{1,3},{2,0},{3,1},{4,6},{5,7},{6,4},{7,5},{8,10},{9,11},{10,... | collective-permute-start | bytes 294920 | tf_op jit(solution)/shard_map/ppermute | solution.py:292
  15.0 1.4 %collective-permute-start.8 = (f32[4,48,128]{2,1,0:T(8,128)S(1)}, f32[4,48,128]{2,1,0:T(8,128)S(1)}, u32[]{:S(2)}, u32[]{:S(2)}) collective-permute-start(f32[4,48,128]{2,1,0:T(8,128)S(1)} %get-tuple-element.55), channel_id=1, source_target_pairs={{0,3},{1,0},{2,1},{3,2},{4,7},{5,4},{6,5},{7,6},{8,11},{9,8},{10,9... | collective-permute-start | bytes 294920 | tf_op jit(solution)/shard_map/ppermute | solution.py:292
  16.4 1.4 %collective-permute-done.6 = f32[4,48,128]{2,1,0:T(8,128)S(1)} collective-permute-done((f32[4,48,128]{2,1,0:T(8,128)S(1)}, f32[4,48,128]{2,1,0:T(8,128)S(1)}, u32[]{:S(2)}, u32[]{:S(2)}) %collective-permute-start.6) | collective-permute-done | bytes 98336 | tf_op jit(solution)/shard_map/ppermute | solution.py:292
  17.8 1.5 %collective-permute-done.7 = f32[4,48,128]{2,1,0:T(8,128)S(1)} collective-permute-done((f32[4,48,128]{2,1,0:T(8,128)S(1)}, f32[4,48,128]{2,1,0:T(8,128)S(1)}, u32[]{:S(2)}, u32[]{:S(2)}) %collective-permute-start.7) | collective-permute-done | bytes 98336 | tf_op jit(solution)/shard_map/ppermute | solution.py:292
  19.3 0.3 %collective-permute-done.8 = f32[4,48,128]{2,1,0:T(8,128)S(1)} collective-permute-done((f32[4,48,128]{2,1,0:T(8,128)S(1)}, f32[4,48,128]{2,1,0:T(8,128)S(1)}, u32[]{:S(2)}, u32[]{:S(2)}) %collective-permute-start.8) | collective-permute-done | bytes 98336 | tf_op jit(solution)/shard_map/ppermute | solution.py:292
  19.7 1.3 %collective-permute-start.9 = (f32[48,128]{1,0:T(8,128)S(1)}, f32[48,128]{1,0:T(8,128)S(1)}, u32[]{:S(2)}, u32[]{:S(2)}) collective-permute-start(f32[48,128]{1,0:T(8,128)S(1)} %get-tuple-element.60), channel_id=1, source_target_pairs={{0,4},{4,8},{8,12},{12,0},{1,5},{5,9},{9,13},{13,1},{2,6},{6,10},{... | collective-permute-start | bytes 73736 | tf_op jit(solution)/shard_map/ppermute | solution.py:292
  21.0 2.9 %collective-permute-start.10 = (f32[48,128]{1,0:T(8,128)S(1)}, f32[48,128]{1,0:T(8,128)S(1)}, u32[]{:S(2)}, u32[]{:S(2)}) collective-permute-start(f32[48,128]{1,0:T(8,128)S(1)} %get-tuple-element.59), channel_id=1, source_target_pairs={{0,8},{4,12},{8,0},{12,4},{1,9},{5,13},{9,1},{13,5},{2,10},{6,14},... | collective-permute-start | bytes 73736 | tf_op jit(solution)/shard_map/ppermute | solution.py:292
  23.9 0.9 %collective-permute-start.11 = (f32[48,128]{1,0:T(8,128)S(1)}, f32[48,128]{1,0:T(8,128)S(1)}, u32[]{:S(2)}, u32[]{:S(2)}) collective-permute-start(f32[48,128]{1,0:T(8,128)S(1)} %get-tuple-element.58), channel_id=1, source_target_pairs={{0,12},{4,0},{8,4},{12,8},{1,13},{5,1},{9,5},{13,9},{2,14},{6,2},{... | collective-permute-start | bytes 73736 | tf_op jit(solution)/shard_map/ppermute | solution.py:292
  24.8 0.9 %shard_map.88 = bf16[16,16,128]{2,1,0:T(8,128)(2,1)} custom-call(bf16[16,16,128]{2,1,0:T(8,128)(2,1)S(1)} %get-tuple-element.29.ct, bf16[256,512]{1,0:T(8,128)(2,1)S(1)} %get-tuple-element.51.mix, bf16[128,512]{1,0:T(8,128)(2,1)S(1)} %copy-done), custom_call_target="tpu_custom_call" | custom-call | tf_op jit(solution)/shard_map/pallas_call | solution.py:24
  25.7 0.4 %collective-permute-done.10.two = f32[48,128]{1,0:T(8,128)S(1)} collective-permute-done((f32[48,128]{1,0:T(8,128)S(1)}, f32[48,128]{1,0:T(8,128)S(1)}, u32[]{:S(2)}, u32[]{:S(2)}) %collective-permute-start.10) | collective-permute-done | bytes 24608 | tf_op jit(solution)/shard_map/ppermute | solution.py:292
  26.1 1.7 %collective-permute-done.11.three = f32[48,128]{1,0:T(8,128)S(1)} collective-permute-done((f32[48,128]{1,0:T(8,128)S(1)}, f32[48,128]{1,0:T(8,128)S(1)}, u32[]{:S(2)}, u32[]{:S(2)}) %collective-permute-start.11) | collective-permute-done | bytes 24608 | tf_op jit(solution)/shard_map/ppermute | solution.py:292
  27.8 0.7 %shard_map.89 = (f32[32,128]{1,0:T(8,128)}, f32[32,64]{1,0:T(8,128)}) custom-call(f32[48,128]{1,0:T(8,128)S(1)} %get-tuple-element.61.mine, f32[48,128]{1,0:T(8,128)S(1)} %collective-permute-done.9.one, f32[48,128]{1,0:T(8,128)S(1)} %collective-permute-done.10.two, f32[48,128]{1,0:T(8,128)S(1)} %collective-permute-done.11.three), custom_call_target="tpu_custom_call" | custom-call | tf_op jit(solution)/shard_map/pallas_call | solution.py:24
  (10 shorter events, 0.1 us)
Async XLA Ops:
  2.6 7.4 %collective-permute-start = (f32[72,128]{1,0:T(8,128)S(1)}, f32[72,128]{1,0:T(8,128)S(1)}, u32[]{:S(2)}, u32[]{:S(2)}) collective-permute-start(f32[72,128]{1,0:T(8,128)S(1)} %get-tuple-element.31), channel_id=1, source_target_pairs={{0,12},{4,8},{8,4},{12,0},{1,13},{5,9},{9,5},{13,1},{2,14},{6,10},... | collective-permute-start | bytes 110600 | tf_op jit(solution)/shard_map/ppermute | solution.py:283
  7.7 4.9 %collective-permute-start.1 = (f32[72,128]{1,0:T(8,128)S(1)}, f32[72,128]{1,0:T(8,128)S(1)}, u32[]{:S(2)}, u32[]{:S(2)}) collective-permute-start(f32[72,128]{1,0:T(8,128)S(1)} %get-tuple-element.32), channel_id=1, source_target_pairs={{0,8},{4,12},{8,0},{12,4},{1,9},{5,13},{9,1},{13,5},{2,10},{6,14},... | collective-permute-start | bytes 110600 | tf_op jit(solution)/shard_map/ppermute | solution.py:283
  7.7 4.9 %collective-permute-start.2 = (f32[72,128]{1,0:T(8,128)S(1)}, f32[72,128]{1,0:T(8,128)S(1)}, u32[]{:S(2)}, u32[]{:S(2)}) collective-permute-start(f32[72,128]{1,0:T(8,128)S(1)} %get-tuple-element.33), channel_id=1, source_target_pairs={{0,4},{4,0},{8,12},{12,8},{1,5},{5,1},{9,13},{13,9},{2,6},{6,2},{1... | collective-permute-start | bytes 110600 | tf_op jit(solution)/shard_map/ppermute | solution.py:283
  8.4 4.2 %collective-permute-start.3 = (f32[72,128]{1,0:T(8,128)S(1)}, f32[72,128]{1,0:T(8,128)S(1)}, u32[]{:S(2)}, u32[]{:S(2)}) collective-permute-start(f32[72,128]{1,0:T(8,128)S(1)} %get-tuple-element.34), channel_id=1, source_target_pairs={{0,3},{1,2},{2,1},{3,0},{4,7},{5,6},{6,5},{7,4},{8,11},{9,10},{10,... | collective-permute-start | bytes 110600 | tf_op jit(solution)/shard_map/ppermute | solution.py:283
  8.7 4.0 %collective-permute-start.4 = (f32[72,128]{1,0:T(8,128)S(1)}, f32[72,128]{1,0:T(8,128)S(1)}, u32[]{:S(2)}, u32[]{:S(2)}) collective-permute-start(f32[72,128]{1,0:T(8,128)S(1)} %get-tuple-element.35), channel_id=1, source_target_pairs={{0,2},{1,3},{2,0},{3,1},{4,6},{5,7},{6,4},{7,5},{8,10},{9,11},{10,... | collective-permute-start | bytes 110600 | tf_op jit(solution)/shard_map/ppermute | solution.py:283
  10.0 2.7 %collective-permute-start.5 = (f32[72,128]{1,0:T(8,128)S(1)}, f32[72,128]{1,0:T(8,128)S(1)}, u32[]{:S(2)}, u32[]{:S(2)}) collective-permute-start(f32[72,128]{1,0:T(8,128)S(1)} %get-tuple-element.36), channel_id=1, source_target_pairs={{0,1},{1,0},{2,3},{3,2},{4,5},{5,4},{6,7},{7,6},{8,9},{9,8},{10,11... | collective-permute-start | bytes 110600 | tf_op jit(solution)/shard_map/ppermute | solution.py:283
  13.4 4.4 %collective-permute-start.6 = (f32[4,48,128]{2,1,0:T(8,128)S(1)}, f32[4,48,128]{2,1,0:T(8,128)S(1)}, u32[]{:S(2)}, u32[]{:S(2)}) collective-permute-start(f32[4,48,128]{2,1,0:T(8,128)S(1)} %get-tuple-element.57), channel_id=1, source_target_pairs={{0,1},{1,2},{2,3},{3,0},{4,5},{5,6},{6,7},{7,4},{8,9},{9,10},{10,1... | collective-permute-start | bytes 294920 | tf_op jit(solution)/shard_map/ppermute | solution.py:292
  13.7 5.6 %collective-permute-start.7 = (f32[4,48,128]{2,1,0:T(8,128)S(1)}, f32[4,48,128]{2,1,0:T(8,128)S(1)}, u32[]{:S(2)}, u32[]{:S(2)}) collective-permute-start(f32[4,48,128]{2,1,0:T(8,128)S(1)} %get-tuple-element.56), channel_id=1, source_target_pairs={{0,2},{1,3},{2,0},{3,1},{4,6},{5,7},{6,4},{7,5},{8,10},{9,11},{10,... | collective-permute-start | bytes 294920 | tf_op jit(solution)/shard_map/ppermute | solution.py:292
  15.0 4.6 %collective-permute-start.8 = (f32[4,48,128]{2,1,0:T(8,128)S(1)}, f32[4,48,128]{2,1,0:T(8,128)S(1)}, u32[]{:S(2)}, u32[]{:S(2)}) collective-permute-start(f32[4,48,128]{2,1,0:T(8,128)S(1)} %get-tuple-element.55), channel_id=1, source_target_pairs={{0,3},{1,0},{2,1},{3,2},{4,7},{5,4},{6,5},{7,6},{8,11},{9,8},{10,9... | collective-permute-start | bytes 294920 | tf_op jit(solution)/shard_map/ppermute | solution.py:292
  19.7 5.2 %copy-start = (bf16[128,512]{1,0:T(8,128)(2,1)S(1)}, bf16[128,512]{1,0:T(8,128)(2,1)}, u32[]{:S(2)}) copy-start(bf16[128,512]{1,0:T(8,128)(2,1)} %wi.1) | copy-start | bytes 393220
  19.7 6.0 %collective-permute-start.9 = (f32[48,128]{1,0:T(8,128)S(1)}, f32[48,128]{1,0:T(8,128)S(1)}, u32[]{:S(2)}, u32[]{:S(2)}) collective-permute-start(f32[48,128]{1,0:T(8,128)S(1)} %get-tuple-element.60), channel_id=1, source_target_pairs={{0,4},{4,8},{8,12},{12,0},{1,5},{5,9},{9,13},{13,1},{2,6},{6,10},{... | collective-permute-start | bytes 73736 | tf_op jit(solution)/shard_map/ppermute | solution.py:292
  21.0 5.1 %collective-permute-start.10 = (f32[48,128]{1,0:T(8,128)S(1)}, f32[48,128]{1,0:T(8,128)S(1)}, u32[]{:S(2)}, u32[]{:S(2)}) collective-permute-start(f32[48,128]{1,0:T(8,128)S(1)} %get-tuple-element.59), channel_id=1, source_target_pairs={{0,8},{4,12},{8,0},{12,4},{1,9},{5,13},{9,1},{13,5},{2,10},{6,14},... | collective-permute-start | bytes 73736 | tf_op jit(solution)/shard_map/ppermute | solution.py:292
  23.9 3.8 %collective-permute-start.11 = (f32[48,128]{1,0:T(8,128)S(1)}, f32[48,128]{1,0:T(8,128)S(1)}, u32[]{:S(2)}, u32[]{:S(2)}) collective-permute-start(f32[48,128]{1,0:T(8,128)S(1)} %get-tuple-element.58), channel_id=1, source_target_pairs={{0,12},{4,0},{8,4},{12,8},{1,13},{5,1},{9,5},{13,9},{2,14},{6,2},{... | collective-permute-start | bytes 73736 | tf_op jit(solution)/shard_map/ppermute | solution.py:292

commit v6 on v5

--- a/solution.py
+++ b/solution.py
@@ -142,10 +142,10 @@
             fwd = dec[two, rows, :] * fwd + wgt[two, rows, :] * get(source, rows)
             adj = dec[one, rows, :] * (adj + get(grad, rows))
         pack_states(payload.at[1], adj, fwd)
-        mine = lax.axis_index(name)
-        for (out_axis, k), out in zip(order, sent):
+        mine, count_of = lax.axis_index(name), 1 + sum(key[0] == name for key in order)
+        for (out_axis, kind, k), out in zip(order, sent):
             if out_axis == name:
-                out[...] = payload[((mine ^ k) < mine).astype(jnp.int32)]
+                out[...] = payload[(target(mine, kind, k, count_of) < mine).astype(jnp.int32)]
 
 
 def local_body(px, ct, mixed, back, dec, wgt, s_loc, g_loc, pre, suf, m_in, m_gate, gated, x_t, c_t, src, seed):
@@ -199,25 +199,31 @@
         go(reversed(range(length)), two, one, False)
 
 
+def target(mine, kind, k, count):
+    if kind == "xor":
+        return mine ^ k
+    place = mine + k
+    return jnp.where(place < count, place, place - count)
+
+
 def entering(axis, rates, received):
-    parts = [received[key] for key in sorted(received) if key[0] == axis]
+    keys = [key for key in received if key[0] == axis]
+    parts = [received[key] for key in keys]
     count, mine = len(parts) + 1, lax.axis_index(axis)
     expand = rates[0].shape[1]
     lines = (parts[0].shape[0] - 8) * 128 // (2 * expand)
     parts, sums = zip(*(unpack(part, lines, expand) for part in parts))
+    places = [target(mine, kind, k if kind == "xor" else count - k, count) for _, kind, k in keys]
     both = jnp.concatenate(rates, axis=1)
     below = jnp.zeros((lines, 2 * expand), F32)
     above = jnp.zeros((lines, 2 * expand), F32)
-    for k in range(1, count):
-        place = mine ^ k
+    for k, place in enumerate(places):
         between = jnp.zeros((lines, 2 * expand), F32)
-        for m in range(1, count):
-            if m == k:
-                continue
-            middle = mine ^ m
-            inside = ((middle - mine) * (middle - place) < 0).astype(F32)
-            between = between + inside * sums[m - 1]
-        value = jnp.exp(-both * between) * parts[k - 1]
+        for m, middle in enumerate(places):
+            if m != k:
+                inside = ((middle - mine) * (middle - place) < 0).astype(F32)
+                between = between + inside * sums[m]
+        value = jnp.exp(-both * between) * parts[k]
         lower = (place < mine).astype(F32)
         below = below + lower * value
         above = above + (1.0 - lower) * value
@@ -279,23 +285,20 @@
     g_out[16:32, :] = total[32:48, 64:128]
 
 
-def partner(value, axis, bit):
-    return lax.ppermute(value, axis, [(i, i ^ bit) for i in range(lax.axis_size(axis))])
-
-
 def send_order(cols, rows):
-    return [("rows", k) for k in reversed(range(1, rows))] + [("cols", k) for k in reversed(range(1, cols))]
-
-
-def shifted(value, axis, k):
+    near = sorted(range(1, rows), key=lambda k: min(k, rows - k))
+    return [("rows", "shift", k) for k in near] + [("cols", "xor", k) for k in reversed(range(1, cols))]
+
+
+def transfer(value, axis, kind, k):
     count = lax.axis_size(axis)
-    return lax.ppermute(value, axis, [(i, (i + k) % count) for i in range(count)])
+    return lax.ppermute(value, axis, [(i, i ^ k if kind == "xor" else (i + k) % count) for i in range(count)])
 
 
 def spread(value, axis, order):
     count, mine = lax.axis_size(axis), lax.axis_index(axis)
     pick = lambda i: lax.dynamic_index_in_dim(value, i, 0, keepdims=False)
-    return [pick(mine)] + [shifted(pick(lax.rem(mine + k, count)), axis, k) for k in order]
+    return [pick(mine)] + [transfer(pick(target(mine, kind, k, count)), axis, kind, k) for kind, k in order]
 
 
 def per_device(pixels, cotangent, w_in, w_out, decay_rates, step_sizes):
@@ -313,7 +316,7 @@
         jax.ShapeDtypeStruct((2 * lines * expand // 128 + 8, 128), F32) for lines in (height, breadth)
     )
     order = send_order(cols, rows)
-    pays = tuple(pay_cols if axis == "cols" else pay_rows for axis, _ in order)
+    pays = tuple(pay_cols if axis == "cols" else pay_rows for axis, _, _ in order)
     outs = vmem_call(
         functools.partial(edges_body, order),
         (*pays, like(pixels), like(cotangent), like(decay_rates), wide, full, four, four),
@@ -335,7 +338,7 @@
         (tall, tall, four_tall, four_tall, full, full, full, turned, turned),
         scratch=[pltpu.VMEM(tall.shape, F32)] * 2,
     )(px, ct, mixed, back, dec, wgt)
-    received = {key: partner(payload, *key) for key, payload in zip(order, sent)}
+    received = {key: transfer(payload, *key) for key, payload in zip(order, sent)}
     split = rows == 4 and cols == 4 and channels == 128 and expand == 256
     if split:
         grads = (jax.ShapeDtypeStruct((4, 4, 48, 128), F32),)
@@ -352,9 +355,9 @@
     mix, grads = outs[0], outs[1:]
     grad_pixels = vmem_call(pixels_body, like(pixels), kept=False)(ct, mix, w_in)
     if split:
-        parts = spread(grads[0], "cols", (1, 2, 3))
+        parts = spread(grads[0], "cols", [("shift", k) for k in (1, 2, 3)])
         value = (parts[0] + parts[1]) + (parts[2] + parts[3])
-        parts = spread(value, "rows", (1, 2, 3))
+        parts = spread(value, "rows", [("shift", k) for k in (1, 2, 3)])
         grad_in, grad_out = vmem_call(
             final_body, (jax.ShapeDtypeStruct((32, 128), F32), jax.ShapeDtypeStruct((32, 64), F32)), kept=False
         )(*parts)

time: 28.6 us -> 27.6 us (0.965)
  waiting for transfers between devices: 5.94 us -> 4.55 us
  starting transfers between devices: 15.7 us -> 16.1 us
    ppermute x12, waiting for transfers between devices: 5.94 us -> 4.55 us  [transfer(): lax.ppermute(value, axis, [(i, i ^ k if kind == 'xor' else (i + k) % coun...]
    ppermute x12, starting transfers between devices: 15.7 us -> 16.1 us  [transfer(): lax.ppermute(value, axis, [(i, i ^ k if kind == 'xor' else (i + k) % coun...]
where the time goes in v6:
time: 27.6 us; the launch traced here: 27.4 us
  starting transfers between devices  16.1 us (58%)
  Pallas kernels  5.98 us (22%)
  waiting for transfers between devices  4.55 us (16%)
  between operations  0.7 us (3%)
    ppermute x12, starting transfers between devices, transfer(): lax.ppermute(value, axis, [(i, i ^ k if kind == 'xor' else (i + k) % coun...  16.1 us
    pallas_call x5, Pallas kernels, call(): pl.pallas_call(body, out_shape=out_shape, in_specs=[pl.BlockSpec(memory_s...  5.98 us
    ppermute x12, waiting for transfers between devices, transfer(): lax.ppermute(value, axis, [(i, i ^ k if kind == 'xor' else (i + k) % coun...  4.55 us
  transfers between devices with their start and end apart: 12, of which 7 were waited for; matrix products, arithmetic and copies ran while one was open for 0% of the time, Pallas kernels for 10%

profile of v6, /device:TPU:0, one launch (start us, length us, event | category | flops | bytes accessed | tf_op | source)
XLA Modules:
  0.0 27.4 jit_solution(11086402410381159604)
XLA Ops:
  0.6 2.0 %shard_map.85 = (f32[72,128]{1,0:T(8,128)S(1)}, f32[72,128]{1,0:T(8,128)S(1)}, f32[72,128]{1,0:T(8,128)S(1)}, f32[72,128]{1,0:T(8,128)S(1)}, f32[72,128]{1,0:T(8...) custom-call(bf16[16,16,128]{2,1,0:T(8,128)(2,1)} %px_in.1, ...), custom_call_target="tpu_custom_call" | custom-call | tf_op jit(solution)/shard_map/pallas_call | solution.py:24
  2.6 3.1 %collective-permute-start = (f32[72,128]{1,0:T(8,128)S(1)}, f32[72,128]{1,0:T(8,128)S(1)}, u32[]{:S(2)}, u32[]{:S(2)}) collective-permute-start(f32[72,128]{1,0:T(8,128)S(1)} %get-tuple-element.31), channel_id=1, source_target_pairs={{0,4},{4,8},{8,12},{12,0},{1,5},{5,9},{9,13},{13,1},{2,6},{6,10},{... | collective-permute-start | bytes 110600 | tf_op jit(solution)/shard_map/ppermute | solution.py:295
  5.7 2.1 %collective-permute-start.1 = (f32[72,128]{1,0:T(8,128)S(1)}, f32[72,128]{1,0:T(8,128)S(1)}, u32[]{:S(2)}, u32[]{:S(2)}) collective-permute-start(f32[72,128]{1,0:T(8,128)S(1)} %get-tuple-element.32), channel_id=1, source_target_pairs={{0,12},{4,0},{8,4},{12,8},{1,13},{5,1},{9,5},{13,9},{2,14},{6,2},{... | collective-permute-start | bytes 110600 | tf_op jit(solution)/shard_map/ppermute | solution.py:295
  7.8 0.9 %collective-permute-start.2 = (f32[72,128]{1,0:T(8,128)S(1)}, f32[72,128]{1,0:T(8,128)S(1)}, u32[]{:S(2)}, u32[]{:S(2)}) collective-permute-start(f32[72,128]{1,0:T(8,128)S(1)} %get-tuple-element.33), channel_id=1, source_target_pairs={{0,8},{4,12},{8,0},{12,4},{1,9},{5,13},{9,1},{13,5},{2,10},{6,14},... | collective-permute-start | bytes 110600 | tf_op jit(solution)/shard_map/ppermute | solution.py:295
  8.7 0.1 collective-permute-start.3
  8.8 1.4 %collective-permute-start.4 = (f32[72,128]{1,0:T(8,128)S(1)}, f32[72,128]{1,0:T(8,128)S(1)}, u32[]{:S(2)}, u32[]{:S(2)}) collective-permute-start(f32[72,128]{1,0:T(8,128)S(1)} %get-tuple-element.35), channel_id=1, source_target_pairs={{0,2},{1,3},{2,0},{3,1},{4,6},{5,7},{6,4},{7,5},{8,10},{9,11},{10,... | collective-permute-start | bytes 110600 | tf_op jit(solution)/shard_map/ppermute | solution.py:295
  10.3 0.3 %collective-permute-start.5 = (f32[72,128]{1,0:T(8,128)S(1)}, f32[72,128]{1,0:T(8,128)S(1)}, u32[]{:S(2)}, u32[]{:S(2)}) collective-permute-start(f32[72,128]{1,0:T(8,128)S(1)} %get-tuple-element.36), channel_id=1, source_target_pairs={{0,1},{1,0},{2,3},{3,2},{4,5},{5,4},{6,7},{7,6},{8,9},{9,8},{10,11... | collective-permute-start | bytes 110600 | tf_op jit(solution)/shard_map/ppermute | solution.py:295
  10.6 1.9 %shard_map.86 = (f32[2,256,128]{2,1,0:T(8,128)S(1)}, f32[2,256,128]{2,1,0:T(8,128)S(1)}, f32[4,2,256,128]{3,2,1,0:T(8,128)S(1)}, f32[4,2,256,128]{3,2,1,0:T(8,12...) custom-call(bf16[16,16,128]{2,1,0:T(8,128)(2,1)S(1)} %get-tuple-elem, ...), custom_call_target="tpu_custom_call" | custom-call | tf_op jit(solution)/shard_map/pallas_call | solution.py:24
  12.5 0.2 collective-permute-done.2.refs_2_
  12.6 0.3 collective-permute-done.4.refs_4_
  12.9 0.6 %shard_map.87 = (bf16[256,512]{1,0:T(8,128)(2,1)S(1)}, f32[4,4,48,128]{3,2,1,0:T(8,128)S(1)}) custom-call(f32[4,256]{1,0:T(4,128)S(1)} %get-tuple-element.30.rt, f32[72,128]{1,0:T(8,128)S(1)} %collective-permute-done.refs_0_, f32[72,128]{1,0:T(8,128)S(1)} %collective-permute-done.1.refs_1_, f32[72,128]{1,0:T(8,128)S(1)} %collective-permute-done.2.refs_2_, ...), custom_call_target="tpu_custom_call" | custom-call | tf_op jit(solution)/shard_map/pallas_call | solution.py:24
  13.6 0.3 %collective-permute-start.6 = (f32[4,48,128]{2,1,0:T(8,128)S(1)}, f32[4,48,128]{2,1,0:T(8,128)S(1)}, u32[]{:S(2)}, u32[]{:S(2)}) collective-permute-start(f32[4,48,128]{2,1,0:T(8,128)S(1)} %get-tuple-element.57), channel_id=1, source_target_pairs={{0,1},{1,2},{2,3},{3,0},{4,5},{5,6},{6,7},{7,4},{8,9},{9,10},{10,1... | collective-permute-start | bytes 294920 | tf_op jit(solution)/shard_map/ppermute | solution.py:295
  13.9 1.3 %collective-permute-start.7 = (f32[4,48,128]{2,1,0:T(8,128)S(1)}, f32[4,48,128]{2,1,0:T(8,128)S(1)}, u32[]{:S(2)}, u32[]{:S(2)}) collective-permute-start(f32[4,48,128]{2,1,0:T(8,128)S(1)} %get-tuple-element.56), channel_id=1, source_target_pairs={{0,2},{1,3},{2,0},{3,1},{4,6},{5,7},{6,4},{7,5},{8,10},{9,11},{10,... | collective-permute-start | bytes 294920 | tf_op jit(solution)/shard_map/ppermute | solution.py:295
  15.2 1.4 %collective-permute-start.8 = (f32[4,48,128]{2,1,0:T(8,128)S(1)}, f32[4,48,128]{2,1,0:T(8,128)S(1)}, u32[]{:S(2)}, u32[]{:S(2)}) collective-permute-start(f32[4,48,128]{2,1,0:T(8,128)S(1)} %get-tuple-element.55), channel_id=1, source_target_pairs={{0,3},{1,0},{2,1},{3,2},{4,7},{5,4},{6,5},{7,6},{8,11},{9,8},{10,9... | collective-permute-start | bytes 294920 | tf_op jit(solution)/shard_map/ppermute | solution.py:295
  16.6 1.3 %collective-permute-done.6 = f32[4,48,128]{2,1,0:T(8,128)S(1)} collective-permute-done((f32[4,48,128]{2,1,0:T(8,128)S(1)}, f32[4,48,128]{2,1,0:T(8,128)S(1)}, u32[]{:S(2)}, u32[]{:S(2)}) %collective-permute-start.6) | collective-permute-done | bytes 98336 | tf_op jit(solution)/shard_map/ppermute | solution.py:295
  17.9 1.6 %collective-permute-done.7 = f32[4,48,128]{2,1,0:T(8,128)S(1)} collective-permute-done((f32[4,48,128]{2,1,0:T(8,128)S(1)}, f32[4,48,128]{2,1,0:T(8,128)S(1)}, u32[]{:S(2)}, u32[]{:S(2)}) %collective-permute-start.7) | collective-permute-done | bytes 98336 | tf_op jit(solution)/shard_map/ppermute | solution.py:295
  19.5 0.3 %collective-permute-done.8 = f32[4,48,128]{2,1,0:T(8,128)S(1)} collective-permute-done((f32[4,48,128]{2,1,0:T(8,128)S(1)}, f32[4,48,128]{2,1,0:T(8,128)S(1)}, u32[]{:S(2)}, u32[]{:S(2)}) %collective-permute-start.8) | collective-permute-done | bytes 98336 | tf_op jit(solution)/shard_map/ppermute | solution.py:295
  19.9 1.6 %collective-permute-start.9 = (f32[48,128]{1,0:T(8,128)S(1)}, f32[48,128]{1,0:T(8,128)S(1)}, u32[]{:S(2)}, u32[]{:S(2)}) collective-permute-start(f32[48,128]{1,0:T(8,128)S(1)} %get-tuple-element.60), channel_id=1, source_target_pairs={{0,4},{4,8},{8,12},{12,0},{1,5},{5,9},{9,13},{13,1},{2,6},{6,10},{... | collective-permute-start | bytes 73736 | tf_op jit(solution)/shard_map/ppermute | solution.py:295
  21.5 1.0 %collective-permute-start.10 = (f32[48,128]{1,0:T(8,128)S(1)}, f32[48,128]{1,0:T(8,128)S(1)}, u32[]{:S(2)}, u32[]{:S(2)}) collective-permute-start(f32[48,128]{1,0:T(8,128)S(1)} %get-tuple-element.59), channel_id=1, source_target_pairs={{0,8},{4,12},{8,0},{12,4},{1,9},{5,13},{9,1},{13,5},{2,10},{6,14},... | collective-permute-start | bytes 73736 | tf_op jit(solution)/shard_map/ppermute | solution.py:295
  22.5 2.5 %collective-permute-start.11 = (f32[48,128]{1,0:T(8,128)S(1)}, f32[48,128]{1,0:T(8,128)S(1)}, u32[]{:S(2)}, u32[]{:S(2)}) collective-permute-start(f32[48,128]{1,0:T(8,128)S(1)} %get-tuple-element.58), channel_id=1, source_target_pairs={{0,12},{4,0},{8,4},{12,8},{1,13},{5,1},{9,5},{13,9},{2,14},{6,2},{... | collective-permute-start | bytes 73736 | tf_op jit(solution)/shard_map/ppermute | solution.py:295
  25.0 0.9 %shard_map.88 = bf16[16,16,128]{2,1,0:T(8,128)(2,1)} custom-call(bf16[16,16,128]{2,1,0:T(8,128)(2,1)S(1)} %get-tuple-element.29.ct, bf16[256,512]{1,0:T(8,128)(2,1)S(1)} %get-tuple-element.51.mix, bf16[128,512]{1,0:T(8,128)(2,1)S(1)} %copy-done), custom_call_target="tpu_custom_call" | custom-call | tf_op jit(solution)/shard_map/pallas_call | solution.py:24
  25.9 0.7 %collective-permute-done.10.two = f32[48,128]{1,0:T(8,128)S(1)} collective-permute-done((f32[48,128]{1,0:T(8,128)S(1)}, f32[48,128]{1,0:T(8,128)S(1)}, u32[]{:S(2)}, u32[]{:S(2)}) %collective-permute-start.10) | collective-permute-done | bytes 24608 | tf_op jit(solution)/shard_map/ppermute | solution.py:295
  26.5 0.2 collective-permute-done.11.three
  26.7 0.7 %shard_map.89 = (f32[32,128]{1,0:T(8,128)}, f32[32,64]{1,0:T(8,128)}) custom-call(f32[48,128]{1,0:T(8,128)S(1)} %get-tuple-element.61.mine, f32[48,128]{1,0:T(8,128)S(1)} %collective-permute-done.9.one, f32[48,128]{1,0:T(8,128)S(1)} %collective-permute-done.10.two, f32[48,128]{1,0:T(8,128)S(1)} %collective-permute-done.11.three), custom_call_target="tpu_custom_call" | custom-call | tf_op jit(solution)/shard_map/pallas_call | solution.py:24
  (10 shorter events, 0.1 us)
Async XLA Ops:
  2.6 7.7 %collective-permute-start = (f32[72,128]{1,0:T(8,128)S(1)}, f32[72,128]{1,0:T(8,128)S(1)}, u32[]{:S(2)}, u32[]{:S(2)}) collective-permute-start(f32[72,128]{1,0:T(8,128)S(1)} %get-tuple-element.31), channel_id=1, source_target_pairs={{0,4},{4,8},{8,12},{12,0},{1,5},{5,9},{9,13},{13,1},{2,6},{6,10},{... | collective-permute-start | bytes 110600 | tf_op jit(solution)/shard_map/ppermute | solution.py:295
  5.7 6.8 %collective-permute-start.1 = (f32[72,128]{1,0:T(8,128)S(1)}, f32[72,128]{1,0:T(8,128)S(1)}, u32[]{:S(2)}, u32[]{:S(2)}) collective-permute-start(f32[72,128]{1,0:T(8,128)S(1)} %get-tuple-element.32), channel_id=1, source_target_pairs={{0,12},{4,0},{8,4},{12,8},{1,13},{5,1},{9,5},{13,9},{2,14},{6,2},{... | collective-permute-start | bytes 110600 | tf_op jit(solution)/shard_map/ppermute | solution.py:295
  7.8 4.9 %collective-permute-start.2 = (f32[72,128]{1,0:T(8,128)S(1)}, f32[72,128]{1,0:T(8,128)S(1)}, u32[]{:S(2)}, u32[]{:S(2)}) collective-permute-start(f32[72,128]{1,0:T(8,128)S(1)} %get-tuple-element.33), channel_id=1, source_target_pairs={{0,8},{4,12},{8,0},{12,4},{1,9},{5,13},{9,1},{13,5},{2,10},{6,14},... | collective-permute-start | bytes 110600 | tf_op jit(solution)/shard_map/ppermute | solution.py:295
  8.7 3.9 %collective-permute-start.3 = (f32[72,128]{1,0:T(8,128)S(1)}, f32[72,128]{1,0:T(8,128)S(1)}, u32[]{:S(2)}, u32[]{:S(2)}) collective-permute-start(f32[72,128]{1,0:T(8,128)S(1)} %get-tuple-element.34), channel_id=1, source_target_pairs={{0,3},{1,2},{2,1},{3,0},{4,7},{5,6},{6,5},{7,4},{8,11},{9,10},{10,... | collective-permute-start | bytes 110600 | tf_op jit(solution)/shard_map/ppermute | solution.py:295
  8.8 4.1 %collective-permute-start.4 = (f32[72,128]{1,0:T(8,128)S(1)}, f32[72,128]{1,0:T(8,128)S(1)}, u32[]{:S(2)}, u32[]{:S(2)}) collective-permute-start(f32[72,128]{1,0:T(8,128)S(1)} %get-tuple-element.35), channel_id=1, source_target_pairs={{0,2},{1,3},{2,0},{3,1},{4,6},{5,7},{6,4},{7,5},{8,10},{9,11},{10,... | collective-permute-start | bytes 110600 | tf_op jit(solution)/shard_map/ppermute | solution.py:295
  10.3 2.6 %collective-permute-start.5 = (f32[72,128]{1,0:T(8,128)S(1)}, f32[72,128]{1,0:T(8,128)S(1)}, u32[]{:S(2)}, u32[]{:S(2)}) collective-permute-start(f32[72,128]{1,0:T(8,128)S(1)} %get-tuple-element.36), channel_id=1, source_target_pairs={{0,1},{1,0},{2,3},{3,2},{4,5},{5,4},{6,7},{7,6},{8,9},{9,8},{10,11... | collective-permute-start | bytes 110600 | tf_op jit(solution)/shard_map/ppermute | solution.py:295
  13.6 4.3 %collective-permute-start.6 = (f32[4,48,128]{2,1,0:T(8,128)S(1)}, f32[4,48,128]{2,1,0:T(8,128)S(1)}, u32[]{:S(2)}, u32[]{:S(2)}) collective-permute-start(f32[4,48,128]{2,1,0:T(8,128)S(1)} %get-tuple-element.57), channel_id=1, source_target_pairs={{0,1},{1,2},{2,3},{3,0},{4,5},{5,6},{6,7},{7,4},{8,9},{9,10},{10,1... | collective-permute-start | bytes 294920 | tf_op jit(solution)/shard_map/ppermute | solution.py:295
  13.9 5.6 %collective-permute-start.7 = (f32[4,48,128]{2,1,0:T(8,128)S(1)}, f32[4,48,128]{2,1,0:T(8,128)S(1)}, u32[]{:S(2)}, u32[]{:S(2)}) collective-permute-start(f32[4,48,128]{2,1,0:T(8,128)S(1)} %get-tuple-element.56), channel_id=1, source_target_pairs={{0,2},{1,3},{2,0},{3,1},{4,6},{5,7},{6,4},{7,5},{8,10},{9,11},{10,... | collective-permute-start | bytes 294920 | tf_op jit(solution)/shard_map/ppermute | solution.py:295
  15.2 4.6 %collective-permute-start.8 = (f32[4,48,128]{2,1,0:T(8,128)S(1)}, f32[4,48,128]{2,1,0:T(8,128)S(1)}, u32[]{:S(2)}, u32[]{:S(2)}) collective-permute-start(f32[4,48,128]{2,1,0:T(8,128)S(1)} %get-tuple-element.55), channel_id=1, source_target_pairs={{0,3},{1,0},{2,1},{3,2},{4,7},{5,4},{6,5},{7,6},{8,11},{9,8},{10,9... | collective-permute-start | bytes 294920 | tf_op jit(solution)/shard_map/ppermute | solution.py:295
  19.9 5.2 %copy-start = (bf16[128,512]{1,0:T(8,128)(2,1)S(1)}, bf16[128,512]{1,0:T(8,128)(2,1)}, u32[]{:S(2)}) copy-start(bf16[128,512]{1,0:T(8,128)(2,1)} %wi.1) | copy-start | bytes 393220
  19.9 6.0 %collective-permute-start.9 = (f32[48,128]{1,0:T(8,128)S(1)}, f32[48,128]{1,0:T(8,128)S(1)}, u32[]{:S(2)}, u32[]{:S(2)}) collective-permute-start(f32[48,128]{1,0:T(8,128)S(1)} %get-tuple-element.60), channel_id=1, source_target_pairs={{0,4},{4,8},{8,12},{12,0},{1,5},{5,9},{9,13},{13,1},{2,6},{6,10},{... | collective-permute-start | bytes 73736 | tf_op jit(solution)/shard_map/ppermute | solution.py:295
  21.5 5.0 %collective-permute-start.10 = (f32[48,128]{1,0:T(8,128)S(1)}, f32[48,128]{1,0:T(8,128)S(1)}, u32[]{:S(2)}, u32[]{:S(2)}) collective-permute-start(f32[48,128]{1,0:T(8,128)S(1)} %get-tuple-element.59), channel_id=1, source_target_pairs={{0,8},{4,12},{8,0},{12,4},{1,9},{5,13},{9,1},{13,5},{2,10},{6,14},... | collective-permute-start | bytes 73736 | tf_op jit(solution)/shard_map/ppermute | solution.py:295
  22.5 4.2 %collective-permute-start.11 = (f32[48,128]{1,0:T(8,128)S(1)}, f32[48,128]{1,0:T(8,128)S(1)}, u32[]{:S(2)}, u32[]{:S(2)}) collective-permute-start(f32[48,128]{1,0:T(8,128)S(1)} %get-tuple-element.58), channel_id=1, source_target_pairs={{0,12},{4,0},{8,4},{12,8},{1,13},{5,1},{9,5},{13,9},{2,14},{6,2},{... | collective-permute-start | bytes 73736 | tf_op jit(solution)/shard_map/ppermute | solution.py:295

commit v7 on v6

--- a/solution.py
+++ b/solution.py
@@ -85,15 +85,15 @@
 def edges_body(order, px_in, ct_in, wi_in, wo_in, rt_in, ss_in, *refs):
     sent = refs[: len(order)]
     px, ct, rt, mixed, back, dec, wgt, wi, wo, ss, src, seed, src_lines, seed_lines, ways, sems = refs[len(order) :]
-    pairs = ((ss_in, ss), (rt_in, rt), (px_in, px), (wi_in, wi), (ct_in, ct), (wo_in, wo))
+    pairs = ((wi_in, wi), (px_in, px), (ct_in, ct), (wo_in, wo), (ss_in, ss), (rt_in, rt))
     copies = [pltpu.make_async_copy(a, b, sems.at[k]) for k, (a, b) in enumerate(pairs)]
     for copy in copies:
         copy.start()
     height, breadth, channels = px.shape
     expand = wo.shape[0]
     count = height * breadth
-    copies[0].wait()
-    copies[1].wait()
+    for copy in copies:
+        copy.wait()
     for axis, length, lines in ((0, breadth, height), (1, height, breadth)):
         one, two = 2 * axis, 2 * axis + 1
         steps = {d: ss[d] if axis == 0 else jnp.transpose(ss[d]) for d in (one, two)}
@@ -104,8 +104,6 @@
         sums = jnp.concatenate([jnp.sum(step, axis=1, keepdims=True) for step in steps.values()], axis=0)
         for way in (0, 1):
             ways[axis, way, 2 * lines * expand // 128 :, :] = pack_column(sums)
-    for copy in copies[2:]:
-        copy.wait()
     both = jnp.dot(px[...].reshape(count, channels), wi[...], preferred_element_type=F32)
     mixed[...] = both
     inner, gate = both[:, :expand], both[:, expand:]

time: 27.6 us -> 27.6 us (level)
  no operation moved by 1% of the time
where the time goes in v7:
time: 27.6 us; the launch traced here: 27.4 us
  starting transfers between devices  16.1 us (58%)
  Pallas kernels  6 us (22%)
  waiting for transfers between devices  4.55 us (16%)
  between operations  0.7 us (3%)
    ppermute x12, starting transfers between devices, transfer(): lax.ppermute(value, axis, [(i, i ^ k if kind == 'xor' else (i + k) % coun...  16.1 us
    pallas_call x5, Pallas kernels, call(): pl.pallas_call(body, out_shape=out_shape, in_specs=[pl.BlockSpec(memory_s...  6 us
    ppermute x12, waiting for transfers between devices, transfer(): lax.ppermute(value, axis, [(i, i ^ k if kind == 'xor' else (i + k) % coun...  4.55 us
  transfers between devices with their start and end apart: 12, of which 7 were waited for; matrix products, arithmetic and copies ran while one was open for 0% of the time, Pallas kernels for 10%

profile of v7, /device:TPU:0, one launch (start us, length us, event | category | flops | bytes accessed | tf_op | source)
XLA Modules:
  0.0 27.4 jit_solution(3343424965893261195)
XLA Ops:
  0.6 2.0 %shard_map.85 = (f32[72,128]{1,0:T(8,128)S(1)}, f32[72,128]{1,0:T(8,128)S(1)}, f32[72,128]{1,0:T(8,128)S(1)}, f32[72,128]{1,0:T(8,128)S(1)}, f32[72,128]{1,0:T(8...) custom-call(bf16[16,16,128]{2,1,0:T(8,128)(2,1)} %px_in.1, ...), custom_call_target="tpu_custom_call" | custom-call | tf_op jit(solution)/shard_map/pallas_call | solution.py:24
  2.6 3.1 %collective-permute-start = (f32[72,128]{1,0:T(8,128)S(1)}, f32[72,128]{1,0:T(8,128)S(1)}, u32[]{:S(2)}, u32[]{:S(2)}) collective-permute-start(f32[72,128]{1,0:T(8,128)S(1)} %get-tuple-element.31), channel_id=1, source_target_pairs={{0,4},{4,8},{8,12},{12,0},{1,5},{5,9},{9,13},{13,1},{2,6},{6,10},{... | collective-permute-start | bytes 110600 | tf_op jit(solution)/shard_map/ppermute | solution.py:293
  5.7 2.1 %collective-permute-start.1 = (f32[72,128]{1,0:T(8,128)S(1)}, f32[72,128]{1,0:T(8,128)S(1)}, u32[]{:S(2)}, u32[]{:S(2)}) collective-permute-start(f32[72,128]{1,0:T(8,128)S(1)} %get-tuple-element.32), channel_id=1, source_target_pairs={{0,12},{4,0},{8,4},{12,8},{1,13},{5,1},{9,5},{13,9},{2,14},{6,2},{... | collective-permute-start | bytes 110600 | tf_op jit(solution)/shard_map/ppermute | solution.py:293
  7.8 0.9 %collective-permute-start.2 = (f32[72,128]{1,0:T(8,128)S(1)}, f32[72,128]{1,0:T(8,128)S(1)}, u32[]{:S(2)}, u32[]{:S(2)}) collective-permute-start(f32[72,128]{1,0:T(8,128)S(1)} %get-tuple-element.33), channel_id=1, source_target_pairs={{0,8},{4,12},{8,0},{12,4},{1,9},{5,13},{9,1},{13,5},{2,10},{6,14},... | collective-permute-start | bytes 110600 | tf_op jit(solution)/shard_map/ppermute | solution.py:293
  8.7 0.1 collective-permute-start.3
  8.8 1.4 %collective-permute-start.4 = (f32[72,128]{1,0:T(8,128)S(1)}, f32[72,128]{1,0:T(8,128)S(1)}, u32[]{:S(2)}, u32[]{:S(2)}) collective-permute-start(f32[72,128]{1,0:T(8,128)S(1)} %get-tuple-element.35), channel_id=1, source_target_pairs={{0,2},{1,3},{2,0},{3,1},{4,6},{5,7},{6,4},{7,5},{8,10},{9,11},{10,... | collective-permute-start | bytes 110600 | tf_op jit(solution)/shard_map/ppermute | solution.py:293
  10.3 0.3 %collective-permute-start.5 = (f32[72,128]{1,0:T(8,128)S(1)}, f32[72,128]{1,0:T(8,128)S(1)}, u32[]{:S(2)}, u32[]{:S(2)}) collective-permute-start(f32[72,128]{1,0:T(8,128)S(1)} %get-tuple-element.36), channel_id=1, source_target_pairs={{0,1},{1,0},{2,3},{3,2},{4,5},{5,4},{6,7},{7,6},{8,9},{9,8},{10,11... | collective-permute-start | bytes 110600 | tf_op jit(solution)/shard_map/ppermute | solution.py:293
  10.6 1.9 %shard_map.86 = (f32[2,256,128]{2,1,0:T(8,128)S(1)}, f32[2,256,128]{2,1,0:T(8,128)S(1)}, f32[4,2,256,128]{3,2,1,0:T(8,128)S(1)}, f32[4,2,256,128]{3,2,1,0:T(8,12...) custom-call(bf16[16,16,128]{2,1,0:T(8,128)(2,1)S(1)} %get-tuple-elem, ...), custom_call_target="tpu_custom_call" | custom-call | tf_op jit(solution)/shard_map/pallas_call | solution.py:24
  12.5 0.2 collective-permute-done.2.refs_2_
  12.6 0.3 collective-permute-done.4.refs_4_
  12.9 0.6 %shard_map.87 = (bf16[256,512]{1,0:T(8,128)(2,1)S(1)}, f32[4,4,48,128]{3,2,1,0:T(8,128)S(1)}) custom-call(f32[4,256]{1,0:T(4,128)S(1)} %get-tuple-element.30.rt, f32[72,128]{1,0:T(8,128)S(1)} %collective-permute-done.refs_0_, f32[72,128]{1,0:T(8,128)S(1)} %collective-permute-done.1.refs_1_, f32[72,128]{1,0:T(8,128)S(1)} %collective-permute-done.2.refs_2_, ...), custom_call_target="tpu_custom_call" | custom-call | tf_op jit(solution)/shard_map/pallas_call | solution.py:24
  13.6 0.3 %collective-permute-start.6 = (f32[4,48,128]{2,1,0:T(8,128)S(1)}, f32[4,48,128]{2,1,0:T(8,128)S(1)}, u32[]{:S(2)}, u32[]{:S(2)}) collective-permute-start(f32[4,48,128]{2,1,0:T(8,128)S(1)} %get-tuple-element.57), channel_id=1, source_target_pairs={{0,1},{1,2},{2,3},{3,0},{4,5},{5,6},{6,7},{7,4},{8,9},{9,10},{10,1... | collective-permute-start | bytes 294920 | tf_op jit(solution)/shard_map/ppermute | solution.py:293
  13.9 1.3 %collective-permute-start.7 = (f32[4,48,128]{2,1,0:T(8,128)S(1)}, f32[4,48,128]{2,1,0:T(8,128)S(1)}, u32[]{:S(2)}, u32[]{:S(2)}) collective-permute-start(f32[4,48,128]{2,1,0:T(8,128)S(1)} %get-tuple-element.56), channel_id=1, source_target_pairs={{0,2},{1,3},{2,0},{3,1},{4,6},{5,7},{6,4},{7,5},{8,10},{9,11},{10,... | collective-permute-start | bytes 294920 | tf_op jit(solution)/shard_map/ppermute | solution.py:293
  15.2 1.4 %collective-permute-start.8 = (f32[4,48,128]{2,1,0:T(8,128)S(1)}, f32[4,48,128]{2,1,0:T(8,128)S(1)}, u32[]{:S(2)}, u32[]{:S(2)}) collective-permute-start(f32[4,48,128]{2,1,0:T(8,128)S(1)} %get-tuple-element.55), channel_id=1, source_target_pairs={{0,3},{1,0},{2,1},{3,2},{4,7},{5,4},{6,5},{7,6},{8,11},{9,8},{10,9... | collective-permute-start | bytes 294920 | tf_op jit(solution)/shard_map/ppermute | solution.py:293
  16.6 1.3 %collective-permute-done.6 = f32[4,48,128]{2,1,0:T(8,128)S(1)} collective-permute-done((f32[4,48,128]{2,1,0:T(8,128)S(1)}, f32[4,48,128]{2,1,0:T(8,128)S(1)}, u32[]{:S(2)}, u32[]{:S(2)}) %collective-permute-start.6) | collective-permute-done | bytes 98336 | tf_op jit(solution)/shard_map/ppermute | solution.py:293
  17.9 1.6 %collective-permute-done.7 = f32[4,48,128]{2,1,0:T(8,128)S(1)} collective-permute-done((f32[4,48,128]{2,1,0:T(8,128)S(1)}, f32[4,48,128]{2,1,0:T(8,128)S(1)}, u32[]{:S(2)}, u32[]{:S(2)}) %collective-permute-start.7) | collective-permute-done | bytes 98336 | tf_op jit(solution)/shard_map/ppermute | solution.py:293
  19.5 0.3 %collective-permute-done.8 = f32[4,48,128]{2,1,0:T(8,128)S(1)} collective-permute-done((f32[4,48,128]{2,1,0:T(8,128)S(1)}, f32[4,48,128]{2,1,0:T(8,128)S(1)}, u32[]{:S(2)}, u32[]{:S(2)}) %collective-permute-start.8) | collective-permute-done | bytes 98336 | tf_op jit(solution)/shard_map/ppermute | solution.py:293
  19.9 1.6 %collective-permute-start.9 = (f32[48,128]{1,0:T(8,128)S(1)}, f32[48,128]{1,0:T(8,128)S(1)}, u32[]{:S(2)}, u32[]{:S(2)}) collective-permute-start(f32[48,128]{1,0:T(8,128)S(1)} %get-tuple-element.60), channel_id=1, source_target_pairs={{0,4},{4,8},{8,12},{12,0},{1,5},{5,9},{9,13},{13,1},{2,6},{6,10},{... | collective-permute-start | bytes 73736 | tf_op jit(solution)/shard_map/ppermute | solution.py:293
  21.6 1.0 %collective-permute-start.10 = (f32[48,128]{1,0:T(8,128)S(1)}, f32[48,128]{1,0:T(8,128)S(1)}, u32[]{:S(2)}, u32[]{:S(2)}) collective-permute-start(f32[48,128]{1,0:T(8,128)S(1)} %get-tuple-element.59), channel_id=1, source_target_pairs={{0,8},{4,12},{8,0},{12,4},{1,9},{5,13},{9,1},{13,5},{2,10},{6,14},... | collective-permute-start | bytes 73736 | tf_op jit(solution)/shard_map/ppermute | solution.py:293
  22.5 2.5 %collective-permute-start.11 = (f32[48,128]{1,0:T(8,128)S(1)}, f32[48,128]{1,0:T(8,128)S(1)}, u32[]{:S(2)}, u32[]{:S(2)}) collective-permute-start(f32[48,128]{1,0:T(8,128)S(1)} %get-tuple-element.58), channel_id=1, source_target_pairs={{0,12},{4,0},{8,4},{12,8},{1,13},{5,1},{9,5},{13,9},{2,14},{6,2},{... | collective-permute-start | bytes 73736 | tf_op jit(solution)/shard_map/ppermute | solution.py:293
  25.0 0.9 %shard_map.88 = bf16[16,16,128]{2,1,0:T(8,128)(2,1)} custom-call(bf16[16,16,128]{2,1,0:T(8,128)(2,1)S(1)} %get-tuple-element.29.ct, bf16[256,512]{1,0:T(8,128)(2,1)S(1)} %get-tuple-element.51.mix, bf16[128,512]{1,0:T(8,128)(2,1)S(1)} %copy-done), custom_call_target="tpu_custom_call" | custom-call | tf_op jit(solution)/shard_map/pallas_call | solution.py:24
  25.9 0.7 %collective-permute-done.10.two = f32[48,128]{1,0:T(8,128)S(1)} collective-permute-done((f32[48,128]{1,0:T(8,128)S(1)}, f32[48,128]{1,0:T(8,128)S(1)}, u32[]{:S(2)}, u32[]{:S(2)}) %collective-permute-start.10) | collective-permute-done | bytes 24608 | tf_op jit(solution)/shard_map/ppermute | solution.py:293
  26.6 0.2 collective-permute-done.11.three
  26.8 0.7 %shard_map.89 = (f32[32,128]{1,0:T(8,128)}, f32[32,64]{1,0:T(8,128)}) custom-call(f32[48,128]{1,0:T(8,128)S(1)} %get-tuple-element.61.mine, f32[48,128]{1,0:T(8,128)S(1)} %collective-permute-done.9.one, f32[48,128]{1,0:T(8,128)S(1)} %collective-permute-done.10.two, f32[48,128]{1,0:T(8,128)S(1)} %collective-permute-done.11.three), custom_call_target="tpu_custom_call" | custom-call | tf_op jit(solution)/shard_map/pallas_call | solution.py:24
  (10 shorter events, 0.1 us)
Async XLA Ops:
  2.6 7.7 %collective-permute-start = (f32[72,128]{1,0:T(8,128)S(1)}, f32[72,128]{1,0:T(8,128)S(1)}, u32[]{:S(2)}, u32[]{:S(2)}) collective-permute-start(f32[72,128]{1,0:T(8,128)S(1)} %get-tuple-element.31), channel_id=1, source_target_pairs={{0,4},{4,8},{8,12},{12,0},{1,5},{5,9},{9,13},{13,1},{2,6},{6,10},{... | collective-permute-start | bytes 110600 | tf_op jit(solution)/shard_map/ppermute | solution.py:293
  5.7 6.8 %collective-permute-start.1 = (f32[72,128]{1,0:T(8,128)S(1)}, f32[72,128]{1,0:T(8,128)S(1)}, u32[]{:S(2)}, u32[]{:S(2)}) collective-permute-start(f32[72,128]{1,0:T(8,128)S(1)} %get-tuple-element.32), channel_id=1, source_target_pairs={{0,12},{4,0},{8,4},{12,8},{1,13},{5,1},{9,5},{13,9},{2,14},{6,2},{... | collective-permute-start | bytes 110600 | tf_op jit(solution)/shard_map/ppermute | solution.py:293
  7.8 4.9 %collective-permute-start.2 = (f32[72,128]{1,0:T(8,128)S(1)}, f32[72,128]{1,0:T(8,128)S(1)}, u32[]{:S(2)}, u32[]{:S(2)}) collective-permute-start(f32[72,128]{1,0:T(8,128)S(1)} %get-tuple-element.33), channel_id=1, source_target_pairs={{0,8},{4,12},{8,0},{12,4},{1,9},{5,13},{9,1},{13,5},{2,10},{6,14},... | collective-permute-start | bytes 110600 | tf_op jit(solution)/shard_map/ppermute | solution.py:293
  8.7 3.9 %collective-permute-start.3 = (f32[72,128]{1,0:T(8,128)S(1)}, f32[72,128]{1,0:T(8,128)S(1)}, u32[]{:S(2)}, u32[]{:S(2)}) collective-permute-start(f32[72,128]{1,0:T(8,128)S(1)} %get-tuple-element.34), channel_id=1, source_target_pairs={{0,3},{1,2},{2,1},{3,0},{4,7},{5,6},{6,5},{7,4},{8,11},{9,10},{10,... | collective-permute-start | bytes 110600 | tf_op jit(solution)/shard_map/ppermute | solution.py:293
  8.8 4.1 %collective-permute-start.4 = (f32[72,128]{1,0:T(8,128)S(1)}, f32[72,128]{1,0:T(8,128)S(1)}, u32[]{:S(2)}, u32[]{:S(2)}) collective-permute-start(f32[72,128]{1,0:T(8,128)S(1)} %get-tuple-element.35), channel_id=1, source_target_pairs={{0,2},{1,3},{2,0},{3,1},{4,6},{5,7},{6,4},{7,5},{8,10},{9,11},{10,... | collective-permute-start | bytes 110600 | tf_op jit(solution)/shard_map/ppermute | solution.py:293
  10.3 2.6 %collective-permute-start.5 = (f32[72,128]{1,0:T(8,128)S(1)}, f32[72,128]{1,0:T(8,128)S(1)}, u32[]{:S(2)}, u32[]{:S(2)}) collective-permute-start(f32[72,128]{1,0:T(8,128)S(1)} %get-tuple-element.36), channel_id=1, source_target_pairs={{0,1},{1,0},{2,3},{3,2},{4,5},{5,4},{6,7},{7,6},{8,9},{9,8},{10,11... | collective-permute-start | bytes 110600 | tf_op jit(solution)/shard_map/ppermute | solution.py:293
  13.6 4.3 %collective-permute-start.6 = (f32[4,48,128]{2,1,0:T(8,128)S(1)}, f32[4,48,128]{2,1,0:T(8,128)S(1)}, u32[]{:S(2)}, u32[]{:S(2)}) collective-permute-start(f32[4,48,128]{2,1,0:T(8,128)S(1)} %get-tuple-element.57), channel_id=1, source_target_pairs={{0,1},{1,2},{2,3},{3,0},{4,5},{5,6},{6,7},{7,4},{8,9},{9,10},{10,1... | collective-permute-start | bytes 294920 | tf_op jit(solution)/shard_map/ppermute | solution.py:293
  13.9 5.6 %collective-permute-start.7 = (f32[4,48,128]{2,1,0:T(8,128)S(1)}, f32[4,48,128]{2,1,0:T(8,128)S(1)}, u32[]{:S(2)}, u32[]{:S(2)}) collective-permute-start(f32[4,48,128]{2,1,0:T(8,128)S(1)} %get-tuple-element.56), channel_id=1, source_target_pairs={{0,2},{1,3},{2,0},{3,1},{4,6},{5,7},{6,4},{7,5},{8,10},{9,11},{10,... | collective-permute-start | bytes 294920 | tf_op jit(solution)/shard_map/ppermute | solution.py:293
  15.2 4.6 %collective-permute-start.8 = (f32[4,48,128]{2,1,0:T(8,128)S(1)}, f32[4,48,128]{2,1,0:T(8,128)S(1)}, u32[]{:S(2)}, u32[]{:S(2)}) collective-permute-start(f32[4,48,128]{2,1,0:T(8,128)S(1)} %get-tuple-element.55), channel_id=1, source_target_pairs={{0,3},{1,0},{2,1},{3,2},{4,7},{5,4},{6,5},{7,6},{8,11},{9,8},{10,9... | collective-permute-start | bytes 294920 | tf_op jit(solution)/shard_map/ppermute | solution.py:293
  19.9 5.2 %copy-start = (bf16[128,512]{1,0:T(8,128)(2,1)S(1)}, bf16[128,512]{1,0:T(8,128)(2,1)}, u32[]{:S(2)}) copy-start(bf16[128,512]{1,0:T(8,128)(2,1)} %wi.1) | copy-start | bytes 393220
  19.9 6.0 %collective-permute-start.9 = (f32[48,128]{1,0:T(8,128)S(1)}, f32[48,128]{1,0:T(8,128)S(1)}, u32[]{:S(2)}, u32[]{:S(2)}) collective-permute-start(f32[48,128]{1,0:T(8,128)S(1)} %get-tuple-element.60), channel_id=1, source_target_pairs={{0,4},{4,8},{8,12},{12,0},{1,5},{5,9},{9,13},{13,1},{2,6},{6,10},{... | collective-permute-start | bytes 73736 | tf_op jit(solution)/shard_map/ppermute | solution.py:293
  21.6 5.0 %collective-permute-start.10 = (f32[48,128]{1,0:T(8,128)S(1)}, f32[48,128]{1,0:T(8,128)S(1)}, u32[]{:S(2)}, u32[]{:S(2)}) collective-permute-start(f32[48,128]{1,0:T(8,128)S(1)} %get-tuple-element.59), channel_id=1, source_target_pairs={{0,8},{4,12},{8,0},{12,4},{1,9},{5,13},{9,1},{13,5},{2,10},{6,14},... | collective-permute-start | bytes 73736 | tf_op jit(solution)/shard_map/ppermute | solution.py:293
  22.5 4.2 %collective-permute-start.11 = (f32[48,128]{1,0:T(8,128)S(1)}, f32[48,128]{1,0:T(8,128)S(1)}, u32[]{:S(2)}, u32[]{:S(2)}) collective-permute-start(f32[48,128]{1,0:T(8,128)S(1)} %get-tuple-element.58), channel_id=1, source_target_pairs={{0,12},{4,0},{8,4},{12,8},{1,13},{5,1},{9,5},{13,9},{2,14},{6,2},{... | collective-permute-start | bytes 73736 | tf_op jit(solution)/shard_map/ppermute | solution.py:293

commit v8 on v7

--- a/solution.py
+++ b/solution.py
@@ -119,9 +119,6 @@
         lines = height if axis == 0 else breadth
 
         if axis == 0:
-            for i in range(length):
-                for ref, line_ref in ((src, src_lines), (seed, seed_lines)):
-                    put(line_ref, pl.ds(i * lines, lines), get(ref, pl.ds(i, lines, stride=length)))
             source, grad = src_lines, seed_lines
         else:
             source, grad = src, seed
@@ -130,6 +127,9 @@
         adj = jnp.zeros((lines, expand), F32)
         for i in range(length):
             rows = slice(i * lines, (i + 1) * lines)
+            if axis == 0:
+                for ref, line_ref in ((src, src_lines), (seed, seed_lines)):
+                    put(line_ref, rows, get(ref, pl.ds(i, lines, stride=length)))
             fwd = dec[one, rows, :] * fwd + wgt[one, rows, :] * get(source, rows)
             adj = dec[two, rows, :] * (adj + get(grad, rows))
         pack_states(payload.at[0], fwd, adj)

time: 27.6 us -> 27.6 us (level)
  no operation moved by 1% of the time
where the time goes in v8:
time: 27.6 us; the launch traced here: 27.4 us
  starting transfers between devices  16.1 us (58%)
  Pallas kernels  5.99 us (22%)
  waiting for transfers between devices  4.55 us (16%)
  between operations  0.7 us (3%)
    ppermute x12, starting transfers between devices, transfer(): lax.ppermute(value, axis, [(i, i ^ k if kind == 'xor' else (i + k) % coun...  16.1 us
    pallas_call x5, Pallas kernels, call(): pl.pallas_call(body, out_shape=out_shape, in_specs=[pl.BlockSpec(memory_s...  5.99 us
    ppermute x12, waiting for transfers between devices, transfer(): lax.ppermute(value, axis, [(i, i ^ k if kind == 'xor' else (i + k) % coun...  4.55 us
  transfers between devices with their start and end apart: 12, of which 7 were waited for; matrix products, arithmetic and copies ran while one was open for 0% of the time, Pallas kernels for 10%

profile of v8, /device:TPU:0, one launch (start us, length us, event | category | flops | bytes accessed | tf_op | source)
XLA Modules:
  0.0 27.4 jit_solution(12639510365837634737)
XLA Ops:
  0.6 2.0 %shard_map.85 = (f32[72,128]{1,0:T(8,128)S(1)}, f32[72,128]{1,0:T(8,128)S(1)}, f32[72,128]{1,0:T(8,128)S(1)}, f32[72,128]{1,0:T(8,128)S(1)}, f32[72,128]{1,0:T(8...) custom-call(bf16[16,16,128]{2,1,0:T(8,128)(2,1)} %px_in.1, ...), custom_call_target="tpu_custom_call" | custom-call | tf_op jit(solution)/shard_map/pallas_call | solution.py:24
  2.6 3.1 %collective-permute-start = (f32[72,128]{1,0:T(8,128)S(1)}, f32[72,128]{1,0:T(8,128)S(1)}, u32[]{:S(2)}, u32[]{:S(2)}) collective-permute-start(f32[72,128]{1,0:T(8,128)S(1)} %get-tuple-element.31), channel_id=1, source_target_pairs={{0,4},{4,8},{8,12},{12,0},{1,5},{5,9},{9,13},{13,1},{2,6},{6,10},{... | collective-permute-start | bytes 110600 | tf_op jit(solution)/shard_map/ppermute | solution.py:293
  5.7 2.1 %collective-permute-start.1 = (f32[72,128]{1,0:T(8,128)S(1)}, f32[72,128]{1,0:T(8,128)S(1)}, u32[]{:S(2)}, u32[]{:S(2)}) collective-permute-start(f32[72,128]{1,0:T(8,128)S(1)} %get-tuple-element.32), channel_id=1, source_target_pairs={{0,12},{4,0},{8,4},{12,8},{1,13},{5,1},{9,5},{13,9},{2,14},{6,2},{... | collective-permute-start | bytes 110600 | tf_op jit(solution)/shard_map/ppermute | solution.py:293
  7.8 0.9 %collective-permute-start.2 = (f32[72,128]{1,0:T(8,128)S(1)}, f32[72,128]{1,0:T(8,128)S(1)}, u32[]{:S(2)}, u32[]{:S(2)}) collective-permute-start(f32[72,128]{1,0:T(8,128)S(1)} %get-tuple-element.33), channel_id=1, source_target_pairs={{0,8},{4,12},{8,0},{12,4},{1,9},{5,13},{9,1},{13,5},{2,10},{6,14},... | collective-permute-start | bytes 110600 | tf_op jit(solution)/shard_map/ppermute | solution.py:293
  8.7 0.1 collective-permute-start.3
  8.8 1.4 %collective-permute-start.4 = (f32[72,128]{1,0:T(8,128)S(1)}, f32[72,128]{1,0:T(8,128)S(1)}, u32[]{:S(2)}, u32[]{:S(2)}) collective-permute-start(f32[72,128]{1,0:T(8,128)S(1)} %get-tuple-element.35), channel_id=1, source_target_pairs={{0,2},{1,3},{2,0},{3,1},{4,6},{5,7},{6,4},{7,5},{8,10},{9,11},{10,... | collective-permute-start | bytes 110600 | tf_op jit(solution)/shard_map/ppermute | solution.py:293
  10.3 0.3 %collective-permute-start.5 = (f32[72,128]{1,0:T(8,128)S(1)}, f32[72,128]{1,0:T(8,128)S(1)}, u32[]{:S(2)}, u32[]{:S(2)}) collective-permute-start(f32[72,128]{1,0:T(8,128)S(1)} %get-tuple-element.36), channel_id=1, source_target_pairs={{0,1},{1,0},{2,3},{3,2},{4,5},{5,4},{6,7},{7,6},{8,9},{9,8},{10,11... | collective-permute-start | bytes 110600 | tf_op jit(solution)/shard_map/ppermute | solution.py:293
  10.6 1.9 %shard_map.86 = (f32[2,256,128]{2,1,0:T(8,128)S(1)}, f32[2,256,128]{2,1,0:T(8,128)S(1)}, f32[4,2,256,128]{3,2,1,0:T(8,128)S(1)}, f32[4,2,256,128]{3,2,1,0:T(8,12...) custom-call(bf16[16,16,128]{2,1,0:T(8,128)(2,1)S(1)} %get-tuple-elem, ...), custom_call_target="tpu_custom_call" | custom-call | tf_op jit(solution)/shard_map/pallas_call | solution.py:24
  12.5 0.2 collective-permute-done.2.refs_2_
  12.6 0.3 collective-permute-done.4.refs_4_
  12.9 0.6 %shard_map.87 = (bf16[256,512]{1,0:T(8,128)(2,1)S(1)}, f32[4,4,48,128]{3,2,1,0:T(8,128)S(1)}) custom-call(f32[4,256]{1,0:T(4,128)S(1)} %get-tuple-element.30.rt, f32[72,128]{1,0:T(8,128)S(1)} %collective-permute-done.refs_0_, f32[72,128]{1,0:T(8,128)S(1)} %collective-permute-done.1.refs_1_, f32[72,128]{1,0:T(8,128)S(1)} %collective-permute-done.2.refs_2_, ...), custom_call_target="tpu_custom_call" | custom-call | tf_op jit(solution)/shard_map/pallas_call | solution.py:24
  13.6 0.3 %collective-permute-start.6 = (f32[4,48,128]{2,1,0:T(8,128)S(1)}, f32[4,48,128]{2,1,0:T(8,128)S(1)}, u32[]{:S(2)}, u32[]{:S(2)}) collective-permute-start(f32[4,48,128]{2,1,0:T(8,128)S(1)} %get-tuple-element.57), channel_id=1, source_target_pairs={{0,1},{1,2},{2,3},{3,0},{4,5},{5,6},{6,7},{7,4},{8,9},{9,10},{10,1... | collective-permute-start | bytes 294920 | tf_op jit(solution)/shard_map/ppermute | solution.py:293
  13.9 1.3 %collective-permute-start.7 = (f32[4,48,128]{2,1,0:T(8,128)S(1)}, f32[4,48,128]{2,1,0:T(8,128)S(1)}, u32[]{:S(2)}, u32[]{:S(2)}) collective-permute-start(f32[4,48,128]{2,1,0:T(8,128)S(1)} %get-tuple-element.56), channel_id=1, source_target_pairs={{0,2},{1,3},{2,0},{3,1},{4,6},{5,7},{6,4},{7,5},{8,10},{9,11},{10,... | collective-permute-start | bytes 294920 | tf_op jit(solution)/shard_map/ppermute | solution.py:293
  15.2 1.4 %collective-permute-start.8 = (f32[4,48,128]{2,1,0:T(8,128)S(1)}, f32[4,48,128]{2,1,0:T(8,128)S(1)}, u32[]{:S(2)}, u32[]{:S(2)}) collective-permute-start(f32[4,48,128]{2,1,0:T(8,128)S(1)} %get-tuple-element.55), channel_id=1, source_target_pairs={{0,3},{1,0},{2,1},{3,2},{4,7},{5,4},{6,5},{7,6},{8,11},{9,8},{10,9... | collective-permute-start | bytes 294920 | tf_op jit(solution)/shard_map/ppermute | solution.py:293
  16.6 1.3 %collective-permute-done.6 = f32[4,48,128]{2,1,0:T(8,128)S(1)} collective-permute-done((f32[4,48,128]{2,1,0:T(8,128)S(1)}, f32[4,48,128]{2,1,0:T(8,128)S(1)}, u32[]{:S(2)}, u32[]{:S(2)}) %collective-permute-start.6) | collective-permute-done | bytes 98336 | tf_op jit(solution)/shard_map/ppermute | solution.py:293
  17.9 1.6 %collective-permute-done.7 = f32[4,48,128]{2,1,0:T(8,128)S(1)} collective-permute-done((f32[4,48,128]{2,1,0:T(8,128)S(1)}, f32[4,48,128]{2,1,0:T(8,128)S(1)}, u32[]{:S(2)}, u32[]{:S(2)}) %collective-permute-start.7) | collective-permute-done | bytes 98336 | tf_op jit(solution)/shard_map/ppermute | solution.py:293
  19.5 0.3 %collective-permute-done.8 = f32[4,48,128]{2,1,0:T(8,128)S(1)} collective-permute-done((f32[4,48,128]{2,1,0:T(8,128)S(1)}, f32[4,48,128]{2,1,0:T(8,128)S(1)}, u32[]{:S(2)}, u32[]{:S(2)}) %collective-permute-start.8) | collective-permute-done | bytes 98336 | tf_op jit(solution)/shard_map/ppermute | solution.py:293
  19.9 1.6 %collective-permute-start.9 = (f32[48,128]{1,0:T(8,128)S(1)}, f32[48,128]{1,0:T(8,128)S(1)}, u32[]{:S(2)}, u32[]{:S(2)}) collective-permute-start(f32[48,128]{1,0:T(8,128)S(1)} %get-tuple-element.60), channel_id=1, source_target_pairs={{0,4},{4,8},{8,12},{12,0},{1,5},{5,9},{9,13},{13,1},{2,6},{6,10},{... | collective-permute-start | bytes 73736 | tf_op jit(solution)/shard_map/ppermute | solution.py:293
  21.5 1.0 %collective-permute-start.10 = (f32[48,128]{1,0:T(8,128)S(1)}, f32[48,128]{1,0:T(8,128)S(1)}, u32[]{:S(2)}, u32[]{:S(2)}) collective-permute-start(f32[48,128]{1,0:T(8,128)S(1)} %get-tuple-element.59), channel_id=1, source_target_pairs={{0,8},{4,12},{8,0},{12,4},{1,9},{5,13},{9,1},{13,5},{2,10},{6,14},... | collective-permute-start | bytes 73736 | tf_op jit(solution)/shard_map/ppermute | solution.py:293
  22.5 2.5 %collective-permute-start.11 = (f32[48,128]{1,0:T(8,128)S(1)}, f32[48,128]{1,0:T(8,128)S(1)}, u32[]{:S(2)}, u32[]{:S(2)}) collective-permute-start(f32[48,128]{1,0:T(8,128)S(1)} %get-tuple-element.58), channel_id=1, source_target_pairs={{0,12},{4,0},{8,4},{12,8},{1,13},{5,1},{9,5},{13,9},{2,14},{6,2},{... | collective-permute-start | bytes 73736 | tf_op jit(solution)/shard_map/ppermute | solution.py:293
  25.0 0.9 %shard_map.88 = bf16[16,16,128]{2,1,0:T(8,128)(2,1)} custom-call(bf16[16,16,128]{2,1,0:T(8,128)(2,1)S(1)} %get-tuple-element.29.ct, bf16[256,512]{1,0:T(8,128)(2,1)S(1)} %get-tuple-element.51.mix, bf16[128,512]{1,0:T(8,128)(2,1)S(1)} %copy-done), custom_call_target="tpu_custom_call" | custom-call | tf_op jit(solution)/shard_map/pallas_call | solution.py:24
  25.9 0.7 %collective-permute-done.10.two = f32[48,128]{1,0:T(8,128)S(1)} collective-permute-done((f32[48,128]{1,0:T(8,128)S(1)}, f32[48,128]{1,0:T(8,128)S(1)}, u32[]{:S(2)}, u32[]{:S(2)}) %collective-permute-start.10) | collective-permute-done | bytes 24608 | tf_op jit(solution)/shard_map/ppermute | solution.py:293
  26.5 0.2 collective-permute-done.11.three
  26.7 0.7 %shard_map.89 = (f32[32,128]{1,0:T(8,128)}, f32[32,64]{1,0:T(8,128)}) custom-call(f32[48,128]{1,0:T(8,128)S(1)} %get-tuple-element.61.mine, f32[48,128]{1,0:T(8,128)S(1)} %collective-permute-done.9.one, f32[48,128]{1,0:T(8,128)S(1)} %collective-permute-done.10.two, f32[48,128]{1,0:T(8,128)S(1)} %collective-permute-done.11.three), custom_call_target="tpu_custom_call" | custom-call | tf_op jit(solution)/shard_map/pallas_call | solution.py:24
  (10 shorter events, 0.1 us)
Async XLA Ops:
  2.6 7.7 %collective-permute-start = (f32[72,128]{1,0:T(8,128)S(1)}, f32[72,128]{1,0:T(8,128)S(1)}, u32[]{:S(2)}, u32[]{:S(2)}) collective-permute-start(f32[72,128]{1,0:T(8,128)S(1)} %get-tuple-element.31), channel_id=1, source_target_pairs={{0,4},{4,8},{8,12},{12,0},{1,5},{5,9},{9,13},{13,1},{2,6},{6,10},{... | collective-permute-start | bytes 110600 | tf_op jit(solution)/shard_map/ppermute | solution.py:293
  5.7 6.8 %collective-permute-start.1 = (f32[72,128]{1,0:T(8,128)S(1)}, f32[72,128]{1,0:T(8,128)S(1)}, u32[]{:S(2)}, u32[]{:S(2)}) collective-permute-start(f32[72,128]{1,0:T(8,128)S(1)} %get-tuple-element.32), channel_id=1, source_target_pairs={{0,12},{4,0},{8,4},{12,8},{1,13},{5,1},{9,5},{13,9},{2,14},{6,2},{... | collective-permute-start | bytes 110600 | tf_op jit(solution)/shard_map/ppermute | solution.py:293
  7.8 4.9 %collective-permute-start.2 = (f32[72,128]{1,0:T(8,128)S(1)}, f32[72,128]{1,0:T(8,128)S(1)}, u32[]{:S(2)}, u32[]{:S(2)}) collective-permute-start(f32[72,128]{1,0:T(8,128)S(1)} %get-tuple-element.33), channel_id=1, source_target_pairs={{0,8},{4,12},{8,0},{12,4},{1,9},{5,13},{9,1},{13,5},{2,10},{6,14},... | collective-permute-start | bytes 110600 | tf_op jit(solution)/shard_map/ppermute | solution.py:293
  8.7 3.9 %collective-permute-start.3 = (f32[72,128]{1,0:T(8,128)S(1)}, f32[72,128]{1,0:T(8,128)S(1)}, u32[]{:S(2)}, u32[]{:S(2)}) collective-permute-start(f32[72,128]{1,0:T(8,128)S(1)} %get-tuple-element.34), channel_id=1, source_target_pairs={{0,3},{1,2},{2,1},{3,0},{4,7},{5,6},{6,5},{7,4},{8,11},{9,10},{10,... | collective-permute-start | bytes 110600 | tf_op jit(solution)/shard_map/ppermute | solution.py:293
  8.8 4.1 %collective-permute-start.4 = (f32[72,128]{1,0:T(8,128)S(1)}, f32[72,128]{1,0:T(8,128)S(1)}, u32[]{:S(2)}, u32[]{:S(2)}) collective-permute-start(f32[72,128]{1,0:T(8,128)S(1)} %get-tuple-element.35), channel_id=1, source_target_pairs={{0,2},{1,3},{2,0},{3,1},{4,6},{5,7},{6,4},{7,5},{8,10},{9,11},{10,... | collective-permute-start | bytes 110600 | tf_op jit(solution)/shard_map/ppermute | solution.py:293
  10.3 2.6 %collective-permute-start.5 = (f32[72,128]{1,0:T(8,128)S(1)}, f32[72,128]{1,0:T(8,128)S(1)}, u32[]{:S(2)}, u32[]{:S(2)}) collective-permute-start(f32[72,128]{1,0:T(8,128)S(1)} %get-tuple-element.36), channel_id=1, source_target_pairs={{0,1},{1,0},{2,3},{3,2},{4,5},{5,4},{6,7},{7,6},{8,9},{9,8},{10,11... | collective-permute-start | bytes 110600 | tf_op jit(solution)/shard_map/ppermute | solution.py:293
  13.6 4.3 %collective-permute-start.6 = (f32[4,48,128]{2,1,0:T(8,128)S(1)}, f32[4,48,128]{2,1,0:T(8,128)S(1)}, u32[]{:S(2)}, u32[]{:S(2)}) collective-permute-start(f32[4,48,128]{2,1,0:T(8,128)S(1)} %get-tuple-element.57), channel_id=1, source_target_pairs={{0,1},{1,2},{2,3},{3,0},{4,5},{5,6},{6,7},{7,4},{8,9},{9,10},{10,1... | collective-permute-start | bytes 294920 | tf_op jit(solution)/shard_map/ppermute | solution.py:293
  13.9 5.6 %collective-permute-start.7 = (f32[4,48,128]{2,1,0:T(8,128)S(1)}, f32[4,48,128]{2,1,0:T(8,128)S(1)}, u32[]{:S(2)}, u32[]{:S(2)}) collective-permute-start(f32[4,48,128]{2,1,0:T(8,128)S(1)} %get-tuple-element.56), channel_id=1, source_target_pairs={{0,2},{1,3},{2,0},{3,1},{4,6},{5,7},{6,4},{7,5},{8,10},{9,11},{10,... | collective-permute-start | bytes 294920 | tf_op jit(solution)/shard_map/ppermute | solution.py:293
  15.2 4.6 %collective-permute-start.8 = (f32[4,48,128]{2,1,0:T(8,128)S(1)}, f32[4,48,128]{2,1,0:T(8,128)S(1)}, u32[]{:S(2)}, u32[]{:S(2)}) collective-permute-start(f32[4,48,128]{2,1,0:T(8,128)S(1)} %get-tuple-element.55), channel_id=1, source_target_pairs={{0,3},{1,0},{2,1},{3,2},{4,7},{5,4},{6,5},{7,6},{8,11},{9,8},{10,9... | collective-permute-start | bytes 294920 | tf_op jit(solution)/shard_map/ppermute | solution.py:293
  19.9 5.2 %copy-start = (bf16[128,512]{1,0:T(8,128)(2,1)S(1)}, bf16[128,512]{1,0:T(8,128)(2,1)}, u32[]{:S(2)}) copy-start(bf16[128,512]{1,0:T(8,128)(2,1)} %wi.1) | copy-start | bytes 393220
  19.9 6.0 %collective-permute-start.9 = (f32[48,128]{1,0:T(8,128)S(1)}, f32[48,128]{1,0:T(8,128)S(1)}, u32[]{:S(2)}, u32[]{:S(2)}) collective-permute-start(f32[48,128]{1,0:T(8,128)S(1)} %get-tuple-element.60), channel_id=1, source_target_pairs={{0,4},{4,8},{8,12},{12,0},{1,5},{5,9},{9,13},{13,1},{2,6},{6,10},{... | collective-permute-start | bytes 73736 | tf_op jit(solution)/shard_map/ppermute | solution.py:293
  21.5 5.0 %collective-permute-start.10 = (f32[48,128]{1,0:T(8,128)S(1)}, f32[48,128]{1,0:T(8,128)S(1)}, u32[]{:S(2)}, u32[]{:S(2)}) collective-permute-start(f32[48,128]{1,0:T(8,128)S(1)} %get-tuple-element.59), channel_id=1, source_target_pairs={{0,8},{4,12},{8,0},{12,4},{1,9},{5,13},{9,1},{13,5},{2,10},{6,14},... | collective-permute-start | bytes 73736 | tf_op jit(solution)/shard_map/ppermute | solution.py:293
  22.5 4.2 %collective-permute-start.11 = (f32[48,128]{1,0:T(8,128)S(1)}, f32[48,128]{1,0:T(8,128)S(1)}, u32[]{:S(2)}, u32[]{:S(2)}) collective-permute-start(f32[48,128]{1,0:T(8,128)S(1)} %get-tuple-element.58), channel_id=1, source_target_pairs={{0,12},{4,0},{8,4},{12,8},{1,13},{5,1},{9,5},{13,9},{2,14},{6,2},{... | collective-permute-start | bytes 73736 | tf_op jit(solution)/shard_map/ppermute | solution.py:293
